TPU v7x, 32 devices: a whole 2x2x4 slice. The times are simulated.
32 devices in a mesh: ctx: 2 (over core), ep: 16 (over z, y, x).
Axes of the slice: x: 2, y: 2, z: 4, core: 2. Of those that a mesh axis runs over, the one named last changes fastest.
Arguments:
- moe_rows: bfloat16 [1024, 3584], P('ep'), may hold values from -6 to 6
- routes: int32 [1024, 8], P('ep'), may hold values from 0 to 127, all different within a row; in each aligned block of 64 rows (0 to 63, 64 to 127, ...) at most 8 rows name the same one
- route_gates: float32 [1024, 8], P('ep'), may hold values from 0.1 to 1
- gate_weight: bfloat16 [128, 3584, 1024], P('ep', None, 'ctx'), may hold values from -0.09375 to 0.09375
- up_weight: bfloat16 [128, 3584, 1024], P('ep', None, 'ctx'), may hold values from -0.09375 to 0.09375
- down_weight: bfloat16 [128, 1024, 3584], P('ep', 'ctx'), may hold values from -0.1875 to 0.1875
- queries: bfloat16 [16, 64, 576], P('ep'), may hold values from -82 to 82
- latent_cache: bfloat16 [16, 4096, 576], P('ep', 'ctx'), may hold values from -6 to 6
- cache_lengths: int32 [16], P('ep'), may hold values from 128 to 4096, as said below
Outputs:
- routed_output: bfloat16 [1024, 3584], P('ep')
- attention_output: bfloat16 [16, 64, 512], P('ep', 'ctx')
Inputs may be any that keep to these rules, and one draw needn't show every extreme that they name: `routes`: each row names 8 different experts. In each aligned block of 64 rows (the rows of one ep index) no expert is named by more than 8 rows, and in some blocks an expert is named by exactly 8 rows. `cache_lengths`: each length is a multiple of 128.
All inputs are finite; a program needn't handle non-finite values.
Results may differ from a plain program's by a relative error of at most 0.014.
Values may be sent and summed in bfloat16 or wider, within the bound.
No kernel may reach another device: no remote copies, remote signals or barrier semaphores. Data moves between devices by JAX's collectives and lax.ppermute only.
A program may use at most 256 MiB of HBM per device.

v0:
```python
import jax
import jax.numpy as jnp
from jax import lax
from jax.sharding import PartitionSpec as P

LAT = 512
EXPERTS = 128
CAP = 8


softmax_scale = 192.0 ** (-0.5)


def joined(x, axis, join):
    gathered = jax.tree.map(
        lambda a, kind: lax.all_gather(a.astype(kind), axis),
        x,
        (jnp.bfloat16, jnp.bfloat16, jnp.bfloat16),
    )

    def take(source):
        return jax.tree.map(
            lambda a, own: lax.dynamic_index_in_dim(a, source, 0, False).astype(own.dtype),
            gathered,
            x,
        )

    return lax.fori_loop(
        1, lax.axis_size(axis), lambda source, state: join(state, take(source)), take(0)
    )


def merge_partials(earlier_part, later_part):
    earlier_top, earlier_total, earlier_values = earlier_part
    later_top, later_total, later_values = later_part
    joined_top = jnp.maximum(earlier_top, later_top)
    earlier_factor = jnp.exp(earlier_top - joined_top)
    later_factor = jnp.exp(later_top - joined_top)
    joined_total = earlier_total * earlier_factor + later_total * later_factor
    joined_values = (
        earlier_values * earlier_factor[:, :, None] + later_values * later_factor[:, :, None]
    )
    return (joined_top, joined_total, joined_values)


def softmax_parts(queries, cache, cache_lengths, offset):
    local_span = cache.shape[1]
    scores = (
        jnp.einsum("rhk,rlk->rhl", queries, cache, preferred_element_type=jnp.float32)
        * softmax_scale
    )
    positions = offset + jnp.arange(local_span, dtype=jnp.int32)
    usable = (positions[None, :] < cache_lengths[:, None])[:, None, :]
    masked = jnp.where(usable, scores, -1e30)
    top_score = jnp.max(masked, axis=2)
    weights = jnp.where(usable, jnp.exp(masked - top_score[:, :, None]), 0.0)
    row_total = jnp.sum(weights, axis=2)
    values = jnp.einsum(
        "rhl,rlv->rhv",
        weights.astype(jnp.bfloat16),
        cache[:, :, :LAT],
        preferred_element_type=jnp.float32,
    )
    return (top_score, row_total, values)


def attend_local(queries, latent_cache, cache_lengths):
    head_count = queries.shape[1]
    head_share = head_count // lax.axis_size("ctx")
    first_head = lax.axis_index("ctx") * head_share
    top_score, row_total, values = softmax_parts(
        queries, latent_cache, cache_lengths, lax.axis_index("ctx") * latent_cache.shape[1]
    )
    joined_top, joined_total, joined_values = joined(
        (top_score, row_total, values), "ctx", merge_partials
    )
    mine_total = lax.dynamic_slice_in_dim(joined_total, first_head, head_share, 1)
    mine_values = lax.dynamic_slice_in_dim(joined_values, first_head, head_share, 1)
    return (mine_values / mine_total[:, :, None]).astype(jnp.bfloat16)


def expert_pass(received, gate_weight, up_weight, down_weight):
    gate_proj = jnp.einsum(
        "sjcd,jdf->sjcf", received, gate_weight, preferred_element_type=jnp.float32
    )
    up_proj = jnp.einsum("sjcd,jdf->sjcf", received, up_weight, preferred_element_type=jnp.float32)
    hidden = (jax.nn.silu(gate_proj) * up_proj).astype(jnp.bfloat16)
    partial_out = jnp.einsum(
        "sjcf,jfd->sjcd", hidden, down_weight, preferred_element_type=jnp.float32
    )
    summed = lax.psum(partial_out.astype(jnp.bfloat16), "ctx")
    result_rows = lax.all_to_all(summed, "ep", split_axis=0, concat_axis=0, tiled=True)
    return result_rows


def route_rows(moe_rows, routes, route_gates, gate_weight, up_weight, down_weight):
    row_count, model_width = moe_rows.shape
    top_count = routes.shape[1]
    pair_count = routes.shape[0] * top_count
    owners = lax.axis_size("ep")
    local_experts = gate_weight.shape[0]
    slot_count = EXPERTS * CAP
    expert_ids = routes.reshape(-1)
    one_hot = (expert_ids[:, None] == jnp.arange(EXPERTS, dtype=jnp.int32)[None, :]).astype(
        jnp.int32
    )
    earlier = jnp.cumsum(one_hot, axis=0) - one_hot
    targets = expert_ids * CAP + jnp.sum(earlier * one_hot, axis=1)
    target_hot = (targets[:, None] == jnp.arange(slot_count, dtype=jnp.int32)[None, :]).astype(
        jnp.bfloat16
    )
    pair_rows = jnp.arange(pair_count, dtype=jnp.int32) // top_count
    row_hot = (pair_rows[:, None] == jnp.arange(row_count, dtype=jnp.int32)[None, :]).astype(
        jnp.bfloat16
    )
    selector = jnp.einsum(
        "as,ar->sr", target_hot, row_hot, preferred_element_type=jnp.float32
    ).astype(jnp.bfloat16)
    outgoing = jnp.dot(selector, moe_rows, preferred_element_type=jnp.float32).astype(jnp.bfloat16)
    outgoing = outgoing.reshape(owners, local_experts, CAP, model_width)
    returned = expert_pass(
        lax.all_to_all(outgoing, "ep", split_axis=0, concat_axis=0, tiled=True),
        gate_weight,
        up_weight,
        down_weight,
    )
    slot_rows = returned.reshape(slot_count, model_width)
    picked = jnp.take(slot_rows, targets, axis=0).reshape(row_count, top_count, model_width)
    combined = jnp.sum(picked.astype(jnp.float32) * route_gates[:, :, None], axis=1)
    return combined.astype(jnp.bfloat16)


def body(
    moe_rows,
    routes,
    route_gates,
    gate_weight,
    up_weight,
    down_weight,
    queries,
    latent_cache,
    cache_lengths,
):
    attention_output = attend_local(queries, latent_cache, cache_lengths)
    routed_output = route_rows(moe_rows, routes, route_gates, gate_weight, up_weight, down_weight)
    return (routed_output, attention_output)


def solution(mesh):
    in_specs = (
        P("ep", None),
        P("ep", None),
        P("ep", None),
        P("ep", None, "ctx"),
        P("ep", None, "ctx"),
        P("ep", "ctx", None),
        P("ep", None, None),
        P("ep", "ctx", None),
        P("ep"),
    )
    out_specs = (P("ep", None), P("ep", "ctx", None))
    return jax.shard_map(body, mesh=mesh, in_specs=in_specs, out_specs=out_specs, check_vma=False)
```

profile of v0, /device:TPU:28, one launch (start us, length us, event | category | flops | bytes accessed | tf_op | source)
XLA Modules:
  0.0 460.3 jit_solution(16248447132515298915)
XLA Ops:
  7.2 0.0 copy-start
  7.2 0.0 all-reduce.5.cloned.1.call-start
  7.2 0.8 copy.31
  8.0 0.1 eq.52
  8.1 0.1 reshape.354
  8.2 0.1 copy.33
  8.3 0.2 fusion.52
  8.7 0.2 fusion.49
  8.9 0.0 copy-done
  8.9 5.0 %convolution_convert_fusion = bf16[1024,3584]{1,0:T(8,128)(2,1)} fusion(bf16[64,3584]{1,0:T(8,128)(2,1)S(1)} %copy-done, s32[512]{0:T(512)S(1)} %get-tuple-element.35, s32[512]{0:T(512)S(1)} %get-tuple-element.34), kind=kOutput, calls=%fused_computation.8 | convolution fusion | flops 541163520 | bytes 7802880 | tf_op jit(solution)/shard_map/dot_general | solution.py:119
  13.9 166.1 %all_to_all.10 = bf16[16,8,8,3584]{3,2,1,0:T(8,128)(2,1)} all-to-all(bf16[16,8,8,3584]{3,2,1,0:T(8,128)(2,1)} %bitcast.122), channel_id=1, replica_groups=mesh['ctx'=2,'ep'=16] {'ep'}, dimensions={0} | all-to-all | bytes 14680064 | tf_op jit(solution)/shard_map/all_to_all | solution.py:122
  180.1 13.6 %fusion.2 = f32[8,16,8,512]{3,2,1,0:T(8,128)S(1)} fusion(bf16[8,3584,512]{2,1,0:T(8,128)(2,1)} %param.13, bf16[16,8,8,3584]{3,2,1,0:T(8,128)(2,1)} %all_to_all.10), kind=kOutput, calls=%fused_computation.3 | convolution fusion | flops 3758096384 | bytes 38797312 | tf_op jit(solution)/shard_map/sjcd,jdf->sjcf/dot_general | solution.py:86
  193.7 25.4 %fusion.9 = bf16[16,8,8,3584]{3,2,0,1:T(8,128)(2,1)} fusion(bf16[8,512,3584]{2,1,0:T(8,128)(2,1)} %param.14, f32[8,16,8,512]{3,2,1,0:T(8,128)S(1)} %fusion.2, bf16[8,3584,512]{2,1,0:T(8,128)(2,1)} %param.12, bf16[16,8,8,3584]{3,2,1,0:T(8,128)(2,1)} %all_to_all.10), kind=kOutput, calls=%fused_computation.10 | convolution fusion | flops 7523008512 | bytes 75497472 | tf_op jit(solution)/shard_map/sjcf,jfd->sjcd/dot_general | solution.py:88
  219.0 0.0 all-reduce.5.cloned.1.call-update
  219.1 34.5 %all-reduce.5.cloned.1.call-done = bf16[16,8,8,3584]{3,2,0,1:T(8,128)(2,1)} async-done(((bf16[16,8,8,3584]{3,2,0,1:T(8,128)(2,1)}), bf16[16,8,8,3584]{3,2,0,1:T(8,128)(2,1)}) %all-reduce.5.cloned.1.call-update) | async-done | bytes 7340048 | tf_op jit(solution)/shard_map/psum | solution.py:91
  253.5 6.9 %copy.39 = bf16[16,8,8,3584]{3,2,1,0:T(8,128)(2,1)} copy(bf16[16,8,8,3584]{3,2,0,1:T(8,128)(2,1)} %all-reduce.5.cloned.1.call-done) | data formatting | bytes 14680064 | tf_op jit(solution)/shard_map/psum | solution.py:91
  260.4 0.0 copy-start.4
  260.4 0.0 copy-start.5
  260.4 0.0 copy-start.2
  260.4 0.0 copy-start.3
  260.4 0.0 copy-start.6
  260.5 7.1 %all-to-all-start.1 = ((bf16[16,8,8,3584]{3,2,1,0:T(8,128)(2,1)}), bf16[16,8,8,3584]{3,2,1,0:T(8,128)(2,1)}, u32[]{:S(2)}, u32[]{:S(2)}) async-start(bf16[16,8,8,3584]{3,2,1,0:T(8,128)(2,1)} %copy.39), calls=%async_computation.1 | async-start | bytes 14680064 | tf_op jit(solution)/shard_map/all_to_all | solution.py:92
  267.5 0.1 reduce_sum.32
  267.6 0.0 copy-done.4
  267.6 0.1 copy.40
  267.7 0.1 mul.128
  267.8 0.0 copy-done.5
  267.8 0.1 copy.41
  267.9 0.1 copy.35
  268.0 0.1 copy.36
  268.8 0.0 copy-done.2
  268.8 0.0 copy-done.3
  268.8 0.7 fusion.75
  269.5 0.0 copy-done.6
  269.5 0.6 dynamic-slice
  270.7 0.2 dynamic-update-slice
  271.0 0.3 fusion.45
  271.2 0.2 dynamic-update-slice.1
  271.5 2.4 all-reduce.2
  273.9 0.1 fusion.65
  274.0 0.1 dynamic-slice.3
  274.1 0.1 dynamic-slice.2
  274.2 0.8 fusion.39
  274.9 2.1 all-gather
  277.0 0.1 fusion.72
  277.1 0.1 fusion.71
  277.2 0.7 fusion.61
  277.9 156.8 %all-to-all-done.1 = bf16[16,8,8,3584]{3,2,1,0:T(8,128)(2,1)} async-done(((bf16[16,8,8,3584]{3,2,1,0:T(8,128)(2,1)}), bf16[16,8,8,3584]{3,2,1,0:T(8,128)(2,1)}, u32[]{:S(2)}, u32[]{:S(2)}) %all-to-all-start.1) | async-done | bytes 7340064 | tf_op jit(solution)/shard_map/all_to_all | solution.py:92
  434.7 0.0 copy-start.1
  434.7 12.0 %gather_fusion = bf16[512,3584]{1,0:T(8,128)(2,1)} fusion(bf16[1024,3584]{1,0:T(8,128)(2,1)} %bitcast.13, s32[1024]{0:T(1024)S(1)} %pad_clamp_fusion), kind=kCustom, calls=%fused_computation | custom fusion | bytes 7342080 | tf_op jit(solution)/shard_map/jit(_take)/gather | solution.py:128
  446.7 6.8 %multiply_reduce_fusion = bf16[64,3584]{1,0:T(8,128)(2,1)} fusion(bf16[512,3584]{1,0:T(8,128)(2,1)} %gather_fusion, f32[64,8]{1,0:T(8,128)S(1)} %copy.41, pred[64,8]{1,0:T(8,128)(4,1)S(1)} %copy.36), kind=kLoop, calls=%fused_computation.9 | loop fusion | flops 7110656 | bytes 4131328 | tf_op jit(solution)/shard_map/reduce_sum | solution.py:129
  453.5 0.0 copy-done.1
  (16 shorter events, 0.2 us)
Async XLA Ops:
  7.2 1.7 copy-start
  7.2 246.3 %all-reduce.5.cloned.1.call-start = ((), (), s32[]{:S(2)}) async-start(), calls=%async_computation.2 | async-start | bytes 14680064 | tf_op jit(solution)/shard_map/psum | solution.py:91
  260.4 7.2 %copy-start.4 = (s32[64,8]{0,1:T(8,128)S(1)}, s32[64,8]{0,1:T(8,128)}, u32[]{:S(2)}) copy-start(s32[64,8]{0,1:T(8,128)} %param.10) | copy-start | bytes 6148
  260.4 7.4 %copy-start.5 = (f32[64,8]{0,1:T(8,128)S(1)}, f32[64,8]{0,1:T(8,128)}, u32[]{:S(2)}) copy-start(f32[64,8]{0,1:T(8,128)} %param.11) | copy-start | bytes 6148
  260.4 8.3 %copy-start.2 = (bf16[1,2048,576]{1,2,0:T(8,128)(2,1)S(1)}, bf16[1,2048,576]{1,2,0:T(8,128)(2,1)}, u32[]{:S(2)}) copy-start(bf16[1,2048,576]{1,2,0:T(8,128)(2,1)} %param.16) | copy-start | bytes 7077892
  260.4 8.3 %copy-start.3 = (bf16[1,64,576]{2,1,0:T(8,128)(2,1)S(1)}, bf16[1,64,576]{2,1,0:T(8,128)(2,1)}, u32[]{:S(2)}) copy-start(bf16[1,64,576]{2,1,0:T(8,128)(2,1)} %param.15) | copy-start | bytes 221188
  260.4 9.0 %copy-start.6 = (u32[32]{0:T(128)S(1)}, u32[32]{0:T(128)}, u32[]{:S(2)}) copy-start(u32[32]{0:T(128)} %constant.95) | copy-start | bytes 388
  260.5 174.2 %all-to-all-start.1 = ((bf16[16,8,8,3584]{3,2,1,0:T(8,128)(2,1)}), bf16[16,8,8,3584]{3,2,1,0:T(8,128)(2,1)}, u32[]{:S(2)}, u32[]{:S(2)}) async-start(bf16[16,8,8,3584]{3,2,1,0:T(8,128)(2,1)} %copy.39), calls=%async_computation.1 | async-start | bytes 14680064 | tf_op jit(solution)/shard_map/all_to_all | solution.py:92
  434.7 18.8 %copy-start.1 = (bf16[64,3584]{1,0:T(8,128)(2,1)S(1)}, bf16[64,3584]{1,0:T(8,128)(2,1)}, u32[]{:S(2)}) copy-start(bf16[64,3584]{1,0:T(8,128)(2,1)} %param.9) | copy-start | bytes 1376260
Sparse Core Ops, SparseCore 0:
  219.2 34.3 all-reduce.4
where the time goes:
time: 461 us; the launch traced here: 460 us
  waiting for transfers between devices  191 us (41%)
  blocking collectives  171 us (37%)
  matrix products  45.4 us (10%)
  local copies, waits for them, and re-layouts  21.9 us (5%)
  between operations  15.5 us (3%)
  other arithmetic  8.46 us (2%)
  starting transfers between devices  7.1 us (2%)
    all_to_all x1, blocking collectives, route_rows(): lax.all_to_all(outgoing, 'ep', split_axis=0, concat_axis=0, tiled=True)  166 us
    all_to_all x1, waiting for transfers between devices, expert_pass(): lax.all_to_all(summed, 'ep', split_axis=0, concat_axis=0, tiled=True)  157 us
    psum x1, waiting for transfers between devices, expert_pass(): summed = lax.psum(partial_out.astype(jnp.bfloat16), 'ctx')  34.5 us
    dot_general x1, matrix products, expert_pass(): jnp.einsum('sjcf,jfd->sjcd', hidden, down_weight, preferred_element_type=...  25.4 us
    dot_general x1, matrix products, expert_pass(): jnp.einsum('sjcd,jdf->sjcf', received, up_weight, preferred_element_type=...  13.6 us
    gather x1, local copies, waits for them, and re-layouts, route_rows(): jnp.take(slot_rows, targets, axis=0)  12 us
  transfers between devices with their start and end apart: 2, of which 2 were waited for; matrix products, arithmetic and copies ran while one was open for 1% of the time, Pallas kernels for 0%

commit v1 on v0

v1 whole, which is shorter than its diff:
```python
import functools

import jax
import jax.numpy as jnp
from jax import lax
from jax.experimental import pallas as pl
from jax.experimental.pallas import tpu as pltpu
from jax.sharding import PartitionSpec as P

LAT = 512
CAP = 8
JOIN = 4
COLS = 512

softmax_scale = 192.0 ** (-0.5)


def softmax_parts(queries, cache, cache_lengths, offset):
    local_span = cache.shape[1]
    scores = (
        jnp.einsum("rhk,rlk->rhl", queries, cache, preferred_element_type=jnp.float32)
        * softmax_scale
    )
    positions = offset + jnp.arange(local_span, dtype=jnp.int32)
    usable = (positions[None, :] < cache_lengths[:, None])[:, None, :]
    masked = jnp.where(usable, scores, -1e30)
    top_score = jnp.max(masked, axis=2)
    weights = jnp.where(usable, jnp.exp(masked - top_score[:, :, None]), 0.0)
    row_total = jnp.sum(weights, axis=2)
    values = jnp.einsum(
        "rhl,rlv->rhv",
        weights.astype(jnp.bfloat16),
        cache[:, :, :LAT],
        preferred_element_type=jnp.float32,
    )
    return (top_score, row_total, values)


def swap_ctx(x):
    return lax.ppermute(x, "ctx", [(0, 1), (1, 0)])


def attend_local(queries, latent_cache, cache_lengths):
    share = queries.shape[1] // 2
    mine = lax.axis_index("ctx")
    top, total, values = softmax_parts(
        queries, latent_cache, cache_lengths, mine * latent_cache.shape[1]
    )
    packed = jnp.concatenate(
        [values, jnp.stack([top, total], axis=2), jnp.zeros(top.shape + (126,), jnp.float32)],
        axis=2,
    )
    kept = lax.dynamic_slice_in_dim(packed, mine * share, share, 1)
    other = swap_ctx(lax.dynamic_slice_in_dim(packed, (1 - mine) * share, share, 1))
    kept_top, other_top = kept[:, :, LAT : LAT + 1], other[:, :, LAT : LAT + 1]
    joined_top = jnp.maximum(kept_top, other_top)
    kept_factor = jnp.exp(kept_top - joined_top)
    other_factor = jnp.exp(other_top - joined_top)
    joined = kept * kept_factor + other * other_factor
    return (joined[:, :, :LAT] / joined[:, :, LAT + 1 : LAT + 2]).astype(jnp.bfloat16)


def plane_of(owners):
    return owners == 16


def send(x, target):
    count = lax.axis_size("ep")
    return lax.ppermute(x, "ep", [(i, target(i)) for i in range(count)])


def to_x(x):
    return send(x, lambda i: i ^ 1)


def to_y(x):
    return send(x, lambda i: i ^ 2)


def to_z(x, steps):
    return send(x, lambda i: (i + 4 * steps) % 16)


def cat(*pieces):
    return jnp.concatenate(pieces, axis=0)


def after(x, other):
    return lax.optimization_barrier((x, other))[0]


def gather_rows(rows):
    n = rows.shape[0]
    h = n // 2
    below, above = to_z(rows, 1), to_z(rows, 3)
    own_x, own_y = to_x(rows), to_y(rows)
    far = to_z(after(rows, below), 2)
    bx = to_x(cat(below, above, own_y[h:]))
    by = to_y(cat(below, above, own_x[:h]))
    cx = to_x(cat(far, by[h:n], by[n + h : 2 * n]))
    cy = to_y(cat(far, bx[:h], bx[n : n + h]))
    dx = to_x(cy[h:n])
    dy = to_y(cx[:h])
    return [
        cat(rows, own_x, own_y, by[2 * n :], bx[2 * n :]),
        cat(below, bx[:n], by[:n], cy[n : n + h], cx[n : n + h]),
        cat(far, cx[:n], cy[:n], dy, dx),
        cat(above, bx[n : 2 * n], by[n : 2 * n], cy[n + h :], cx[n + h :]),
    ]


def scatter_sums(groups):
    n = groups[0].shape[0] // 4
    h = n // 2

    def part(k, j):
        return groups[k][j * n : (j + 1) * n]

    def plus(*terms):
        return sum(t.astype(jnp.float32) for t in terms).astype(jnp.bfloat16)

    dx = to_x(part(2, 3)[h:])
    dy = to_y(part(2, 3)[:h])
    far_x = cat(plus(part(2, 1)[:h], dy), part(2, 1)[h:])
    far_y = cat(part(2, 2)[:h], plus(part(2, 2)[h:], dx))
    cx = to_x(cat(far_x, part(1, 3)[h:], part(3, 3)[h:]))
    cy = to_y(cat(far_y, part(1, 3)[:h], part(3, 3)[:h]))
    far = to_z(plus(part(2, 0), cx[:n], cy[:n]), 2)
    bx = to_x(
        cat(
            plus(part(1, 1)[:h], cy[n : n + h]),
            part(1, 1)[h:],
            plus(part(3, 1)[:h], cy[n + h :]),
            part(3, 1)[h:],
            part(0, 3)[h:],
        )
    )
    by = to_y(
        cat(
            part(1, 2)[:h],
            plus(part(1, 2)[h:], cx[n : n + h]),
            part(3, 2)[:h],
            plus(part(3, 2)[h:], cx[n + h :]),
            part(0, 3)[:h],
        )
    )
    below = to_z(plus(part(1, 0), bx[:n], by[:n]), 3)
    above = to_z(plus(part(3, 0), bx[n : 2 * n], by[n : 2 * n]), 1)
    own_x = to_x(cat(plus(part(0, 1)[:h], by[2 * n :]), part(0, 1)[h:]))
    own_y = to_y(cat(part(0, 2)[:h], plus(part(0, 2)[h:], bx[2 * n :])))
    return plus(part(0, 0), own_x, own_y, below, above, far)


def expert_kernel(
    group_count,
    expert_count,
    first_ref,
    ids_ref,
    gates_ref,
    own_ref,
    other_ref,
    gate_ref,
    up_ref,
    down_ref,
    own_out,
    other_out,
    slots,
    results,
    select,
    scales,
):
    step = pl.program_id(0)
    half = own_ref.shape[0]
    lanes = 2 * half
    piece = half // JOIN
    block = JOIN * CAP
    width = own_ref.shape[1]

    @pl.when(step < group_count)
    def _():
        group = step
        first = first_ref[0]
        ids, gates = ids_ref[...], gates_ref[...]
        earlier = lax.broadcasted_iota(jnp.int32, (lanes, lanes), 0)
        later = lax.broadcasted_iota(jnp.int32, (lanes, lanes), 1)
        same = ((earlier // piece) % JOIN) == ((later // piece) % JOIN)
        before = jnp.where(same & (earlier < later), 1.0, 0.0).astype(jnp.bfloat16)
        named, gated = [], []
        for e in range(expert_count):
            hit = ids == (first + e).astype(jnp.float32)
            named.append(jnp.sum(jnp.where(hit, 1.0, 0.0), axis=0, keepdims=True))
            gated.append(jnp.sum(jnp.where(hit, gates, 0.0), axis=0, keepdims=True))
        padded = named + [jnp.zeros_like(named[0])] * (-expert_count % 8)
        places = jnp.dot(
            jnp.concatenate(padded, axis=0).astype(jnp.bfloat16),
            before,
            preferred_element_type=jnp.float32,
        )
        slot = lax.broadcasted_iota(jnp.int32, (block, lanes), 0)
        lane = lax.broadcasted_iota(jnp.int32, (block, lanes), 1)
        fits = (slot // CAP) == ((lane // piece) % JOIN)
        place = (slot % CAP).astype(jnp.float32)
        at = pl.ds(pl.multiple_of(group * block, block), block)
        for e in range(expert_count):
            wanted = jnp.where(named[e] > 0.5, places[e : e + 1], -1.0)
            picked = jnp.where(fits & (wanted == place), 1.0, 0.0)
            scale = jnp.sum(picked * gated[e], axis=1, keepdims=True)
            scales[e, at, :] = jnp.broadcast_to(scale, (block, 128))
            select[group, e * block : (e + 1) * block, :] = picked.astype(jnp.bfloat16)
        chosen = select[group]
        for c in range(0, width, COLS):
            rows = jnp.concatenate([own_ref[:, c : c + COLS], other_ref[:, c : c + COLS]], axis=0)
            sorted_rows = jnp.dot(chosen, rows, preferred_element_type=jnp.float32)
            for e in range(expert_count):
                slots[e, at, c : c + COLS] = sorted_rows[e * block : (e + 1) * block].astype(
                    jnp.bfloat16
                )

    @pl.when((step >= group_count) & (step < group_count + expert_count))
    def _():
        e = step - group_count
        rows = slots[e]
        gate = jnp.dot(rows, gate_ref[0], preferred_element_type=jnp.float32)
        up = jnp.dot(rows, up_ref[0], preferred_element_type=jnp.float32)
        hidden = (gate / (1.0 + jnp.exp(-gate))) * up * scales[e][:, :1]
        hidden = hidden.astype(jnp.bfloat16)
        for c in range(0, width, COLS):
            results[e, :, c : c + COLS] = jnp.dot(
                hidden, down_ref[0, :, c : c + COLS], preferred_element_type=jnp.float32
            ).astype(jnp.bfloat16)

    @pl.when(step >= group_count + expert_count)
    def _():
        group = step - group_count - expert_count
        chosen = select[group]
        at = pl.ds(pl.multiple_of(group * block, block), block)
        for c in range(0, width, COLS):
            outs = jnp.concatenate(
                [results[e, at, c : c + COLS] for e in range(expert_count)], axis=0
            )
            rows = lax.dot_general(
                chosen, outs, (((0,), (0,)), ((), ())), preferred_element_type=jnp.float32
            ).astype(jnp.bfloat16)
            own_out[:, c : c + COLS] = rows[:half]
            other_out[:, c : c + COLS] = rows[half:]


def expert_sums(own, other, ids, gates, first, gate_weight, up_weight, down_weight):
    expert_count, width, hidden = gate_weight.shape
    lanes = 8 * CAP * JOIN
    half = lanes // 2
    group_count = own.shape[0] // half
    slot_rows = group_count * JOIN * CAP

    def dealt(i, first_ref):
        return (jnp.minimum(i, group_count - 1), 0)

    def lane_block(i, first_ref):
        return (0, jnp.minimum(i, group_count - 1))

    def expert(i, first_ref):
        return (jnp.clip(i - group_count, 0, expert_count - 1), 0, 0)

    def summed(i, first_ref):
        return (jnp.maximum(i - group_count - expert_count, 0), 0)

    row_block = pl.BlockSpec((half, width), dealt)
    out_block = pl.BlockSpec((half, width), summed)
    weight_bytes = 3 * expert_count * width * hidden * 2
    return pl.pallas_call(
        functools.partial(expert_kernel, group_count, expert_count),
        out_shape=(jax.ShapeDtypeStruct(own.shape, jnp.bfloat16),) * 2,
        grid_spec=pltpu.PrefetchScalarGridSpec(
            num_scalar_prefetch=1,
            grid=(2 * group_count + expert_count,),
            in_specs=[
                pl.BlockSpec((ids.shape[0], lanes), lane_block),
                pl.BlockSpec((ids.shape[0], lanes), lane_block),
                row_block,
                row_block,
                pl.BlockSpec((1, width, hidden), expert),
                pl.BlockSpec((1, width, hidden), expert),
                pl.BlockSpec((1, hidden, width), expert),
            ],
            out_specs=[out_block, out_block],
            scratch_shapes=[
                pltpu.VMEM((expert_count, slot_rows, width), jnp.bfloat16),
                pltpu.VMEM((expert_count, slot_rows, width), jnp.bfloat16),
                pltpu.VMEM((group_count, expert_count * JOIN * CAP, lanes), jnp.bfloat16),
                pltpu.VMEM((expert_count, slot_rows, 128), jnp.float32),
            ],
        ),
        compiler_params=pltpu.CompilerParams(
            dimension_semantics=("arbitrary",), vmem_limit_bytes=56 * 1024 * 1024
        ),
        cost_estimate=pl.CostEstimate(
            flops=2 * slot_rows * weight_bytes // 2,
            bytes_accessed=weight_bytes,
            transcendentals=expert_count * slot_rows * hidden,
        ),
    )(first, ids, gates, own, other, gate_weight, up_weight, down_weight)


def route_rows(moe_rows, routes, route_gates, gate_weight, up_weight, down_weight):
    owners = lax.axis_size("ep")
    row_count, width = moe_rows.shape
    half = row_count // 2
    core, chip = lax.axis_index("ctx"), lax.axis_index("ep")
    local_experts = gate_weight.shape[0]
    group_count = owners // JOIN

    mine = lax.dynamic_slice_in_dim(moe_rows, core * half, half, 0)
    if plane_of(owners):
        own_groups = gather_rows(mine)
        other_groups = [swap_ctx(g) for g in own_groups]
        own, other = cat(*own_groups), cat(*other_groups)
        steps = jnp.arange(owners, dtype=jnp.int32)
        order = ((chip // 4 - steps // 4) % 4) * 4 + ((chip % 4) ^ (steps % 4))
    else:
        own = lax.all_gather(mine, "ep", tiled=True)
        other = swap_ctx(own)
        order = jnp.arange(owners, dtype=jnp.int32)

    named = jnp.concatenate([routes.astype(jnp.float32), route_gates], axis=1)
    named = lax.all_gather(named, "ep").reshape(owners, -1)
    placed = order[:, None] == jnp.arange(owners, dtype=jnp.int32)[None, :]
    named = jnp.sum(jnp.where(placed[:, :, None], named[None], 0.0), axis=1)
    named = named.reshape(group_count, JOIN, 2, half, -1)
    named = jnp.where(core == 0, named, named[:, :, ::-1])
    named = named.transpose(4, 0, 2, 1, 3).reshape(named.shape[-1], -1)
    top = routes.shape[1]
    first = (chip * local_experts).astype(jnp.int32).reshape(1)

    own_sums, other_sums = expert_sums(
        own, other, named[:top], named[top:], first, gate_weight, up_weight, down_weight
    )

    if plane_of(owners):
        rows = JOIN * half
        groups = [None] * group_count
        for k in (2, 1, 3, 0):
            at = slice(k * rows, (k + 1) * rows)
            groups[k] = own_sums[at] + swap_ctx(other_sums[at])
        own_final = scatter_sums(groups)
    else:
        both = own_sums + swap_ctx(other_sums)
        own_final = lax.psum_scatter(both, "ep", scatter_dimension=0, tiled=True)
    other_final = swap_ctx(own_final)
    return jnp.where(core == 0, cat(own_final, other_final), cat(other_final, own_final))


def body(
    moe_rows,
    routes,
    route_gates,
    gate_weight,
    up_weight,
    down_weight,
    queries,
    latent_cache,
    cache_lengths,
):
    routed_output = route_rows(moe_rows, routes, route_gates, gate_weight, up_weight, down_weight)
    attention_output = attend_local(queries, latent_cache, cache_lengths)
    return (routed_output, attention_output)


def solution(mesh):
    in_specs = (
        P("ep", None),
        P("ep", None),
        P("ep", None),
        P("ep", None, "ctx"),
        P("ep", None, "ctx"),
        P("ep", "ctx", None),
        P("ep", None, None),
        P("ep", "ctx", None),
        P("ep"),
    )
    out_specs = (P("ep", None), P("ep", "ctx", None))
    return jax.shard_map(body, mesh=mesh, in_specs=in_specs, out_specs=out_specs, check_vma=False)
```

time: 461 us -> 223 us (0.48)
  the two profiles are of different devices: /device:TPU:28 before, /device:TPU:0 now
where the time goes in v1:
time: 223 us; the launch traced here: 222 us
  waiting for transfers between devices  69.6 us (31%)
  Pallas kernels  39 us (17%)
  blocking collectives  38.4 us (17%)
  local copies, waits for them, and re-layouts  25.8 us (12%)
  starting transfers between devices  24.4 us (11%)
  other arithmetic  21.1 us (9%)
    ppermute x22, waiting for transfers between devices, send(): return lax.ppermute(x, 'ep', [(i, target(i)) for i in range(count)])  64.2 us
    pallas_call x1, Pallas kernels, expert_sums(): pl.pallas_call(functools.partial(expert_kernel, group_count, expert_count...  39 us
    all_gather x1, blocking collectives, route_rows(): named = lax.all_gather(named, 'ep').reshape(owners, -1)  38.4 us
    ppermute x22, starting transfers between devices, send(): return lax.ppermute(x, 'ep', [(i, target(i)) for i in range(count)])  22.8 us
    unnamed x27, local copies, waits for them, and re-layouts  14.3 us
    unnamed x5, other arithmetic  5.57 us
    concatenate x7, other arithmetic, cat(): return jnp.concatenate(pieces, axis=0)  5.48 us
    ppermute x10, waiting for transfers between devices, swap_ctx(): return lax.ppermute(x, 'ctx', [(0, 1), (1, 0)])  5.46 us
  transfers between devices with their start and end apart: 32, of which 19 were waited for; matrix products, arithmetic and copies ran while one was open for 15% of the time, Pallas kernels for 0%

profile of v1, /device:TPU:0, one launch (start us, length us, event | category | flops | bytes accessed | tf_op | source)
XLA Modules:
  0.0 222.1 jit_solution(9975303746824150581)
XLA Ops:
  0.7 1.7 constant_dynamic-update-slice_fusion.18
  2.4 2.9 %collective-permute-start = (bf16[32,3584]{1,0:T(8,128)(2,1)S(1)}, bf16[32,3584]{1,0:T(8,128)(2,1)S(1)}, u32[]{:S(2)}, u32[]{:S(2)}) collective-permute-start(bf16[32,3584]{1,0:T(8,128)(2,1)S(1)} %get-tuple-element.5), channel_id=1, source_target_pairs={{0,1},{1,0},{2,3},{3,2},{4,5},{5,4},{6,7},{7,6},{8,9},{9,8},{10,11... | collective-permute-start | bytes 688136 | tf_op jit(solution)/shard_map/ppermute | solution.py:69
  5.3 1.5 collective-permute-start.1
  6.8 1.6 collective-permute-start.2
  8.4 2.2 %collective-permute-start.3 = (bf16[32,3584]{1,0:T(8,128)(2,1)S(1)}, bf16[32,3584]{1,0:T(8,128)(2,1)S(1)}, u32[]{:S(2)}, u32[]{:S(2)}) collective-permute-start(bf16[32,3584]{1,0:T(8,128)(2,1)S(1)} %get-tuple-element.5), channel_id=1, source_target_pairs={{0,12},{1,13},{2,14},{3,15},{4,0},{5,1},{6,2},{7,3},{8,4},{9,5},{1... | collective-permute-start | bytes 688136 | tf_op jit(solution)/shard_map/ppermute | solution.py:69
  10.6 0.7 constant_dynamic-update-slice_fusion.13
  12.8 4.4 %collective-permute-done.2 = bf16[32,3584]{1,0:T(8,128)(2,1)S(1)} collective-permute-done((bf16[32,3584]{1,0:T(8,128)(2,1)S(1)}, bf16[32,3584]{1,0:T(8,128)(2,1)S(1)}, u32[]{:S(2)}, u32[]{:S(2)}) %collective-permute-start.2) | collective-permute-done | bytes 229408 | tf_op jit(solution)/shard_map/ppermute | solution.py:69
  17.2 2.6 %collective-permute-done.3 = bf16[32,3584]{1,0:T(8,128)(2,1)S(1)} collective-permute-done((bf16[32,3584]{1,0:T(8,128)(2,1)S(1)}, bf16[32,3584]{1,0:T(8,128)(2,1)S(1)}, u32[]{:S(2)}, u32[]{:S(2)}) %collective-permute-start.3) | collective-permute-done | bytes 229408 | tf_op jit(solution)/shard_map/ppermute | solution.py:69
  21.0 1.3 collective-permute-start.6
  22.3 0.8 constant_dynamic-update-slice_fusion.17
  23.1 0.8 constant_dynamic-update-slice_fusion.16
  23.9 10.3 %collective-permute-done.4 = bf16[80,3584]{1,0:T(8,128)(2,1)S(1)} collective-permute-done((bf16[80,3584]{1,0:T(8,128)(2,1)S(1)}, bf16[80,3584]{1,0:T(8,128)(2,1)S(1)}, u32[]{:S(2)}, u32[]{:S(2)}) %collective-permute-start.4) | collective-permute-done | bytes 573472 | tf_op jit(solution)/shard_map/ppermute | solution.py:69
  34.2 0.7 constant_dynamic-update-slice_fusion.15
  34.9 0.7 constant_dynamic-update-slice_fusion.14
  35.7 1.1 collective-permute-start.7
  37.3 0.8 constant_dynamic-update-slice_fusion.21
  38.1 0.7 slice_dynamic-update-slice_fusion.11
  38.8 0.7 slice_dynamic-update-slice_fusion.9
  39.6 7.0 %collective-permute-done.7 = bf16[64,3584]{1,0:T(8,128)(2,1)S(1)} collective-permute-done((bf16[64,3584]{1,0:T(8,128)(2,1)S(1)}, bf16[64,3584]{1,0:T(8,128)(2,1)S(1)}, u32[]{:S(2)}, u32[]{:S(2)}) %collective-permute-start.7) | collective-permute-done | bytes 458784 | tf_op jit(solution)/shard_map/ppermute | solution.py:69
  47.9 1.1 collective-permute-start.9
  49.6 0.8 constant_dynamic-update-slice_fusion.24
  50.4 0.8 slice_dynamic-update-slice_fusion.6
  51.2 0.8 slice_dynamic-update-slice_fusion.4
  52.0 0.7 collective-permute-done.9
  53.8 0.7 constant_dynamic-update-slice_fusion.22
  54.5 0.8 constant_dynamic-update-slice_fusion.27
  55.4 0.9 slice_dynamic-update-slice_fusion.10
  56.3 0.9 slice_dynamic-update-slice_fusion.8
  57.2 0.7 constant_dynamic-update-slice_fusion.20
  57.9 0.8 constant_dynamic-update-slice_fusion.19
  59.2 38.4 %all-gather.1 = f32[16,64,16]{1,2,0:T(8,128)S(1)} all-gather(f32[1,64,16]{1,2,0:T(8,128)S(1)} %maximum_bitcast_fusion), channel_id=2, replica_groups=mesh['ctx'=2,'ep'=16] {'ep'}, dimensions={0}, use_global_device_ids=true | all-gather | bytes 69632 | tf_op jit(solution)/shard_map/all_gather | solution.py:325
  99.1 0.8 slice.280.ids_ref
  100.1 0.8 slice.282.gates_ref
  100.9 5.2 %pad_maximum_fusion.other_ref = bf16[512,3584]{1,0:T(8,128)(2,1)} fusion(bf16[128,3584]{1,0:T(8,128)(2,1)} %collective-permute-done.14, bf16[128,3584]{1,0:T(8,128)(2,1)} %collective-permute-done.13, bf16[128,3584]{1,0:T(8,128)(2,1)S(1)} %collective-permute-done.12, bf16[128,3584]{1,0:T(8,128)(2,1)S(1)} %collective-permute-done.11), kind=kLoop, calls=%fused_computation | loop fusion | flops 14680064 | bytes 7340032 | tf_op jit(solution)/shard_map/concatenate | solution.py:85
  106.1 39.0 %shard_map.104 = (bf16[512,3584]{1,0:T(8,128)(2,1)}, bf16[512,3584]{1,0:T(8,128)(2,1)}) custom-call(s32[1]{0:T(128)} %bitcast.first_ref, f32[8,1024]{1,0:T(8,128)} %slice.280.ids_ref, f32[8,1024]{1,0:T(8,128)} %slice.282.gates_ref, bf16[512,3584]{1,0:T(8,128)(2,1)} %get-tuple-element.61.own_ref, bf16[512,3584]{1,0:T(8,128)(2,1)} %pad_maximum_fusion.other_ref, ...), custom_call_target="tpu_custom_call" | custom-call | flops 11274289152 | bytes 88080384 | tf_op jit(solution)/shard_map/pallas_call | solution.py:270
  145.1 3.3 %fusion.39 = (bf16[128,3584]{1,0:T(8,128)(2,1)}, bf16[128,3584]{1,0:T(8,128)(2,1)S(1)}, bf16[128,3584]{1,0:T(8,128)(2,1)S(1)}, bf16[128,3584]{1,0:T(8,128)(2,1)S(1)}) fusion(bf16[512,3584]{1,0:T(8,128)(2,1)} %get-tuple-element.7), kind=kLoop, calls=%fused_computation.127 | loop fusion | bytes 7340032 | tf_op jit(solution)/shard_map/slice | solution.py:343
  150.1 2.4 %collective-permute-done.15 = bf16[128,3584]{1,0:T(8,128)(2,1)} collective-permute-done((bf16[128,3584]{1,0:T(8,128)(2,1)}, bf16[128,3584]{1,0:T(8,128)(2,1)}, u32[]{:S(2)}, u32[]{:S(2)}) %collective-permute-start.15) | collective-permute-done | bytes 917536 | tf_op jit(solution)/shard_map/ppermute | solution.py:40
  152.5 1.1 collective-permute-done.17
  153.6 1.3 collective-permute-done.19
  154.9 3.5 %slice_add_fusion.3 = (bf16[128,3584]{1,0:T(8,128)(2,1)S(1)}, bf16[128,3584]{1,0:T(8,128)(2,1)S(1)}, bf16[128,3584]{1,0:T(8,128)(2,1)S(1)}, bf16[128,3584]{1,0:T(8,128)(2,1)S(1)}) fusion(bf16[128,3584]{1,0:T(8,128)(2,1)} %collective-permute-done.15, bf16[512,3584]{1,0:T(8,128)(2,1)} %get-tuple-element.6, bf16[128,3584]{1,0:T(8,128)(2,1)} %collective-permute-done.19, ...), kind=kLoop, calls=%fused_computation.13 | loop fusion | flops 1835008 | bytes 11010048 | tf_op jit(solution)/shard_map/add | solution.py:343
  158.7 5.1 %collective-permute-done.18 = bf16[16,3584]{1,0:T(8,128)(2,1)S(1)} collective-permute-done((bf16[16,3584]{1,0:T(8,128)(2,1)S(1)}, bf16[16,3584]{1,0:T(8,128)(2,1)S(1)}, u32[]{:S(2)}, u32[]{:S(2)}) %collective-permute-start.18) | collective-permute-done | bytes 114720 | tf_op jit(solution)/shard_map/ppermute | solution.py:69
  163.9 1.7 collective-permute-start.24
  166.3 1.5 fusion.11
  167.8 7.9 %collective-permute-done.24 = bf16[64,3584]{1,0:T(8,128)(2,1)S(1)} collective-permute-done((bf16[64,3584]{1,0:T(8,128)(2,1)S(1)}, bf16[64,3584]{1,0:T(8,128)(2,1)S(1)}, u32[]{:S(2)}, u32[]{:S(2)}) %collective-permute-start.24) | collective-permute-done | bytes 458784 | tf_op jit(solution)/shard_map/ppermute | solution.py:69
  175.8 0.8 slice_dynamic-update-slice_fusion.14
  177.8 1.0 maximum_maximum_fusion
  179.4 8.1 %collective-permute-done.20 = bf16[64,3584]{1,0:T(8,128)(2,1)} collective-permute-done((bf16[64,3584]{1,0:T(8,128)(2,1)S(1)}, bf16[64,3584]{1,0:T(8,128)(2,1)}, u32[]{:S(2)}, u32[]{:S(2)}) %collective-permute-start.20) | collective-permute-done | bytes 458784 | tf_op jit(solution)/shard_map/ppermute | solution.py:69
  187.5 1.6 fusion.23
  189.2 1.6 fusion.26
  190.8 1.6 slice_dynamic-update-slice_fusion.13
  192.4 0.7 fusion.40
  193.1 1.0 collective-permute-start.21
  194.1 0.9 collective-permute-start.25
  195.0 1.1 add_convert_fusion.1
  196.3 9.4 %collective-permute-done.21 = bf16[80,3584]{1,0:T(8,128)(2,1)S(1)} collective-permute-done((bf16[80,3584]{1,0:T(8,128)(2,1)}, bf16[80,3584]{1,0:T(8,128)(2,1)S(1)}, u32[]{:S(2)}, u32[]{:S(2)}) %collective-permute-start.21) | collective-permute-done | bytes 573472 | tf_op jit(solution)/shard_map/ppermute | solution.py:69
  205.7 1.5 collective-permute-done.25
  207.2 0.9 collective-permute-start.22
  208.2 1.3 collective-permute-start.26
  209.5 1.1 add_convert_fusion.3
  210.7 2.0 collective-permute-start.28
  213.3 1.0 collective-permute-done.26
  214.3 5.3 %collective-permute-done.27 = bf16[32,3584]{1,0:T(8,128)(2,1)S(1)} collective-permute-done((bf16[32,3584]{1,0:T(8,128)(2,1)S(1)}, bf16[32,3584]{1,0:T(8,128)(2,1)S(1)}, u32[]{:S(2)}, u32[]{:S(2)}) %collective-permute-start.27) | collective-permute-done | bytes 229408 | tf_op jit(solution)/shard_map/ppermute | solution.py:69
  220.0 0.7 fusion.28
  221.3 0.8 maximum_select_fusion
  (87 shorter events, 14.2 us)
Async XLA Ops:
  0.6 165.0 %copy-start = (bf16[1,64,576]{2,1,0:T(8,128)(2,1)S(1)}, bf16[1,64,576]{2,1,0:T(8,128)(2,1)}, u32[]{:S(2)}) copy-start(bf16[1,64,576]{2,1,0:T(8,128)(2,1)} %param.15) | copy-start | bytes 221188
  2.4 10.4 %collective-permute-start = (bf16[32,3584]{1,0:T(8,128)(2,1)S(1)}, bf16[32,3584]{1,0:T(8,128)(2,1)S(1)}, u32[]{:S(2)}, u32[]{:S(2)}) collective-permute-start(bf16[32,3584]{1,0:T(8,128)(2,1)S(1)} %get-tuple-element.5), channel_id=1, source_target_pairs={{0,1},{1,0},{2,3},{3,2},{4,5},{5,4},{6,7},{7,6},{8,9},{9,8},{10,11... | collective-permute-start | bytes 688136 | tf_op jit(solution)/shard_map/ppermute | solution.py:69
  5.3 7.4 %collective-permute-start.1 = (bf16[32,3584]{1,0:T(8,128)(2,1)S(1)}, bf16[32,3584]{1,0:T(8,128)(2,1)S(1)}, u32[]{:S(2)}, u32[]{:S(2)}) collective-permute-start(bf16[32,3584]{1,0:T(8,128)(2,1)S(1)} %get-tuple-element.5), channel_id=1, source_target_pairs={{0,2},{1,3},{2,0},{3,1},{4,6},{5,7},{6,4},{7,5},{8,10},{9,11},{10,... | collective-permute-start | bytes 688136 | tf_op jit(solution)/shard_map/ppermute | solution.py:69
  6.8 10.4 %collective-permute-start.2 = (bf16[32,3584]{1,0:T(8,128)(2,1)S(1)}, bf16[32,3584]{1,0:T(8,128)(2,1)S(1)}, u32[]{:S(2)}, u32[]{:S(2)}) collective-permute-start(bf16[32,3584]{1,0:T(8,128)(2,1)S(1)} %get-tuple-element.5), channel_id=1, source_target_pairs={{0,4},{1,5},{2,6},{3,7},{4,8},{5,9},{6,10},{7,11},{8,12},{9,13},{1... | collective-permute-start | bytes 688136 | tf_op jit(solution)/shard_map/ppermute | solution.py:69
  8.4 11.4 %collective-permute-start.3 = (bf16[32,3584]{1,0:T(8,128)(2,1)S(1)}, bf16[32,3584]{1,0:T(8,128)(2,1)S(1)}, u32[]{:S(2)}, u32[]{:S(2)}) collective-permute-start(bf16[32,3584]{1,0:T(8,128)(2,1)S(1)} %get-tuple-element.5), channel_id=1, source_target_pairs={{0,12},{1,13},{2,14},{3,15},{4,0},{5,1},{6,2},{7,3},{8,4},{9,5},{1... | collective-permute-start | bytes 688136 | tf_op jit(solution)/shard_map/ppermute | solution.py:69
  19.9 14.3 %collective-permute-start.4 = (bf16[80,3584]{1,0:T(8,128)(2,1)S(1)}, bf16[80,3584]{1,0:T(8,128)(2,1)S(1)}, u32[]{:S(2)}, u32[]{:S(2)}) collective-permute-start(bf16[80,3584]{1,0:T(8,128)(2,1)S(1)} %get-tuple-element.74), channel_id=1, source_target_pairs={{0,2},{1,3},{2,0},{3,1},{4,6},{5,7},{6,4},{7,5},{8,10},{9,11},{10,... | collective-permute-start | bytes 1720328 | tf_op jit(solution)/shard_map/ppermute | solution.py:69
  20.5 14.4 %collective-permute-start.5 = (bf16[80,3584]{1,0:T(8,128)(2,1)S(1)}, bf16[80,3584]{1,0:T(8,128)(2,1)S(1)}, u32[]{:S(2)}, u32[]{:S(2)}) collective-permute-start(bf16[80,3584]{1,0:T(8,128)(2,1)S(1)} %get-tuple-element.73), channel_id=1, source_target_pairs={{0,1},{1,0},{2,3},{3,2},{4,5},{5,4},{6,7},{7,6},{8,9},{9,8},{10,11... | collective-permute-start | bytes 1720328 | tf_op jit(solution)/shard_map/ppermute | solution.py:69
  21.0 14.6 %collective-permute-start.6 = (bf16[32,3584]{1,0:T(8,128)(2,1)S(1)}, bf16[32,3584]{1,0:T(8,128)(2,1)S(1)}, u32[]{:S(2)}, u32[]{:S(2)}) collective-permute-start(bf16[32,3584]{1,0:T(8,128)(2,1)S(1)} %get-tuple-element.5), channel_id=1, source_target_pairs={{0,8},{1,9},{2,10},{3,11},{4,12},{5,13},{6,14},{7,15},{8,0},{9,1},... | collective-permute-start | bytes 688136 | tf_op jit(solution)/shard_map/ppermute | solution.py:69
  35.7 10.9 %collective-permute-start.7 = (bf16[64,3584]{1,0:T(8,128)(2,1)S(1)}, bf16[64,3584]{1,0:T(8,128)(2,1)S(1)}, u32[]{:S(2)}, u32[]{:S(2)}) collective-permute-start(bf16[64,3584]{1,0:T(8,128)(2,1)S(1)} %get-tuple-element.86), channel_id=1, source_target_pairs={{0,2},{1,3},{2,0},{3,1},{4,6},{5,7},{6,4},{7,5},{8,10},{9,11},{10,... | collective-permute-start | bytes 1376264 | tf_op jit(solution)/shard_map/ppermute | solution.py:69
  36.8 10.5 %collective-permute-start.8 = (bf16[64,3584]{1,0:T(8,128)(2,1)S(1)}, bf16[64,3584]{1,0:T(8,128)(2,1)S(1)}, u32[]{:S(2)}, u32[]{:S(2)}) collective-permute-start(bf16[64,3584]{1,0:T(8,128)(2,1)S(1)} %get-tuple-element.85), channel_id=1, source_target_pairs={{0,1},{1,0},{2,3},{3,2},{4,5},{5,4},{6,7},{7,6},{8,9},{9,8},{10,11... | collective-permute-start | bytes 1376264 | tf_op jit(solution)/shard_map/ppermute | solution.py:69
  37.3 63.6 %collective-permute-start.11 = (bf16[128,3584]{1,0:T(8,128)(2,1)}, bf16[128,3584]{1,0:T(8,128)(2,1)S(1)}, u32[]{:S(2)}, u32[]{:S(2)}) collective-permute-start(bf16[128,3584]{1,0:T(8,128)(2,1)} %get-tuple-element.43), channel_id=1, source_target_pairs={{0,16},{16,0},{1,17},{17,1},{2,18},{18,2},{3,19},{19,3},{4,20},{20... | collective-permute-start | bytes 2752520 | tf_op jit(solution)/shard_map/ppermute | solution.py:40
  47.9 4.8 %collective-permute-start.9 = (bf16[16,3584]{1,0:T(8,128)(2,1)S(1)}, bf16[16,3584]{1,0:T(8,128)(2,1)S(1)}, u32[]{:S(2)}, u32[]{:S(2)}) collective-permute-start(bf16[16,3584]{1,0:T(8,128)(2,1)S(1)} %get-tuple-element.71), channel_id=1, source_target_pairs={{0,2},{1,3},{2,0},{3,1},{4,6},{5,7},{6,4},{7,5},{8,10},{9,11},{10,... | collective-permute-start | bytes 344072 | tf_op jit(solution)/shard_map/ppermute | solution.py:69
  49.0 4.8 %collective-permute-start.10 = (bf16[16,3584]{1,0:T(8,128)(2,1)S(1)}, bf16[16,3584]{1,0:T(8,128)(2,1)S(1)}, u32[]{:S(2)}, u32[]{:S(2)}) collective-permute-start(bf16[16,3584]{1,0:T(8,128)(2,1)S(1)} %get-tuple-element.69), channel_id=1, source_target_pairs={{0,1},{1,0},{2,3},{3,2},{4,5},{5,4},{6,7},{7,6},{8,9},{9,8},{10,11... | collective-permute-start | bytes 344072 | tf_op jit(solution)/shard_map/ppermute | solution.py:69
  58.7 42.2 %collective-permute-start.12 = (bf16[128,3584]{1,0:T(8,128)(2,1)}, bf16[128,3584]{1,0:T(8,128)(2,1)S(1)}, u32[]{:S(2)}, u32[]{:S(2)}) collective-permute-start(bf16[128,3584]{1,0:T(8,128)(2,1)} %get-tuple-element.59), channel_id=1, source_target_pairs={{0,16},{16,0},{1,17},{17,1},{2,18},{18,2},{3,19},{19,3},{4,20},{20... | collective-permute-start | bytes 2752520 | tf_op jit(solution)/shard_map/ppermute | solution.py:40
  58.7 42.2 %collective-permute-start.14 = (bf16[128,3584]{1,0:T(8,128)(2,1)}, bf16[128,3584]{1,0:T(8,128)(2,1)}, u32[]{:S(2)}, u32[]{:S(2)}) collective-permute-start(bf16[128,3584]{1,0:T(8,128)(2,1)} %get-tuple-element.60), channel_id=1, source_target_pairs={{0,16},{16,0},{1,17},{17,1},{2,18},{18,2},{3,19},{19,3},{4,20},{20... | collective-permute-start | bytes 2752520 | tf_op jit(solution)/shard_map/ppermute | solution.py:40
  59.2 41.7 %collective-permute-start.13 = (bf16[128,3584]{1,0:T(8,128)(2,1)}, bf16[128,3584]{1,0:T(8,128)(2,1)}, u32[]{:S(2)}, u32[]{:S(2)}) collective-permute-start(bf16[128,3584]{1,0:T(8,128)(2,1)} %get-tuple-element.87), channel_id=1, source_target_pairs={{0,16},{16,0},{1,17},{17,1},{2,18},{18,2},{3,19},{19,3},{4,20},{20... | collective-permute-start | bytes 2752520 | tf_op jit(solution)/shard_map/ppermute | solution.py:40
  148.4 4.1 %collective-permute-start.15 = (bf16[128,3584]{1,0:T(8,128)(2,1)}, bf16[128,3584]{1,0:T(8,128)(2,1)}, u32[]{:S(2)}, u32[]{:S(2)}) collective-permute-start(bf16[128,3584]{1,0:T(8,128)(2,1)} %get-tuple-element.16), channel_id=1, source_target_pairs={{0,16},{16,0},{1,17},{17,1},{2,18},{18,2},{3,19},{19,3},{4,20},{20... | collective-permute-start | bytes 2752520 | tf_op jit(solution)/shard_map/ppermute | solution.py:40
  148.4 4.1 %collective-permute-start.16 = (bf16[128,3584]{1,0:T(8,128)(2,1)S(1)}, bf16[128,3584]{1,0:T(8,128)(2,1)}, u32[]{:S(2)}, u32[]{:S(2)}) collective-permute-start(bf16[128,3584]{1,0:T(8,128)(2,1)S(1)} %get-tuple-element.19), channel_id=1, source_target_pairs={{0,16},{16,0},{1,17},{17,1},{2,18},{18,2},{3,19},{19,3},{4,20},{20... | collective-permute-start | bytes 2752520 | tf_op jit(solution)/shard_map/ppermute | solution.py:40
  148.9 4.7 %collective-permute-start.17 = (bf16[128,3584]{1,0:T(8,128)(2,1)S(1)}, bf16[128,3584]{1,0:T(8,128)(2,1)}, u32[]{:S(2)}, u32[]{:S(2)}) collective-permute-start(bf16[128,3584]{1,0:T(8,128)(2,1)S(1)} %get-tuple-element.18), channel_id=1, source_target_pairs={{0,16},{16,0},{1,17},{17,1},{2,18},{18,2},{3,19},{19,3},{4,20},{20... | collective-permute-start | bytes 2752520 | tf_op jit(solution)/shard_map/ppermute | solution.py:40
  148.9 6.0 %collective-permute-start.19 = (bf16[128,3584]{1,0:T(8,128)(2,1)S(1)}, bf16[128,3584]{1,0:T(8,128)(2,1)}, u32[]{:S(2)}, u32[]{:S(2)}) collective-permute-start(bf16[128,3584]{1,0:T(8,128)(2,1)S(1)} %get-tuple-element.17), channel_id=1, source_target_pairs={{0,16},{16,0},{1,17},{17,1},{2,18},{18,2},{3,19},{19,3},{4,20},{20... | collective-permute-start | bytes 2752520 | tf_op jit(solution)/shard_map/ppermute | solution.py:40
  158.4 17.3 %copy-start.1 = (bf16[128,3584]{1,0:T(8,128)(2,1)}, bf16[128,3584]{1,0:T(8,128)(2,1)S(1)}, u32[]{:S(2)}) copy-start(bf16[128,3584]{1,0:T(8,128)(2,1)S(1)} %get-tuple-element.15) | copy-start | bytes 2752516
  158.4 7.2 %copy-start.2 = (bf16[1,2048,576]{1,2,0:T(8,128)(2,1)S(1)}, bf16[1,2048,576]{1,2,0:T(8,128)(2,1)}, u32[]{:S(2)}) copy-start(bf16[1,2048,576]{1,2,0:T(8,128)(2,1)} %param.16) | copy-start | bytes 7077892
  158.5 5.3 %collective-permute-start.18 = (bf16[16,3584]{1,0:T(8,128)(2,1)S(1)}, bf16[16,3584]{1,0:T(8,128)(2,1)S(1)}, u32[]{:S(2)}, u32[]{:S(2)}) collective-permute-start(bf16[16,3584]{1,0:T(8,128)(2,1)S(1)} %get-tuple-element.37), channel_id=1, source_target_pairs={{0,2},{1,3},{2,0},{3,1},{4,6},{5,7},{6,4},{7,5},{8,10},{9,11},{10,... | collective-permute-start | bytes 344072 | tf_op jit(solution)/shard_map/ppermute | solution.py:69
  158.6 5.3 %collective-permute-start.23 = (bf16[16,3584]{1,0:T(8,128)(2,1)S(1)}, bf16[16,3584]{1,0:T(8,128)(2,1)S(1)}, u32[]{:S(2)}, u32[]{:S(2)}) collective-permute-start(bf16[16,3584]{1,0:T(8,128)(2,1)S(1)} %get-tuple-element.38), channel_id=1, source_target_pairs={{0,1},{1,0},{2,3},{3,2},{4,5},{5,4},{6,7},{7,6},{8,9},{9,8},{10,11... | collective-permute-start | bytes 344072 | tf_op jit(solution)/shard_map/ppermute | solution.py:69
  163.9 11.8 %collective-permute-start.24 = (bf16[64,3584]{1,0:T(8,128)(2,1)S(1)}, bf16[64,3584]{1,0:T(8,128)(2,1)S(1)}, u32[]{:S(2)}, u32[]{:S(2)}) collective-permute-start(bf16[64,3584]{1,0:T(8,128)(2,1)S(1)} %pad_maximum_fusion.7), channel_id=1, source_target_pairs={{0,2},{1,3},{2,0},{3,1},{4,6},{5,7},{6,4},{7,5},{8,10},{9,11},{10,... | collective-permute-start | bytes 1376264 | tf_op jit(solution)/shard_map/ppermute | solution.py:69
  175.7 1.8 copy-start.3
  176.5 1.0 copy-start.4
  176.6 11.0 %collective-permute-start.20 = (bf16[64,3584]{1,0:T(8,128)(2,1)S(1)}, bf16[64,3584]{1,0:T(8,128)(2,1)}, u32[]{:S(2)}, u32[]{:S(2)}) collective-permute-start(bf16[64,3584]{1,0:T(8,128)(2,1)S(1)} %pad_maximum_fusion.6), channel_id=1, source_target_pairs={{0,1},{1,0},{2,3},{3,2},{4,5},{5,4},{6,7},{7,6},{8,9},{9,8},{10,11... | collective-permute-start | bytes 1376264 | tf_op jit(solution)/shard_map/ppermute | solution.py:69
  179.4 31.3 %collective-permute-start.31 = (f32[1,32,640]{2,1,0:T(8,128)}, f32[1,32,640]{2,1,0:T(8,128)S(1)}, u32[]{:S(2)}, u32[]{:S(2)}) collective-permute-start(f32[1,32,640]{2,1,0:T(8,128)} %constant_dynamic-slice_fusion), channel_id=1, source_target_pairs={{0,16},{16,0},{1,17},{17,1},{2,18},{18,2},{3,19},{19,3},{4,20},{20... | collective-permute-start | bytes 245768 | tf_op jit(solution)/shard_map/ppermute | solution.py:40
  193.1 12.6 %collective-permute-start.21 = (bf16[80,3584]{1,0:T(8,128)(2,1)}, bf16[80,3584]{1,0:T(8,128)(2,1)S(1)}, u32[]{:S(2)}, u32[]{:S(2)}) collective-permute-start(bf16[80,3584]{1,0:T(8,128)(2,1)} %get-tuple-element.27), channel_id=1, source_target_pairs={{0,2},{1,3},{2,0},{3,1},{4,6},{5,7},{6,4},{7,5},{8,10},{9,11},{10,... | collective-permute-start | bytes 1720328 | tf_op jit(solution)/shard_map/ppermute | solution.py:69
  194.1 13.0 %collective-permute-start.25 = (bf16[80,3584]{1,0:T(8,128)(2,1)}, bf16[80,3584]{1,0:T(8,128)(2,1)S(1)}, u32[]{:S(2)}, u32[]{:S(2)}) collective-permute-start(bf16[80,3584]{1,0:T(8,128)(2,1)} %get-tuple-element.25), channel_id=1, source_target_pairs={{0,1},{1,0},{2,3},{3,2},{4,5},{5,4},{6,7},{7,6},{8,9},{9,8},{10,11... | collective-permute-start | bytes 1720328 | tf_op jit(solution)/shard_map/ppermute | solution.py:69
  196.2 16.7 %collective-permute-start.29 = (bf16[32,3584]{1,0:T(8,128)(2,1)S(1)}, bf16[32,3584]{1,0:T(8,128)(2,1)S(1)}, u32[]{:S(2)}, u32[]{:S(2)}) collective-permute-start(bf16[32,3584]{1,0:T(8,128)(2,1)S(1)} %add_convert_fusion.1), channel_id=1, source_target_pairs={{0,8},{1,9},{2,10},{3,11},{4,12},{5,13},{6,14},{7,15},{8,0},{9,1},... | collective-permute-start | bytes 688136 | tf_op jit(solution)/shard_map/ppermute | solution.py:69
  207.2 6.1 %collective-permute-start.22 = (bf16[32,3584]{1,0:T(8,128)(2,1)S(1)}, bf16[32,3584]{1,0:T(8,128)(2,1)S(1)}, u32[]{:S(2)}, u32[]{:S(2)}) collective-permute-start(bf16[32,3584]{1,0:T(8,128)(2,1)S(1)} %pad_maximum_fusion.8), channel_id=1, source_target_pairs={{0,1},{1,0},{2,3},{3,2},{4,5},{5,4},{6,7},{7,6},{8,9},{9,8},{10,11... | collective-permute-start | bytes 688136 | tf_op jit(solution)/shard_map/ppermute | solution.py:69
  208.2 6.1 %collective-permute-start.26 = (bf16[32,3584]{1,0:T(8,128)(2,1)S(1)}, bf16[32,3584]{1,0:T(8,128)(2,1)S(1)}, u32[]{:S(2)}, u32[]{:S(2)}) collective-permute-start(bf16[32,3584]{1,0:T(8,128)(2,1)S(1)} %pad_maximum_fusion.9), channel_id=1, source_target_pairs={{0,2},{1,3},{2,0},{3,1},{4,6},{5,7},{6,4},{7,5},{8,10},{9,11},{10,... | collective-permute-start | bytes 688136 | tf_op jit(solution)/shard_map/ppermute | solution.py:69
  210.6 8.9 %collective-permute-start.27 = (bf16[32,3584]{1,0:T(8,128)(2,1)S(1)}, bf16[32,3584]{1,0:T(8,128)(2,1)S(1)}, u32[]{:S(2)}, u32[]{:S(2)}) collective-permute-start(bf16[32,3584]{1,0:T(8,128)(2,1)S(1)} %get-tuple-element.20), channel_id=1, source_target_pairs={{0,12},{1,13},{2,14},{3,15},{4,0},{5,1},{6,2},{7,3},{8,4},{9,5},{1... | collective-permute-start | bytes 688136 | tf_op jit(solution)/shard_map/ppermute | solution.py:69
  210.7 8.9 %collective-permute-start.28 = (bf16[32,3584]{1,0:T(8,128)(2,1)S(1)}, bf16[32,3584]{1,0:T(8,128)(2,1)S(1)}, u32[]{:S(2)}, u32[]{:S(2)}) collective-permute-start(bf16[32,3584]{1,0:T(8,128)(2,1)S(1)} %get-tuple-element.21), channel_id=1, source_target_pairs={{0,4},{1,5},{2,6},{3,7},{4,8},{5,9},{6,10},{7,11},{8,12},{9,13},{1... | collective-permute-start | bytes 688136 | tf_op jit(solution)/shard_map/ppermute | solution.py:69
  219.7 1.6 collective-permute-start.30

commit v2 on v1

v2 whole, which is shorter than its diff:
```python
import functools

import jax
import jax.numpy as jnp
from jax import lax
from jax.experimental import pallas as pl
from jax.experimental.pallas import tpu as pltpu
from jax.sharding import PartitionSpec as P

LAT = 512
CAP = 8
JOIN = 4
COLS = 512

softmax_scale = 192.0 ** (-0.5)


def softmax_parts(queries, cache, cache_lengths, offset):
    local_span = cache.shape[1]
    scores = (
        jnp.einsum("rhk,rlk->rhl", queries, cache, preferred_element_type=jnp.float32)
        * softmax_scale
    )
    positions = offset + jnp.arange(local_span, dtype=jnp.int32)
    usable = (positions[None, :] < cache_lengths[:, None])[:, None, :]
    masked = jnp.where(usable, scores, -1e30)
    top_score = jnp.max(masked, axis=2)
    weights = jnp.where(usable, jnp.exp(masked - top_score[:, :, None]), 0.0)
    row_total = jnp.sum(weights, axis=2)
    values = jnp.einsum(
        "rhl,rlv->rhv",
        weights.astype(jnp.bfloat16),
        cache[:, :, :LAT],
        preferred_element_type=jnp.float32,
    )
    return (top_score, row_total, values)


def swap_ctx(x):
    return lax.ppermute(x, "ctx", [(0, 1), (1, 0)])


def attend_local(queries, latent_cache, cache_lengths):
    share = queries.shape[1] // 2
    mine = lax.axis_index("ctx")
    top, total, values = softmax_parts(
        queries, latent_cache, cache_lengths, mine * latent_cache.shape[1]
    )
    packed = jnp.concatenate(
        [values, jnp.stack([top, total], axis=2), jnp.zeros(top.shape + (126,), jnp.float32)],
        axis=2,
    )
    kept = lax.dynamic_slice_in_dim(packed, mine * share, share, 1)
    other = swap_ctx(lax.dynamic_slice_in_dim(packed, (1 - mine) * share, share, 1))
    kept_top, other_top = kept[:, :, LAT : LAT + 1], other[:, :, LAT : LAT + 1]
    joined_top = jnp.maximum(kept_top, other_top)
    kept_factor = jnp.exp(kept_top - joined_top)
    other_factor = jnp.exp(other_top - joined_top)
    joined = kept * kept_factor + other * other_factor
    return (joined[:, :, :LAT] / joined[:, :, LAT + 1 : LAT + 2]).astype(jnp.bfloat16)


def plane_of(owners):
    return owners == 16


def send(x, target):
    count = lax.axis_size("ep")
    return lax.ppermute(x, "ep", [(i, target(i)) for i in range(count)])


def to_x(x):
    return send(x, lambda i: i ^ 1)


def to_y(x):
    return send(x, lambda i: i ^ 2)


def to_z(x, steps):
    return send(x, lambda i: (i + 4 * steps) % 16)


def cat(*pieces):
    return jnp.concatenate(pieces, axis=0)


def after(x, other):
    return lax.optimization_barrier((x, other))[0]


def gather_rows(rows):
    n = rows.shape[0]
    h = n // 2
    below, above = to_z(rows, 1), to_z(rows, 3)
    own_x, own_y = to_x(rows), to_y(rows)
    far = to_z(after(rows, below), 2)
    bx = to_x(cat(below, above, own_y[h:]))
    by = to_y(cat(below, above, own_x[:h]))
    cx = to_x(cat(far, by[h:n], by[n + h : 2 * n]))
    cy = to_y(cat(far, bx[:h], bx[n : n + h]))
    dx = to_x(cy[h:n])
    dy = to_y(cx[:h])
    return (
        cat(rows, own_x, own_y, below, above),
        cat(bx, by),
        cat(far, cx, cy),
        cat(dx, dy),
    )


PLACES = (
    ((0, 0, 2), (0, 2, 4), (0, 4, 6), (1, 9, 10), (1, 4, 5)),
    ((0, 6, 8), (1, 0, 2), (1, 5, 7), (2, 8, 9), (2, 4, 5)),
    ((2, 0, 2), (2, 2, 4), (2, 6, 8), (3, 1, 2), (3, 0, 1)),
    ((0, 8, 10), (1, 2, 4), (1, 7, 9), (2, 9, 10), (2, 5, 6)),
)
BUNDLES = (10, 10, 10, 2)


def scatter_sums(kept, came):
    n = kept[3].shape[0]
    h = n // 2

    def share(b, first, last):
        at = slice(first * h, last * h)
        return kept[b][at].astype(jnp.float32) + came[b][at].astype(jnp.float32)

    def wide(x):
        return x.astype(jnp.float32)

    def narrow(*pieces):
        return cat(*pieces).astype(jnp.bfloat16)

    dx = wide(to_x(narrow(share(3, 0, 1))))
    dy = wide(to_y(narrow(share(3, 1, 2))))
    cx = wide(to_x(narrow(share(2, 2, 3) + dy, share(2, 3, 6))))
    cy = wide(to_y(narrow(share(2, 6, 7), share(2, 7, 8) + dx, share(2, 8, 10))))
    far = wide(to_z(narrow(share(2, 0, 2) + cx[:n] + cy[:n]), 2))
    bx = wide(
        to_x(
            narrow(
                share(1, 0, 1) + cy[n : n + h],
                share(1, 1, 2),
                share(1, 2, 3) + cy[n + h :],
                share(1, 3, 5),
            )
        )
    )
    by = wide(
        to_y(
            narrow(
                share(1, 5, 6),
                share(1, 6, 7) + cx[n : n + h],
                share(1, 7, 8),
                share(1, 8, 9) + cx[n + h :],
                share(1, 9, 10),
            )
        )
    )
    below = wide(to_z(narrow(share(0, 6, 8) + bx[:n] + by[:n]), 3))
    above = wide(to_z(narrow(share(0, 8, 10) + bx[n : 2 * n] + by[n : 2 * n]), 1))
    own_x = wide(to_x(narrow(share(0, 2, 3) + by[2 * n :], share(0, 3, 4))))
    own_y = wide(to_y(narrow(share(0, 4, 5), share(0, 5, 6) + bx[2 * n :])))
    return narrow(share(0, 0, 2) + own_x + own_y + below + above + far)


def expert_kernel(plan, first_ref, *refs):
    bundled, group_count, expert_count, width, top = plan
    count = len(BUNDLES) if bundled else 1
    own, other = refs[:count], refs[count : 2 * count]
    gate_ref, up_ref, down_ref = refs[2 * count : 2 * count + 3]
    own_out = refs[2 * count + 3 : 3 * count + 3]
    other_out = refs[3 * count + 3 : 4 * count + 3]
    slots, select, scales = refs[4 * count + 3 :]
    step = pl.program_id(0)
    lanes = select.shape[2]
    half = lanes // 2
    piece = half // JOIN
    block = JOIN * CAP
    unit = piece // 2

    def rows_of(group, at):
        parts = []
        for side in (own, other):
            if bundled:
                parts += [side[b][f * unit : t * unit, at] for b, f, t in PLACES[group]]
            else:
                parts.append(side[0][:, at])
        return jnp.concatenate(parts, axis=0)

    def put_rows(group, at, rows):
        done = 0
        for side in (own_out, other_out):
            if bundled:
                for b, f, t in PLACES[group]:
                    side[b][f * unit : t * unit, at] = rows[done : done + (t - f) * unit]
                    done += (t - f) * unit
            else:
                side[0][:, at] = rows[done : done + half]
                done += half

    def slot_range(group):
        if bundled:
            return slice(group * block, (group + 1) * block)
        return pl.ds(pl.multiple_of(group * block, block), block)

    def sort_rows(group):
        first = first_ref[0]
        named = rows_of(group, slice(width, width + 128)).astype(jnp.float32).T
        ids = named[:top]
        gates = named[top : 2 * top] + named[2 * top : 3 * top] + named[3 * top : 4 * top]
        earlier = lax.broadcasted_iota(jnp.int32, (lanes, lanes), 0)
        later = lax.broadcasted_iota(jnp.int32, (lanes, lanes), 1)
        same = ((earlier // piece) % JOIN) == ((later // piece) % JOIN)
        before = jnp.where(same & (earlier < later), 1.0, 0.0).astype(jnp.bfloat16)
        hits, gated = [], []
        for e in range(expert_count):
            hit = ids == (first + e).astype(jnp.float32)
            hits.append(jnp.sum(jnp.where(hit, 1.0, 0.0), axis=0, keepdims=True))
            gated.append(jnp.sum(jnp.where(hit, gates, 0.0), axis=0, keepdims=True))
        padded = hits + [jnp.zeros_like(hits[0])] * (-expert_count % 8)
        places = jnp.dot(
            jnp.concatenate(padded, axis=0).astype(jnp.bfloat16),
            before,
            preferred_element_type=jnp.float32,
        )
        slot = lax.broadcasted_iota(jnp.int32, (block, lanes), 0)
        lane = lax.broadcasted_iota(jnp.int32, (block, lanes), 1)
        fits = (slot // CAP) == ((lane // piece) % JOIN)
        place = (slot % CAP).astype(jnp.float32)
        at = slot_range(group)
        for e in range(expert_count):
            wanted = jnp.where(hits[e] > 0.5, places[e : e + 1], -1.0)
            picked = jnp.where(fits & (wanted == place), 1.0, 0.0)
            scale = jnp.sum(picked * gated[e], axis=1, keepdims=True)
            scales[e, at, :] = jnp.broadcast_to(scale, (block, 128))
            select[group, e * block : (e + 1) * block, :] = picked.astype(jnp.bfloat16)
        chosen = select[group]
        for c in range(0, width, COLS):
            columns = slice(c, c + COLS)
            sorted_rows = jnp.dot(
                chosen, rows_of(group, columns), preferred_element_type=jnp.float32
            ).astype(jnp.bfloat16)
            for e in range(expert_count):
                slots[e, at, columns] = sorted_rows[e * block : (e + 1) * block]

    def sum_rows(group):
        chosen = select[group]
        at = slot_range(group)
        for c in range(0, width, COLS):
            columns = slice(c, c + COLS)
            outs = jnp.concatenate([slots[e, at, columns] for e in range(expert_count)], axis=0)
            rows = lax.dot_general(
                chosen, outs, (((0,), (0,)), ((), ())), preferred_element_type=jnp.float32
            )
            put_rows(group, columns, rows.astype(jnp.bfloat16))

    def each_group(from_step, work):
        if bundled:
            for group in range(group_count):
                pl.when(step == from_step + group)(functools.partial(work, group))
        else:
            inside = (step >= from_step) & (step < from_step + group_count)
            pl.when(inside)(functools.partial(work, step - from_step))

    each_group(0, sort_rows)

    @pl.when((step >= group_count) & (step < group_count + expert_count))
    def _():
        e = step - group_count
        rows = slots[e]
        gate = jnp.dot(rows, gate_ref[0], preferred_element_type=jnp.float32)
        up = jnp.dot(rows, up_ref[0], preferred_element_type=jnp.float32)
        hidden = (gate / (1.0 + jnp.exp(-gate))) * up * scales[e][:, :1]
        hidden = hidden.astype(jnp.bfloat16)
        for c in range(0, width, COLS):
            slots[e, :, c : c + COLS] = jnp.dot(
                hidden, down_ref[0, :, c : c + COLS], preferred_element_type=jnp.float32
            ).astype(jnp.bfloat16)

    each_group(group_count + expert_count, sum_rows)


def expert_sums(own, other, top, owners, first, gate_weight, up_weight, down_weight):
    expert_count, width, hidden = gate_weight.shape
    bundled = len(own) > 1
    group_count = owners // JOIN
    half = sum(x.shape[0] for x in own) // group_count
    slot_rows = group_count * JOIN * CAP

    def expert(i, first_ref):
        return (jnp.clip(i - group_count, 0, expert_count - 1), 0, 0)

    if bundled:
        once = pl.Buffered(1)
        in_rows = [
            pl.BlockSpec(x.shape, lambda i, f: (0, 0), pipeline_mode=once) for x in own + other
        ]
        out_rows = [
            pl.BlockSpec((x.shape[0], width), lambda i, f: (0, 0), pipeline_mode=once)
            for x in own + other
        ]
    else:
        in_rows = [
            pl.BlockSpec((half, x.shape[1]), lambda i, f: (jnp.minimum(i, group_count - 1), 0))
            for x in own + other
        ]
        out_rows = [
            pl.BlockSpec((half, width), lambda i, f: (jnp.maximum(i - group_count - expert_count, 0), 0))
            for x in own + other
        ]
    weight_bytes = 3 * expert_count * width * hidden * 2
    sums = pl.pallas_call(
        functools.partial(
            expert_kernel, (bundled, group_count, expert_count, width, top)
        ),
        out_shape=[jax.ShapeDtypeStruct((x.shape[0], width), jnp.bfloat16) for x in own + other],
        grid_spec=pltpu.PrefetchScalarGridSpec(
            num_scalar_prefetch=1,
            grid=(2 * group_count + expert_count,),
            in_specs=in_rows
            + [
                pl.BlockSpec((1, width, hidden), expert),
                pl.BlockSpec((1, width, hidden), expert),
                pl.BlockSpec((1, hidden, width), expert),
            ],
            out_specs=out_rows,
            scratch_shapes=[
                pltpu.VMEM((expert_count, slot_rows, width), jnp.bfloat16),
                pltpu.VMEM((group_count, expert_count * JOIN * CAP, 2 * half), jnp.bfloat16),
                pltpu.VMEM((expert_count, slot_rows, 128), jnp.float32),
            ],
        ),
        compiler_params=pltpu.CompilerParams(
            dimension_semantics=("arbitrary",), vmem_limit_bytes=50 * 1024 * 1024
        ),
        cost_estimate=pl.CostEstimate(
            flops=slot_rows * weight_bytes,
            bytes_accessed=weight_bytes,
            transcendentals=expert_count * slot_rows * hidden,
        ),
    )(first, *own, *other, gate_weight, up_weight, down_weight)
    return sums[: len(own)], sums[len(own) :]


def as_three(x):
    terms = []
    for _ in range(3):
        term = lax.reduce_precision(x, 8, 7)
        terms.append(term.astype(jnp.bfloat16))
        x = x - term
    return terms


def route_rows(moe_rows, routes, route_gates, gate_weight, up_weight, down_weight):
    owners = lax.axis_size("ep")
    row_count = moe_rows.shape[0]
    top = routes.shape[1]
    half = row_count // 2
    core, chip = lax.axis_index("ctx"), lax.axis_index("ep")
    first = (chip * gate_weight.shape[0]).astype(jnp.int32).reshape(1)

    asked = [routes.astype(jnp.bfloat16)] + as_three(route_gates)
    blank = jnp.zeros((row_count, 128 - 4 * top), jnp.bfloat16)
    sent = jnp.concatenate([moe_rows] + asked + [blank], axis=1)
    sent = lax.dynamic_slice_in_dim(sent, core * half, half, 0)
    if plane_of(owners):
        own = gather_rows(sent)
    else:
        own = (lax.all_gather(sent, "ep", tiled=True),)
    other = tuple(swap_ctx(x) for x in own)
    own_sums, other_sums = expert_sums(
        own, other, top, owners, first, gate_weight, up_weight, down_weight
    )
    came = [None] * len(own)
    for b in reversed(range(len(own))):
        came[b] = swap_ctx(other_sums[b])
    if plane_of(owners):
        own_final = scatter_sums(own_sums, came)
    else:
        own_final = lax.psum_scatter(own_sums[0] + came[0], "ep", scatter_dimension=0, tiled=True)
    other_final = swap_ctx(own_final)
    return jnp.where(core == 0, cat(own_final, other_final), cat(other_final, own_final))


def body(
    moe_rows,
    routes,
    route_gates,
    gate_weight,
    up_weight,
    down_weight,
    queries,
    latent_cache,
    cache_lengths,
):
    routed_output = route_rows(moe_rows, routes, route_gates, gate_weight, up_weight, down_weight)
    attention_output = attend_local(queries, latent_cache, cache_lengths)
    return (routed_output, attention_output)


def solution(mesh):
    in_specs = (
        P("ep", None),
        P("ep", None),
        P("ep", None),
        P("ep", None, "ctx"),
        P("ep", None, "ctx"),
        P("ep", "ctx", None),
        P("ep", None, None),
        P("ep", "ctx", None),
        P("ep"),
    )
    out_specs = (P("ep", None), P("ep", "ctx", None))
    return jax.shard_map(body, mesh=mesh, in_specs=in_specs, out_specs=out_specs, check_vma=False)
```

time: 223 us -> 160 us (0.72)
  blocking collectives: 38.4 us -> 0 us
  local copies, waits for them, and re-layouts: 25.8 us -> 14.3 us
  other arithmetic: 21.1 us -> 9.85 us
  waiting for transfers between devices: 69.6 us -> 59.4 us
  starting transfers between devices: 24.4 us -> 29.5 us
    all_gather x1 -> x0, blocking collectives: 38.4 us -> none  [route_rows(): named = lax.all_gather(named, 'ep').reshape(owners, -1)]
    unnamed x27, local copies, waits for them, and re-layouts: 14.3 us -> 7.38 us
    ppermute x22, waiting for transfers between devices: 64.2 us -> 57.4 us  [send(): return lax.ppermute(x, 'ep', [(i, target(i)) for i in range(count)])]
    slice x10 -> x2, local copies, waits for them, and re-layouts: 6.22 us -> 0.04 us  [the longest x1 0.02 us: gather_rows(): cx = to_x(cat(far, by[h:n], by[n + h:2 * n]))]
    unnamed x5 -> x4, other arithmetic: 5.57 us -> 0.14 us
    concatenate x7 -> x8, other arithmetic: 5.48 us -> 0.34 us  [cat(): return jnp.concatenate(pieces, axis=0)]
    ppermute x22, starting transfers between devices: 22.8 us -> 27.8 us  [send(): return lax.ppermute(x, 'ep', [(i, target(i)) for i in range(count)])]
    another operation x0 -> x6, other arithmetic: none -> 3.56 us
  transfers between devices with their start and end apart: 32 -> 32, of which waited for: 19 -> 16; matrix products, arithmetic and copies ran while one was open for 15% -> 14% of each run, Pallas kernels for 0% -> 0%
where the time goes in v2:
time: 160 us; the launch traced here: 159 us
  waiting for transfers between devices  59.4 us (37%)
  Pallas kernels  40.4 us (25%)
  starting transfers between devices  29.5 us (18%)
  local copies, waits for them, and re-layouts  14.3 us (9%)
  other arithmetic  9.85 us (6%)
  matrix products  4.16 us (3%)
  between operations  1.71 us (1%)
    ppermute x22, waiting for transfers between devices, send(): return lax.ppermute(x, 'ep', [(i, target(i)) for i in range(count)])  57.4 us
    pallas_call x1, Pallas kernels, expert_sums(): pl.pallas_call(functools.partial(expert_kernel, (bundled, group_count, ex...  40.4 us
    ppermute x22, starting transfers between devices, send(): return lax.ppermute(x, 'ep', [(i, target(i)) for i in range(count)])  27.8 us
    unnamed x27, local copies, waits for them, and re-layouts  7.38 us
    another operation x6, other arithmetic  3.56 us
  transfers between devices with their start and end apart: 32, of which 16 were waited for; matrix products, arithmetic and copies ran while one was open for 14% of the time, Pallas kernels for 0%

profile of v2, /device:TPU:0, one launch (start us, length us, event | category | flops | bytes accessed | tf_op | source)
XLA Modules:
  0.0 159.3 jit_solution(6398321861482080503)
XLA Ops:
  0.6 0.7 fusion.47
  1.4 0.8 copy.21
  2.3 0.7 convert_element_type.220
  3.2 1.1 concatenate.60
  4.3 0.7 constant_dynamic-update-slice_fusion.4
  5.0 3.0 %collective-permute-start.2 = (bf16[32,3712]{1,0:T(8,128)(2,1)S(1)}, bf16[32,3712]{1,0:T(8,128)(2,1)S(1)}, u32[]{:S(2)}, u32[]{:S(2)}) collective-permute-start(bf16[32,3712]{1,0:T(8,128)(2,1)S(1)} %get-tuple-element.11), channel_id=1, source_target_pairs={{0,4},{1,5},{2,6},{3,7},{4,8},{5,9},{6,10},{7,11},{8,12},{9,13},{1... | collective-permute-start | bytes 712712 | tf_op jit(solution)/shard_map/ppermute | solution.py:69
  8.1 1.5 collective-permute-start.1
  9.6 1.5 collective-permute-start
  11.1 2.2 %collective-permute-start.3 = (bf16[32,3712]{1,0:T(8,128)(2,1)S(1)}, bf16[32,3712]{1,0:T(8,128)(2,1)S(1)}, u32[]{:S(2)}, u32[]{:S(2)}) collective-permute-start(bf16[32,3712]{1,0:T(8,128)(2,1)S(1)} %get-tuple-element.11), channel_id=1, source_target_pairs={{0,12},{1,13},{2,14},{3,15},{4,0},{5,1},{6,2},{7,3},{8,4},{9,5},{1... | collective-permute-start | bytes 712712 | tf_op jit(solution)/shard_map/ppermute | solution.py:69
  14.0 2.3 %fusion.48 = (f32[64]{0:T(128)S(1)}, f32[64,2048]{1,0:T(8,128)S(1)}) fusion(bf16[1,2048,576]{1,2,0:T(8,128)(2,1)} %param.16, bf16[1,64,576]{2,1,0:T(8,128)(2,1)S(1)} %copy-done, pred[2048]{0:T(1024)(128)(4,1)S(1)} %add_compare_fusion), kind=kOutput, calls=%fused_computation.104 | convolution fusion | flops 151388096 | bytes 2959616 | tf_op jit(solution)/shard_map/rhk,rlk->rhl/dot_general | solution.py:21
  16.7 4.3 %collective-permute-done.3 = bf16[32,3712]{1,0:T(8,128)(2,1)S(1)} collective-permute-done((bf16[32,3712]{1,0:T(8,128)(2,1)S(1)}, bf16[32,3712]{1,0:T(8,128)(2,1)S(1)}, u32[]{:S(2)}, u32[]{:S(2)}) %collective-permute-start.3) | collective-permute-done | bytes 237600 | tf_op jit(solution)/shard_map/ppermute | solution.py:69
  21.0 1.6 collective-permute-start.4
  22.6 1.4 collective-permute-start.5
  24.0 0.8 collective-permute-start.6
  24.8 0.7 constant_dynamic-update-slice_fusion.3
  25.6 0.7 constant_dynamic-update-slice_fusion.2
  26.3 0.7 constant_dynamic-update-slice_fusion.1
  27.0 0.7 constant_dynamic-update-slice_fusion.refs_0_
  27.7 9.3 %collective-permute-done.6 = bf16[32,3712]{1,0:T(8,128)(2,1)S(1)} collective-permute-done((bf16[32,3712]{1,0:T(8,128)(2,1)S(1)}, bf16[32,3712]{1,0:T(8,128)(2,1)S(1)}, u32[]{:S(2)}, u32[]{:S(2)}) %collective-permute-start.6) | collective-permute-done | bytes 237600 | tf_op jit(solution)/shard_map/ppermute | solution.py:69
  37.0 0.7 constant_dynamic-update-slice_fusion.9
  37.9 1.2 collective-permute-start.8
  39.1 0.7 collective-permute-start.7
  40.0 10.5 %collective-permute-done.8 = bf16[64,3712]{1,0:T(8,128)(2,1)S(1)} collective-permute-done((bf16[64,3712]{1,0:T(8,128)(2,1)S(1)}, bf16[64,3712]{1,0:T(8,128)(2,1)S(1)}, u32[]{:S(2)}, u32[]{:S(2)}) %collective-permute-start.8) | collective-permute-done | bytes 475168 | tf_op jit(solution)/shard_map/ppermute | solution.py:69
  50.6 0.7 slice.298
  51.2 0.9 collective-permute-start.9
  52.1 2.0 %constant_dynamic-update-slice_fusion.8 = bf16[160,3712]{1,0:T(8,128)(2,1)} fusion(bf16[160,3712]{1,0:T(8,128)(2,1)} %constant_dynamic-update-slice_fusion.9, bf16[64,3712]{1,0:T(8,128)(2,1)} %collective-permute-done.7), kind=kLoop, calls=%fused_computation.83 | loop fusion | bytes 950272
  54.1 0.8 constant_dynamic-update-slice_fusion.7.refs_2_
  54.9 0.8 fusion.19
  55.7 1.3 copy.26
  57.0 0.7 copy.25
  57.7 0.9 slice.299
  58.7 0.5 collective-permute-start.10
  59.1 0.9 constant_dynamic-update-slice_fusion.11
  60.1 4.3 %collective-permute-done.10 = bf16[16,3712]{1,0:T(8,128)(2,1)S(1)} collective-permute-done((bf16[16,3712]{1,0:T(8,128)(2,1)S(1)}, bf16[16,3712]{1,0:T(8,128)(2,1)S(1)}, u32[]{:S(2)}, u32[]{:S(2)}) %collective-permute-start.10) | collective-permute-done | bytes 118816 | tf_op jit(solution)/shard_map/ppermute | solution.py:69
  64.5 1.8 %fusion.11 = f32[1,64,512]{2,1,0:T(8,128)S(1)} fusion(bf16[1,2048,576]{1,2,0:T(8,128)(2,1)S(1)} %copy-done.3, f32[64,2048]{1,0:T(8,128)} %copy-done.4, f32[64]{0:T(128)} %copy-done.8, pred[2048]{0:T(1024)(128)(4,1)S(1)} %add_compare_fusion), kind=kOutput, calls=%fused_computation.7 | convolution fusion | flops 134610944 | bytes 2754816 | tf_op jit(solution)/shard_map/rhl,rlv->rhv/dot_general | solution.py:30
  66.3 40.4 %shard_map.104 = (bf16[160,3584]{1,0:T(8,128)(2,1)S(1)}, bf16[160,3584]{1,0:T(8,128)(2,1)S(1)}, bf16[160,3584]{1,0:T(8,128)(2,1)}, bf16[32,3584]{1,0:T(8,128)(2,...) custom-call(s32[1]{0:T(128)} %bitcast.first_ref, ...), custom_call_target="tpu_custom_call" | custom-call | flops 11274289152 | bytes 88080384 | tf_op jit(solution)/shard_map/pallas_call | solution.py:314
  106.8 0.5 collective-permute-start.18
  107.4 0.5 collective-permute-start.31
  108.5 0.5 collective-permute-start.19
  109.0 1.4 collective-permute-done.17
  110.4 1.2 collective-permute-start.23
  111.6 1.1 add_convert_fusion.3
  112.7 1.2 collective-permute-done.19
  113.9 1.9 %collective-permute-done.23 = bf16[16,3584]{1,0:T(8,128)(2,1)S(1)} collective-permute-done((bf16[16,3584]{1,0:T(8,128)(2,1)S(1)}, bf16[16,3584]{1,0:T(8,128)(2,1)S(1)}, u32[]{:S(2)}, u32[]{:S(2)}) %collective-permute-start.23) | collective-permute-done | bytes 114720 | tf_op jit(solution)/shard_map/ppermute | solution.py:69
  115.8 1.1 add_convert_fusion.12
  117.0 0.5 collective-permute-start.24
  117.5 1.1 add_convert_fusion
  118.6 1.6 %collective-permute-start.20 = (bf16[64,3584]{1,0:T(8,128)(2,1)S(1)}, bf16[64,3584]{1,0:T(8,128)(2,1)S(1)}, u32[]{:S(2)}, u32[]{:S(2)}) collective-permute-start(bf16[64,3584]{1,0:T(8,128)(2,1)S(1)} %pad_maximum_fusion.6), channel_id=1, source_target_pairs={{0,1},{1,0},{2,3},{3,2},{4,5},{5,4},{6,7},{7,6},{8,9},{9,8},{10,11... | collective-permute-start | bytes 1376264 | tf_op jit(solution)/shard_map/ppermute | solution.py:69
  120.3 8.7 %collective-permute-done.24 = bf16[64,3584]{1,0:T(8,128)(2,1)S(1)} collective-permute-done((bf16[64,3584]{1,0:T(8,128)(2,1)S(1)}, bf16[64,3584]{1,0:T(8,128)(2,1)S(1)}, u32[]{:S(2)}, u32[]{:S(2)}) %collective-permute-start.24) | collective-permute-done | bytes 458784 | tf_op jit(solution)/shard_map/ppermute | solution.py:69
  129.2 1.2 collective-permute-start.25
  130.7 2.5 %collective-permute-start.21 = (bf16[80,3584]{1,0:T(8,128)(2,1)S(1)}, bf16[80,3584]{1,0:T(8,128)(2,1)S(1)}, u32[]{:S(2)}, u32[]{:S(2)}) collective-permute-start(bf16[80,3584]{1,0:T(8,128)(2,1)S(1)} %fusion.33), channel_id=1, source_target_pairs={{0,2},{1,3},{2,0},{3,1},{4,6},{5,7},{6,4},{7,5},{8,10},{9,11},{10,... | collective-permute-start | bytes 1720328 | tf_op jit(solution)/shard_map/ppermute | solution.py:69
  133.1 1.0 fusion.16
  134.2 8.5 %collective-permute-done.25 = bf16[80,3584]{1,0:T(8,128)(2,1)S(1)} collective-permute-done((bf16[80,3584]{1,0:T(8,128)(2,1)S(1)}, bf16[80,3584]{1,0:T(8,128)(2,1)S(1)}, u32[]{:S(2)}, u32[]{:S(2)}) %collective-permute-start.25) | collective-permute-done | bytes 573472 | tf_op jit(solution)/shard_map/ppermute | solution.py:69
  142.8 1.1 collective-permute-done.21
  144.2 1.5 collective-permute-start.22
  145.7 1.3 collective-permute-start.26
  147.2 0.5 collective-permute-start.27
  147.6 1.6 %collective-permute-start.28 = (bf16[32,3584]{1,0:T(8,128)(2,1)S(1)}, bf16[32,3584]{1,0:T(8,128)(2,1)S(1)}, u32[]{:S(2)}, u32[]{:S(2)}) collective-permute-start(bf16[32,3584]{1,0:T(8,128)(2,1)S(1)} %get-tuple-element.25), channel_id=1, source_target_pairs={{0,4},{1,5},{2,6},{3,7},{4,8},{5,9},{6,10},{7,11},{8,12},{9,13},{1... | collective-permute-start | bytes 688136 | tf_op jit(solution)/shard_map/ppermute | solution.py:69
  149.5 0.8 collective-permute-done.22
  150.3 1.5 collective-permute-done.26
  151.8 4.9 %collective-permute-done.27 = bf16[32,3584]{1,0:T(8,128)(2,1)S(1)} collective-permute-done((bf16[32,3584]{1,0:T(8,128)(2,1)S(1)}, bf16[32,3584]{1,0:T(8,128)(2,1)S(1)}, u32[]{:S(2)}, u32[]{:S(2)}) %collective-permute-start.27) | collective-permute-done | bytes 229408 | tf_op jit(solution)/shard_map/ppermute | solution.py:69
  157.2 0.7 fusion.37
  157.9 0.6 collective-permute-done.30
  158.5 0.8 maximum_select_fusion
  (87 shorter events, 3.8 us)
Async XLA Ops:
  0.6 13.4 %copy-start = (bf16[1,64,576]{2,1,0:T(8,128)(2,1)S(1)}, bf16[1,64,576]{2,1,0:T(8,128)(2,1)}, u32[]{:S(2)}) copy-start(bf16[1,64,576]{2,1,0:T(8,128)(2,1)} %param.15) | copy-start | bytes 221188
  5.0 11.7 %collective-permute-start.2 = (bf16[32,3712]{1,0:T(8,128)(2,1)S(1)}, bf16[32,3712]{1,0:T(8,128)(2,1)S(1)}, u32[]{:S(2)}, u32[]{:S(2)}) collective-permute-start(bf16[32,3712]{1,0:T(8,128)(2,1)S(1)} %get-tuple-element.11), channel_id=1, source_target_pairs={{0,4},{1,5},{2,6},{3,7},{4,8},{5,9},{6,10},{7,11},{8,12},{9,13},{1... | collective-permute-start | bytes 712712 | tf_op jit(solution)/shard_map/ppermute | solution.py:69
  8.1 8.3 %collective-permute-start.1 = (bf16[32,3712]{1,0:T(8,128)(2,1)S(1)}, bf16[32,3712]{1,0:T(8,128)(2,1)S(1)}, u32[]{:S(2)}, u32[]{:S(2)}) collective-permute-start(bf16[32,3712]{1,0:T(8,128)(2,1)S(1)} %get-tuple-element.11), channel_id=1, source_target_pairs={{0,2},{1,3},{2,0},{3,1},{4,6},{5,7},{6,4},{7,5},{8,10},{9,11},{10,... | collective-permute-start | bytes 712712 | tf_op jit(solution)/shard_map/ppermute | solution.py:69
  9.6 7.0 %collective-permute-start = (bf16[32,3712]{1,0:T(8,128)(2,1)S(1)}, bf16[32,3712]{1,0:T(8,128)(2,1)S(1)}, u32[]{:S(2)}, u32[]{:S(2)}) collective-permute-start(bf16[32,3712]{1,0:T(8,128)(2,1)S(1)} %get-tuple-element.11), channel_id=1, source_target_pairs={{0,1},{1,0},{2,3},{3,2},{4,5},{5,4},{6,7},{7,6},{8,9},{9,8},{10,11... | collective-permute-start | bytes 712712 | tf_op jit(solution)/shard_map/ppermute | solution.py:69
  11.1 9.9 %collective-permute-start.3 = (bf16[32,3712]{1,0:T(8,128)(2,1)S(1)}, bf16[32,3712]{1,0:T(8,128)(2,1)S(1)}, u32[]{:S(2)}, u32[]{:S(2)}) collective-permute-start(bf16[32,3712]{1,0:T(8,128)(2,1)S(1)} %get-tuple-element.11), channel_id=1, source_target_pairs={{0,12},{1,13},{2,14},{3,15},{4,0},{5,1},{6,2},{7,3},{8,4},{9,5},{1... | collective-permute-start | bytes 712712 | tf_op jit(solution)/shard_map/ppermute | solution.py:69
  16.3 38.6 %copy-start.4 = (f32[64,2048]{1,0:T(8,128)}, f32[64,2048]{1,0:T(8,128)S(1)}, u32[]{:S(2)}) copy-start(f32[64,2048]{1,0:T(8,128)S(1)} %get-tuple-element.51) | copy-start | bytes 1572868
  16.3 40.6 %copy-start.8 = (f32[64]{0:T(128)}, f32[64]{0:T(128)S(1)}, u32[]{:S(2)}) copy-start(f32[64]{0:T(128)S(1)} %get-tuple-element.50) | copy-start | bytes 772
  21.0 16.7 %collective-permute-start.4 = (bf16[80,3712]{1,0:T(8,128)(2,1)S(1)}, bf16[80,3712]{1,0:T(8,128)(2,1)S(1)}, u32[]{:S(2)}, u32[]{:S(2)}) collective-permute-start(bf16[80,3712]{1,0:T(8,128)(2,1)S(1)} %get-tuple-element.41), channel_id=1, source_target_pairs={{0,1},{1,0},{2,3},{3,2},{4,5},{5,4},{6,7},{7,6},{8,9},{9,8},{10,11... | collective-permute-start | bytes 1781768 | tf_op jit(solution)/shard_map/ppermute | solution.py:69
  22.6 15.2 %collective-permute-start.5 = (bf16[80,3712]{1,0:T(8,128)(2,1)S(1)}, bf16[80,3712]{1,0:T(8,128)(2,1)S(1)}, u32[]{:S(2)}, u32[]{:S(2)}) collective-permute-start(bf16[80,3712]{1,0:T(8,128)(2,1)S(1)} %get-tuple-element.40), channel_id=1, source_target_pairs={{0,2},{1,3},{2,0},{3,1},{4,6},{5,7},{6,4},{7,5},{8,10},{9,11},{10,... | collective-permute-start | bytes 1781768 | tf_op jit(solution)/shard_map/ppermute | solution.py:69
  24.0 13.0 %collective-permute-start.6 = (bf16[32,3712]{1,0:T(8,128)(2,1)S(1)}, bf16[32,3712]{1,0:T(8,128)(2,1)S(1)}, u32[]{:S(2)}, u32[]{:S(2)}) collective-permute-start(bf16[32,3712]{1,0:T(8,128)(2,1)S(1)} %get-tuple-element.11), channel_id=1, source_target_pairs={{0,8},{1,9},{2,10},{3,11},{4,12},{5,13},{6,14},{7,15},{8,0},{9,1},... | collective-permute-start | bytes 712712 | tf_op jit(solution)/shard_map/ppermute | solution.py:69
  27.7 38.6 %collective-permute-start.11 = (bf16[160,3712]{1,0:T(8,128)(2,1)}, bf16[160,3712]{1,0:T(8,128)(2,1)}, u32[]{:S(2)}, u32[]{:S(2)}) collective-permute-start(bf16[160,3712]{1,0:T(8,128)(2,1)} %constant_dynamic-update-slice_fusion.refs_0_), channel_id=1, source_target_pairs={{0,16},{16,0},{1,17},{17,1},{2,18},{18,2},{3,19},{19,3},{4,20},{20... | collective-permute-start | bytes 3563528 | tf_op jit(solution)/shard_map/ppermute | solution.py:40
  37.9 12.6 %collective-permute-start.8 = (bf16[64,3712]{1,0:T(8,128)(2,1)S(1)}, bf16[64,3712]{1,0:T(8,128)(2,1)S(1)}, u32[]{:S(2)}, u32[]{:S(2)}) collective-permute-start(bf16[64,3712]{1,0:T(8,128)(2,1)S(1)} %get-tuple-element.44), channel_id=1, source_target_pairs={{0,2},{1,3},{2,0},{3,1},{4,6},{5,7},{6,4},{7,5},{8,10},{9,11},{10,... | collective-permute-start | bytes 1425416 | tf_op jit(solution)/shard_map/ppermute | solution.py:69
  39.1 12.9 %collective-permute-start.7 = (bf16[64,3712]{1,0:T(8,128)(2,1)S(1)}, bf16[64,3712]{1,0:T(8,128)(2,1)}, u32[]{:S(2)}, u32[]{:S(2)}) collective-permute-start(bf16[64,3712]{1,0:T(8,128)(2,1)S(1)} %get-tuple-element.45), channel_id=1, source_target_pairs={{0,1},{1,0},{2,3},{3,2},{4,5},{5,4},{6,7},{7,6},{8,9},{9,8},{10,11... | collective-permute-start | bytes 1425416 | tf_op jit(solution)/shard_map/ppermute | solution.py:69
  39.9 15.7 %copy-start.2 = (bf16[160,3712]{1,0:T(8,128)(2,1)}, bf16[160,3712]{1,0:T(8,128)(2,1)S(1)}, u32[]{:S(2)}) copy-start(bf16[160,3712]{1,0:T(8,128)(2,1)S(1)} %constant_dynamic-update-slice_fusion.5.refs_1_) | copy-start | bytes 3563524
  40.0 26.4 %collective-permute-start.12 = (bf16[160,3712]{1,0:T(8,128)(2,1)S(1)}, bf16[160,3712]{1,0:T(8,128)(2,1)}, u32[]{:S(2)}, u32[]{:S(2)}) collective-permute-start(bf16[160,3712]{1,0:T(8,128)(2,1)S(1)} %constant_dynamic-update-slice_fusion.5.refs_1_), channel_id=1, source_target_pairs={{0,16},{16,0},{1,17},{17,1},{2,18},{18,2},{3,19},{19,3},{4,20},{20... | collective-permute-start | bytes 3563528 | tf_op jit(solution)/shard_map/ppermute | solution.py:40
  51.2 7.9 %collective-permute-start.9 = (bf16[16,3712]{1,0:T(8,128)(2,1)}, bf16[16,3712]{1,0:T(8,128)(2,1)}, u32[]{:S(2)}, u32[]{:S(2)}) collective-permute-start(bf16[16,3712]{1,0:T(8,128)(2,1)} %slice.298), channel_id=1, source_target_pairs={{0,1},{1,0},{2,3},{3,2},{4,5},{5,4},{6,7},{7,6},{8,9},{9,8},{10,11... | collective-permute-start | bytes 356360 | tf_op jit(solution)/shard_map/ppermute | solution.py:69
  52.1 12.4 %copy-start.3 = (bf16[1,2048,576]{1,2,0:T(8,128)(2,1)S(1)}, bf16[1,2048,576]{1,2,0:T(8,128)(2,1)}, u32[]{:S(2)}) copy-start(bf16[1,2048,576]{1,2,0:T(8,128)(2,1)} %param.16) | copy-start | bytes 7077892
  54.9 11.4 %collective-permute-start.13 = (bf16[160,3712]{1,0:T(8,128)(2,1)}, bf16[160,3712]{1,0:T(8,128)(2,1)}, u32[]{:S(2)}, u32[]{:S(2)}) collective-permute-start(bf16[160,3712]{1,0:T(8,128)(2,1)} %constant_dynamic-update-slice_fusion.7.refs_2_), channel_id=1, source_target_pairs={{0,16},{16,0},{1,17},{17,1},{2,18},{18,2},{3,19},{19,3},{4,20},{20... | collective-permute-start | bytes 3563528 | tf_op jit(solution)/shard_map/ppermute | solution.py:40
  58.7 5.7 %collective-permute-start.10 = (bf16[16,3712]{1,0:T(8,128)(2,1)S(1)}, bf16[16,3712]{1,0:T(8,128)(2,1)S(1)}, u32[]{:S(2)}, u32[]{:S(2)}) collective-permute-start(bf16[16,3712]{1,0:T(8,128)(2,1)S(1)} %slice.299), channel_id=1, source_target_pairs={{0,2},{1,3},{2,0},{3,1},{4,6},{5,7},{6,4},{7,5},{8,10},{9,11},{10,... | collective-permute-start | bytes 356360 | tf_op jit(solution)/shard_map/ppermute | solution.py:69
  64.4 1.9 %collective-permute-start.14 = (bf16[32,3712]{1,0:T(8,128)(2,1)S(1)}, bf16[32,3712]{1,0:T(8,128)(2,1)S(1)}, u32[]{:S(2)}, u32[]{:S(2)}) collective-permute-start(bf16[32,3712]{1,0:T(8,128)(2,1)S(1)} %constant_dynamic-update-slice_fusion.10.refs_3_), channel_id=1, source_target_pairs={{0,16},{16,0},{1,17},{17,1},{2,18},{18,2},{3,19},{19,3},{4,20},{20... | collective-permute-start | bytes 712712 | tf_op jit(solution)/shard_map/ppermute | solution.py:40
  66.3 41.0 %copy-start.6 = (f32[1,64,1]{2,1,0:T(8,128)S(1)}, f32[1,64,1]{2,1,0:T(8,128)}, u32[]{:S(2)}) copy-start(f32[1,64,1]{2,1,0:T(8,128)} %copy.26) | copy-start | bytes 772
  66.3 41.0 %copy-start.7 = (f32[1,64,1]{2,1,0:T(8,128)S(1)}, f32[1,64,1]{2,1,0:T(8,128)}, u32[]{:S(2)}) copy-start(f32[1,64,1]{2,1,0:T(8,128)} %copy.25) | copy-start | bytes 772
  106.8 1.7 %collective-permute-start.18 = (bf16[32,3584]{1,0:T(8,128)(2,1)S(1)}, bf16[32,3584]{1,0:T(8,128)(2,1)S(1)}, u32[]{:S(2)}, u32[]{:S(2)}) collective-permute-start(bf16[32,3584]{1,0:T(8,128)(2,1)S(1)} %get-tuple-element.19), channel_id=1, source_target_pairs={{0,16},{16,0},{1,17},{17,1},{2,18},{18,2},{3,19},{19,3},{4,20},{20... | collective-permute-start | bytes 688136 | tf_op jit(solution)/shard_map/ppermute | solution.py:40
  107.3 3.1 %collective-permute-start.17 = (bf16[160,3584]{1,0:T(8,128)(2,1)}, bf16[160,3584]{1,0:T(8,128)(2,1)}, u32[]{:S(2)}, u32[]{:S(2)}) collective-permute-start(bf16[160,3584]{1,0:T(8,128)(2,1)} %get-tuple-element.17), channel_id=1, source_target_pairs={{0,16},{16,0},{1,17},{17,1},{2,18},{18,2},{3,19},{19,3},{4,20},{20... | collective-permute-start | bytes 3440648 | tf_op jit(solution)/shard_map/ppermute | solution.py:40
  107.4 40.2 %collective-permute-start.31 = (f32[1,32,640]{2,1,0:T(8,128)S(1)}, f32[1,32,640]{2,1,0:T(8,128)S(1)}, u32[]{:S(2)}, u32[]{:S(2)}) collective-permute-start(f32[1,32,640]{2,1,0:T(8,128)S(1)} %constant_dynamic-slice_fusion), channel_id=1, source_target_pairs={{0,16},{16,0},{1,17},{17,1},{2,18},{18,2},{3,19},{19,3},{4,20},{20... | collective-permute-start | bytes 245768 | tf_op jit(solution)/shard_map/ppermute | solution.py:40
  107.9 7.9 %copy-start.5 = (bf16[160,3584]{1,0:T(8,128)(2,1)S(1)}, bf16[160,3584]{1,0:T(8,128)(2,1)}, u32[]{:S(2)}) copy-start(bf16[160,3584]{1,0:T(8,128)(2,1)} %get-tuple-element.16) | copy-start | bytes 3440644
  108.0 12.3 %collective-permute-start.16 = (bf16[160,3584]{1,0:T(8,128)(2,1)}, bf16[160,3584]{1,0:T(8,128)(2,1)S(1)}, u32[]{:S(2)}, u32[]{:S(2)}) collective-permute-start(bf16[160,3584]{1,0:T(8,128)(2,1)} %get-tuple-element.15), channel_id=1, source_target_pairs={{0,16},{16,0},{1,17},{17,1},{2,18},{18,2},{3,19},{19,3},{4,20},{20... | collective-permute-start | bytes 3440648 | tf_op jit(solution)/shard_map/ppermute | solution.py:40
  108.0 36.0 %collective-permute-start.15 = (bf16[160,3584]{1,0:T(8,128)(2,1)}, bf16[160,3584]{1,0:T(8,128)(2,1)S(1)}, u32[]{:S(2)}, u32[]{:S(2)}) collective-permute-start(bf16[160,3584]{1,0:T(8,128)(2,1)} %get-tuple-element.13), channel_id=1, source_target_pairs={{0,16},{16,0},{1,17},{17,1},{2,18},{18,2},{3,19},{19,3},{4,20},{20... | collective-permute-start | bytes 3440648 | tf_op jit(solution)/shard_map/ppermute | solution.py:40
  108.5 5.4 %collective-permute-start.19 = (bf16[16,3584]{1,0:T(8,128)(2,1)S(1)}, bf16[16,3584]{1,0:T(8,128)(2,1)S(1)}, u32[]{:S(2)}, u32[]{:S(2)}) collective-permute-start(bf16[16,3584]{1,0:T(8,128)(2,1)S(1)} %get-tuple-element.42), channel_id=1, source_target_pairs={{0,2},{1,3},{2,0},{3,1},{4,6},{5,7},{6,4},{7,5},{8,10},{9,11},{10,... | collective-permute-start | bytes 344072 | tf_op jit(solution)/shard_map/ppermute | solution.py:69
  110.4 5.4 %collective-permute-start.23 = (bf16[16,3584]{1,0:T(8,128)(2,1)S(1)}, bf16[16,3584]{1,0:T(8,128)(2,1)S(1)}, u32[]{:S(2)}, u32[]{:S(2)}) collective-permute-start(bf16[16,3584]{1,0:T(8,128)(2,1)S(1)} %get-tuple-element.43), channel_id=1, source_target_pairs={{0,1},{1,0},{2,3},{3,2},{4,5},{5,4},{6,7},{7,6},{8,9},{9,8},{10,11... | collective-permute-start | bytes 344072 | tf_op jit(solution)/shard_map/ppermute | solution.py:69
  117.0 12.0 %collective-permute-start.24 = (bf16[64,3584]{1,0:T(8,128)(2,1)S(1)}, bf16[64,3584]{1,0:T(8,128)(2,1)S(1)}, u32[]{:S(2)}, u32[]{:S(2)}) collective-permute-start(bf16[64,3584]{1,0:T(8,128)(2,1)S(1)} %pad_maximum_fusion.7), channel_id=1, source_target_pairs={{0,2},{1,3},{2,0},{3,1},{4,6},{5,7},{6,4},{7,5},{8,10},{9,11},{10,... | collective-permute-start | bytes 1376264 | tf_op jit(solution)/shard_map/ppermute | solution.py:69
  118.6 11.9 %collective-permute-start.20 = (bf16[64,3584]{1,0:T(8,128)(2,1)S(1)}, bf16[64,3584]{1,0:T(8,128)(2,1)S(1)}, u32[]{:S(2)}, u32[]{:S(2)}) collective-permute-start(bf16[64,3584]{1,0:T(8,128)(2,1)S(1)} %pad_maximum_fusion.6), channel_id=1, source_target_pairs={{0,1},{1,0},{2,3},{3,2},{4,5},{5,4},{6,7},{7,6},{8,9},{9,8},{10,11... | collective-permute-start | bytes 1376264 | tf_op jit(solution)/shard_map/ppermute | solution.py:69
  129.2 13.6 %collective-permute-start.25 = (bf16[80,3584]{1,0:T(8,128)(2,1)S(1)}, bf16[80,3584]{1,0:T(8,128)(2,1)S(1)}, u32[]{:S(2)}, u32[]{:S(2)}) collective-permute-start(bf16[80,3584]{1,0:T(8,128)(2,1)S(1)} %pad_maximum_fusion.3), channel_id=1, source_target_pairs={{0,1},{1,0},{2,3},{3,2},{4,5},{5,4},{6,7},{7,6},{8,9},{9,8},{10,11... | collective-permute-start | bytes 1720328 | tf_op jit(solution)/shard_map/ppermute | solution.py:69
  130.7 13.3 %collective-permute-start.21 = (bf16[80,3584]{1,0:T(8,128)(2,1)S(1)}, bf16[80,3584]{1,0:T(8,128)(2,1)S(1)}, u32[]{:S(2)}, u32[]{:S(2)}) collective-permute-start(bf16[80,3584]{1,0:T(8,128)(2,1)S(1)} %fusion.33), channel_id=1, source_target_pairs={{0,2},{1,3},{2,0},{3,1},{4,6},{5,7},{6,4},{7,5},{8,10},{9,11},{10,... | collective-permute-start | bytes 1720328 | tf_op jit(solution)/shard_map/ppermute | solution.py:69
  134.2 15.3 %collective-permute-start.29 = (bf16[32,3584]{1,0:T(8,128)(2,1)S(1)}, bf16[32,3584]{1,0:T(8,128)(2,1)S(1)}, u32[]{:S(2)}, u32[]{:S(2)}) collective-permute-start(bf16[32,3584]{1,0:T(8,128)(2,1)S(1)} %fusion.16), channel_id=1, source_target_pairs={{0,8},{1,9},{2,10},{3,11},{4,12},{5,13},{6,14},{7,15},{8,0},{9,1},... | collective-permute-start | bytes 688136 | tf_op jit(solution)/shard_map/ppermute | solution.py:69
  144.2 6.1 %collective-permute-start.22 = (bf16[32,3584]{1,0:T(8,128)(2,1)S(1)}, bf16[32,3584]{1,0:T(8,128)(2,1)S(1)}, u32[]{:S(2)}, u32[]{:S(2)}) collective-permute-start(bf16[32,3584]{1,0:T(8,128)(2,1)S(1)} %pad_maximum_fusion.8), channel_id=1, source_target_pairs={{0,1},{1,0},{2,3},{3,2},{4,5},{5,4},{6,7},{7,6},{8,9},{9,8},{10,11... | collective-permute-start | bytes 688136 | tf_op jit(solution)/shard_map/ppermute | solution.py:69
  145.7 6.1 %collective-permute-start.26 = (bf16[32,3584]{1,0:T(8,128)(2,1)S(1)}, bf16[32,3584]{1,0:T(8,128)(2,1)S(1)}, u32[]{:S(2)}, u32[]{:S(2)}) collective-permute-start(bf16[32,3584]{1,0:T(8,128)(2,1)S(1)} %pad_maximum_fusion.9), channel_id=1, source_target_pairs={{0,2},{1,3},{2,0},{3,1},{4,6},{5,7},{6,4},{7,5},{8,10},{9,11},{10,... | collective-permute-start | bytes 688136 | tf_op jit(solution)/shard_map/ppermute | solution.py:69
  147.2 9.6 %collective-permute-start.27 = (bf16[32,3584]{1,0:T(8,128)(2,1)S(1)}, bf16[32,3584]{1,0:T(8,128)(2,1)S(1)}, u32[]{:S(2)}, u32[]{:S(2)}) collective-permute-start(bf16[32,3584]{1,0:T(8,128)(2,1)S(1)} %get-tuple-element.24), channel_id=1, source_target_pairs={{0,12},{1,13},{2,14},{3,15},{4,0},{5,1},{6,2},{7,3},{8,4},{9,5},{1... | collective-permute-start | bytes 688136 | tf_op jit(solution)/shard_map/ppermute | solution.py:69
  147.6 9.1 %collective-permute-start.28 = (bf16[32,3584]{1,0:T(8,128)(2,1)S(1)}, bf16[32,3584]{1,0:T(8,128)(2,1)S(1)}, u32[]{:S(2)}, u32[]{:S(2)}) collective-permute-start(bf16[32,3584]{1,0:T(8,128)(2,1)S(1)} %get-tuple-element.25), channel_id=1, source_target_pairs={{0,4},{1,5},{2,6},{3,7},{4,8},{5,9},{6,10},{7,11},{8,12},{9,13},{1... | collective-permute-start | bytes 688136 | tf_op jit(solution)/shard_map/ppermute | solution.py:69
  149.4 10.0 %copy-start.1 = (bf16[1,64,576]{2,1,0:T(8,128)(2,1)S(1)}, bf16[1,64,576]{2,1,0:T(8,128)(2,1)}, u32[]{:S(2)}) copy-start(bf16[1,64,576]{2,1,0:T(8,128)(2,1)} %param.15) | copy-start | bytes 221188
  156.9 1.6 collective-permute-start.30

commit v3 on v2

v3 whole, which is shorter than its diff:
```python
import functools

import jax
import jax.numpy as jnp
from jax import lax
from jax.experimental import pallas as pl
from jax.experimental.pallas import tpu as pltpu
from jax.sharding import PartitionSpec as P

LAT = 512
CAP = 8
JOIN = 4
COLS = 512
VMEM_LIMIT = 51 * 1024 * 1024

softmax_scale = 192.0 ** (-0.5)


def attend_kernel(span_ref, queries_ref, cache_ref, out_ref):
    heads, span = queries_ref.shape[0], cache_ref.shape[1]
    scores = (
        jnp.dot(queries_ref[...], cache_ref[...], preferred_element_type=jnp.float32)
        * softmax_scale
    )
    usable = lax.broadcasted_iota(jnp.int32, (heads, span), 1) < span_ref[0]
    masked = jnp.where(usable, scores, -1e30)
    top = jnp.max(masked, axis=1, keepdims=True)
    weights = jnp.where(usable, jnp.exp(masked - top), 0.0)
    total = jnp.sum(weights, axis=1, keepdims=True)
    out_ref[:, :LAT] = lax.dot_general(
        weights.astype(jnp.bfloat16),
        cache_ref[:LAT],
        (((1,), (1,)), ((), ())),
        preferred_element_type=jnp.float32,
    )
    lane = lax.broadcasted_iota(jnp.int32, (heads, 128), 1)
    out_ref[:, LAT:] = jnp.where(lane == 0, top, total)


def attend_part(queries, cache, span):
    heads, depth = queries.shape
    return pl.pallas_call(
        attend_kernel,
        out_shape=jax.ShapeDtypeStruct((heads, LAT + 128), jnp.float32),
        in_specs=[
            pl.BlockSpec(memory_space=pltpu.SMEM),
            pl.BlockSpec(memory_space=pltpu.VMEM),
            pl.BlockSpec(memory_space=pltpu.VMEM),
        ],
        out_specs=pl.BlockSpec(memory_space=pltpu.VMEM),
        compiler_params=pltpu.CompilerParams(vmem_limit_bytes=16 * 1024 * 1024),
        cost_estimate=pl.CostEstimate(
            flops=2 * heads * cache.shape[0] * (depth + LAT),
            bytes_accessed=cache.size * 2,
            transcendentals=heads * cache.shape[0],
        ),
    )(span, queries, cache.T)


def swap_ctx(x):
    return lax.ppermute(x, "ctx", [(0, 1), (1, 0)])


def attend_local(queries, latent_cache, cache_lengths):
    mine = lax.axis_index("ctx")
    spans = jnp.clip(
        cache_lengths - mine * latent_cache.shape[1], 0, latent_cache.shape[1]
    ).astype(jnp.int32)
    return jnp.stack(
        [
            attend_part(queries[r], latent_cache[r], spans[r : r + 1])
            for r in range(queries.shape[0])
        ]
    )


def join_cores(packed):
    mine, share = lax.axis_index("ctx"), packed.shape[1] // 2
    kept = lax.dynamic_slice_in_dim(packed, mine * share, share, 1)
    other = swap_ctx(lax.dynamic_slice_in_dim(packed, (1 - mine) * share, share, 1))
    kept_top, other_top = kept[:, :, LAT : LAT + 1], other[:, :, LAT : LAT + 1]
    joined_top = jnp.maximum(kept_top, other_top)
    kept_factor = jnp.exp(kept_top - joined_top)
    other_factor = jnp.exp(other_top - joined_top)
    joined = kept * kept_factor + other * other_factor
    return (joined[:, :, :LAT] / joined[:, :, LAT + 1 : LAT + 2]).astype(jnp.bfloat16)


def plane_of(owners):
    return owners == 16


def send(x, target):
    count = lax.axis_size("ep")
    return lax.ppermute(x, "ep", [(i, target(i)) for i in range(count)])


def to_x(x):
    return send(x, lambda i: i ^ 1)


def to_y(x):
    return send(x, lambda i: i ^ 2)


def to_z(x, steps):
    return send(x, lambda i: (i + 4 * steps) % 16)


def cat(*pieces):
    return jnp.concatenate(pieces, axis=0)


def after(x, other):
    return lax.optimization_barrier((x, other))[0]


def gather_rows(rows):
    n = rows.shape[0]
    h = n // 2
    below, above = to_z(rows, 1), to_z(rows, 3)
    own_x, own_y = to_x(rows), to_y(rows)
    far = to_z(after(rows, below), 2)
    bx = to_x(cat(below, above, own_y[h:]))
    by = to_y(cat(below, above, own_x[:h]))
    cx = to_x(cat(far, by[h:n], by[n + h : 2 * n]))
    cy = to_y(cat(far, bx[:h], bx[n : n + h]))
    dx = to_x(cy[h:n])
    dy = to_y(cx[:h])
    return [rows, own_x, own_y, below, above, bx, by, far, cx, cy, dx, dy]


TAKEN = (
    ((0, 0, 2), (1, 0, 2), (2, 0, 2), (6, 4, 5), (5, 4, 5)),
    ((3, 0, 2), (5, 0, 2), (6, 0, 2), (9, 2, 3), (8, 2, 3)),
    ((7, 0, 2), (8, 0, 2), (9, 0, 2), (11, 0, 1), (10, 0, 1)),
    ((4, 0, 2), (5, 2, 4), (6, 2, 4), (9, 3, 4), (8, 3, 4)),
)
OTHER = (
    ((0, 0, 2), (1, 0, 2), (1, 2, 4), (2, 9, 10), (2, 4, 5)),
    ((1, 4, 6), (2, 0, 2), (2, 5, 7), (3, 6, 7), (3, 2, 3)),
    ((2, 10, 12), (3, 0, 2), (3, 4, 6), (3, 9, 10), (3, 8, 9)),
    ((1, 6, 8), (2, 2, 4), (2, 7, 9), (3, 7, 8), (3, 3, 4)),
)
PLACES = (
    ((0, 0, 2), (0, 2, 4), (0, 4, 6), (1, 9, 10), (1, 4, 5)),
    ((0, 6, 8), (1, 0, 2), (1, 5, 7), (2, 8, 9), (2, 4, 5)),
    ((2, 0, 2), (2, 2, 4), (2, 6, 8), (3, 1, 2), (3, 0, 1)),
    ((0, 8, 10), (1, 2, 4), (1, 7, 9), (2, 9, 10), (2, 5, 6)),
)
BUNDLES = (10, 10, 10, 2)


def scatter_sums(kept, came):
    n = kept[3].shape[0]
    h = n // 2

    def share(b, first, last):
        at = slice(first * h, last * h)
        return kept[b][at].astype(jnp.float32) + came[b][at].astype(jnp.float32)

    def wide(x):
        return x.astype(jnp.float32)

    def narrow(*pieces):
        return cat(*pieces).astype(jnp.bfloat16)

    dx = wide(to_x(narrow(share(3, 0, 1))))
    dy = wide(to_y(narrow(share(3, 1, 2))))
    cx = wide(to_x(narrow(share(2, 2, 3) + dy, share(2, 3, 6))))
    cy = wide(to_y(narrow(share(2, 6, 7), share(2, 7, 8) + dx, share(2, 8, 10))))
    far = wide(to_z(narrow(share(2, 0, 2) + cx[:n] + cy[:n]), 2))
    bx = wide(
        to_x(
            narrow(
                share(1, 0, 1) + cy[n : n + h],
                share(1, 1, 2),
                share(1, 2, 3) + cy[n + h :],
                share(1, 3, 5),
            )
        )
    )
    by = wide(
        to_y(
            narrow(
                share(1, 5, 6),
                share(1, 6, 7) + cx[n : n + h],
                share(1, 7, 8),
                share(1, 8, 9) + cx[n + h :],
                share(1, 9, 10),
            )
        )
    )
    below = wide(to_z(narrow(share(0, 6, 8) + bx[:n] + by[:n]), 3))
    above = wide(to_z(narrow(share(0, 8, 10) + bx[n : 2 * n] + by[n : 2 * n]), 1))
    own_x = wide(to_x(narrow(share(0, 2, 3) + by[2 * n :], share(0, 3, 4))))
    own_y = wide(to_y(narrow(share(0, 4, 5), share(0, 5, 6) + bx[2 * n :])))
    return narrow(share(0, 0, 2) + own_x + own_y + below + above + far)


def expert_kernel(plan, first_ref, *refs):
    planes, group_count, expert_count, width, top = plan
    counts = (12, 4, 3) if planes else (1, 1, 3)
    counts += (4, 4) if planes else (1, 1)
    parts, done = [], 0
    for count in counts:
        parts.append(refs[done : done + count])
        done += count
    own, other, (gate_hbm, up_hbm, down_hbm), own_out, other_out = parts
    slots, select, scales, gate_buf, up_buf, down_buf, staged, sems, in_sems, out_sems = refs[done:]
    lanes = select.shape[2]
    half = lanes // 2
    piece = half // JOIN
    block = JOIN * CAP
    unit = piece // 2
    depth = gate_buf.shape[0]

    def loads(e):
        slot = lax.rem(e, depth)
        return [
            pltpu.make_async_copy(hbm.at[e], buf.at[slot], sems.at[k, slot])
            for k, (hbm, buf) in enumerate(
                ((gate_hbm, gate_buf), (up_hbm, up_buf), (down_hbm, down_buf))
            )
        ]

    def slot_range(group):
        if planes:
            return slice(group * block, (group + 1) * block)
        return pl.ds(pl.multiple_of(group * block, block), block)

    def block_of(group):
        return pl.ds(pl.multiple_of(group * half, half), half)

    def takes(group):
        if not planes:
            return [
                pltpu.make_async_copy(
                    ref[0].at[block_of(group)],
                    staged.at[0, pl.ds(k * half, half)],
                    in_sems.at[k],
                )
                for k, ref in enumerate((own, other))
            ]
        copies, at = [], 0
        for side, where in ((own, TAKEN), (other, OTHER)):
            for b, f, t in where[group]:
                rows = (t - f) * unit
                copies.append(
                    pltpu.make_async_copy(
                        side[b].at[pl.ds(f * unit, rows)],
                        staged.at[group, pl.ds(at, rows)],
                        in_sems.at[len(copies) + 10 * group],
                    )
                )
                at += rows
        return copies

    def puts(group):
        if not planes:
            return [
                pltpu.make_async_copy(
                    staged.at[0, pl.ds(k * half, half), pl.ds(0, width)],
                    ref[0].at[block_of(group)],
                    out_sems.at[k],
                )
                for k, ref in enumerate((own_out, other_out))
            ]
        copies, at = [], 0
        for side in (own_out, other_out):
            for b, f, t in PLACES[group]:
                rows = (t - f) * unit
                copies.append(
                    pltpu.make_async_copy(
                        staged.at[group, pl.ds(at, rows), pl.ds(0, width)],
                        side[b].at[pl.ds(f * unit, rows)],
                        out_sems.at[len(copies) + 10 * group],
                    )
                )
                at += rows
        return copies

    def stage_of(group):
        return group if planes else 0

    def sort_rows(group):
        copies = takes(group)
        if not planes:
            for copy in copies:
                copy.start()
        for copy in copies:
            copy.wait()
        rows_ref = staged.at[stage_of(group)]
        first = first_ref[0]
        named = rows_ref[:, width:].astype(jnp.float32).T
        ids = named[:top]
        gates = named[top : 2 * top] + named[2 * top : 3 * top] + named[3 * top : 4 * top]
        earlier = lax.broadcasted_iota(jnp.int32, (lanes, lanes), 0)
        later = lax.broadcasted_iota(jnp.int32, (lanes, lanes), 1)
        same = ((earlier // piece) % JOIN) == ((later // piece) % JOIN)
        before = jnp.where(same & (earlier < later), 1.0, 0.0).astype(jnp.bfloat16)
        hits, gated = [], []
        for e in range(expert_count):
            hit = ids == (first + e).astype(jnp.float32)
            hits.append(jnp.sum(jnp.where(hit, 1.0, 0.0), axis=0, keepdims=True))
            gated.append(jnp.sum(jnp.where(hit, gates, 0.0), axis=0, keepdims=True))
        padded = hits + [jnp.zeros_like(hits[0])] * (-expert_count % 8)
        places = jnp.dot(
            jnp.concatenate(padded, axis=0).astype(jnp.bfloat16),
            before,
            preferred_element_type=jnp.float32,
        )
        slot = lax.broadcasted_iota(jnp.int32, (block, lanes), 0)
        lane = lax.broadcasted_iota(jnp.int32, (block, lanes), 1)
        fits = (slot // CAP) == ((lane // piece) % JOIN)
        place = (slot % CAP).astype(jnp.float32)
        at = slot_range(group)
        for e in range(expert_count):
            wanted = jnp.where(hits[e] > 0.5, places[e : e + 1], -1.0)
            picked = jnp.where(fits & (wanted == place), 1.0, 0.0)
            scale = jnp.sum(picked * gated[e], axis=1, keepdims=True)
            scales[e, at, :] = jnp.broadcast_to(scale, (block, 128))
            select[group, e * block : (e + 1) * block, :] = picked.astype(jnp.bfloat16)
        chosen = select[group]
        for c in range(0, width, COLS):
            columns = slice(c, c + COLS)
            sorted_rows = jnp.dot(
                chosen, rows_ref[:, columns], preferred_element_type=jnp.float32
            ).astype(jnp.bfloat16)
            for e in range(expert_count):
                slots[e, at, columns] = sorted_rows[e * block : (e + 1) * block]

    def run_expert(e):
        slot = lax.rem(e, depth)
        gate_copy, up_copy, down_copy = loads(e)
        rows = slots[e]
        gate_copy.wait()
        gate = jnp.dot(rows, gate_buf[slot], preferred_element_type=jnp.float32)
        up_copy.wait()
        up = jnp.dot(rows, up_buf[slot], preferred_element_type=jnp.float32)
        hidden = (gate / (1.0 + jnp.exp(-gate))) * up * scales[e][:, :1]
        hidden = hidden.astype(jnp.bfloat16)
        down_copy.wait()
        for c in range(0, width, COLS):
            slots[e, :, c : c + COLS] = jnp.dot(
                hidden, down_buf[slot, :, c : c + COLS], preferred_element_type=jnp.float32
            ).astype(jnp.bfloat16)

        @pl.when(e + depth < expert_count)
        def _():
            for copy in loads(e + depth):
                copy.start()

    def sum_rows(group):
        chosen = select[group]
        at = slot_range(group)
        for c in range(0, width, COLS):
            columns = slice(c, c + COLS)
            outs = jnp.concatenate([slots[e, at, columns] for e in range(expert_count)], axis=0)
            rows = lax.dot_general(
                chosen, outs, (((0,), (0,)), ((), ())), preferred_element_type=jnp.float32
            )
            staged[stage_of(group), :, columns] = rows.astype(jnp.bfloat16)
        for copy in puts(group):
            copy.start()
        if not planes:
            for copy in puts(group):
                copy.wait()

    def each(count, work):
        lax.fori_loop(0, count, lambda i, _: (work(i), 0)[1], 0)

    if planes:
        for group in range(group_count):
            for copy in takes(group):
                copy.start()
    for e in range(min(depth, expert_count)):
        for copy in loads(e):
            copy.start()
    if planes:
        for group in range(group_count):
            sort_rows(group)
    else:
        each(group_count, sort_rows)
    each(expert_count, run_expert)
    if planes:
        for group in (2, 1, 3, 0):
            sum_rows(group)
        for group in (2, 1, 3, 0):
            for copy in puts(group):
                copy.wait()
    else:
        each(group_count, sum_rows)


def expert_sums(own, other, top, owners, first, gate_weight, up_weight, down_weight):
    expert_count, width, hidden = gate_weight.shape
    planes = plane_of(owners)
    group_count = owners // JOIN
    half = sum(x.shape[0] for x in own) // group_count
    slot_rows = group_count * JOIN * CAP
    depth = min(3, expert_count)
    if planes:
        out_rows = [u * half // 8 for u in BUNDLES] * 2
    else:
        out_rows = [own[0].shape[0]] * 2
    stages, copies = (group_count, 10 * group_count) if planes else (1, 2)
    weight_bytes = 3 * expert_count * width * hidden * 2
    sums = pl.pallas_call(
        functools.partial(expert_kernel, (planes, group_count, expert_count, width, top)),
        out_shape=[jax.ShapeDtypeStruct((r, width), jnp.bfloat16) for r in out_rows],
        in_specs=[pl.BlockSpec(memory_space=pltpu.SMEM)]
        + [pl.BlockSpec(memory_space=pl.ANY)] * (len(own) + len(other) + 3),
        out_specs=[pl.BlockSpec(memory_space=pl.ANY)] * len(out_rows),
        scratch_shapes=[
            pltpu.VMEM((expert_count, slot_rows, width), jnp.bfloat16),
            pltpu.VMEM((group_count, expert_count * JOIN * CAP, 2 * half), jnp.bfloat16),
            pltpu.VMEM((expert_count, slot_rows, 128), jnp.float32),
            pltpu.VMEM((depth, width, hidden), jnp.bfloat16),
            pltpu.VMEM((depth, width, hidden), jnp.bfloat16),
            pltpu.VMEM((depth, hidden, width), jnp.bfloat16),
            pltpu.VMEM((stages, 2 * half, own[0].shape[1]), jnp.bfloat16),
            pltpu.SemaphoreType.DMA((3, depth)),
            pltpu.SemaphoreType.DMA((copies,)),
            pltpu.SemaphoreType.DMA((copies,)),
        ],
        compiler_params=pltpu.CompilerParams(vmem_limit_bytes=VMEM_LIMIT),
        cost_estimate=pl.CostEstimate(
            flops=slot_rows * weight_bytes,
            bytes_accessed=weight_bytes,
            transcendentals=expert_count * slot_rows * hidden,
        ),
    )(first, *own, *other, gate_weight, up_weight, down_weight)
    return sums[: len(sums) // 2], sums[len(sums) // 2 :]


def ask_kernel(core_ref, rows_hbm, routes_hbm, gates_hbm, own_ref, other_ref, routes, gates, sems):
    width = rows_hbm.shape[1]
    half = rows_hbm.shape[0] // 2
    small = [
        pltpu.make_async_copy(routes_hbm, routes, sems.at[0]),
        pltpu.make_async_copy(gates_hbm, gates, sems.at[1]),
    ]
    large = [
        pltpu.make_async_copy(
            rows_hbm.at[pl.ds(pl.multiple_of(from_half * half, half), half)],
            ref.at[:, pl.ds(0, width)],
            sems.at[2 + k],
        )
        for k, (from_half, ref) in enumerate(
            ((core_ref[0], own_ref), (1 - core_ref[0], other_ref))
        )
    ]
    for copy in small + large:
        copy.start()
    for copy in small:
        copy.wait()
    terms = [routes[...].astype(jnp.float32)]
    left = gates[...]
    for _ in range(3):
        term = left.astype(jnp.bfloat16).astype(jnp.float32)
        terms.append(term)
        left = left - term
    blank = 128 - sum(t.shape[0] for t in terms)
    asked = jnp.concatenate(terms + [jnp.zeros((blank, 2 * half), jnp.float32)], axis=0).T
    asked = asked.astype(jnp.bfloat16)
    first, last = asked[:half], asked[half:]
    mine = core_ref[0] == 0
    own_ref[:, width:] = jnp.where(mine, first, last)
    other_ref[:, width:] = jnp.where(mine, last, first)
    for copy in large:
        copy.wait()


def ask(moe_rows, routes, route_gates, core):
    rows, width = moe_rows.shape
    half = jax.ShapeDtypeStruct((rows // 2, width + 128), jnp.bfloat16)
    return pl.pallas_call(
        ask_kernel,
        out_shape=(half, half),
        in_specs=[pl.BlockSpec(memory_space=pltpu.SMEM)]
        + [pl.BlockSpec(memory_space=pl.ANY)] * 3,
        out_specs=[pl.BlockSpec(memory_space=pltpu.VMEM)] * 2,
        scratch_shapes=[
            pltpu.VMEM(routes.shape[::-1], jnp.int32),
            pltpu.VMEM(routes.shape[::-1], jnp.float32),
            pltpu.SemaphoreType.DMA((4,)),
        ],
        compiler_params=pltpu.CompilerParams(vmem_limit_bytes=4 * 1024 * 1024),
    )(core.astype(jnp.int32).reshape(1), moe_rows, routes.T, route_gates.T)


def route_rows(moe_rows, routes, route_gates, gate_weight, up_weight, down_weight, packed):
    owners = lax.axis_size("ep")
    top = routes.shape[1]
    core, chip = lax.axis_index("ctx"), lax.axis_index("ep")
    first = (chip * gate_weight.shape[0]).astype(jnp.int32).reshape(1)

    mine, theirs = ask(moe_rows, routes, route_gates, core)
    if plane_of(owners):
        own = gather_rows(mine)
        other = [theirs] + [swap_ctx(cat(*x)) for x in (own[1:5], own[5:8], own[8:])]
    else:
        own = [lax.all_gather(mine, "ep", tiled=True)]
        other = [swap_ctx(own[0])]
    first, packed = lax.optimization_barrier((first, packed))
    own_sums, other_sums = expert_sums(
        own, other, top, owners, first, gate_weight, up_weight, down_weight
    )
    came = [None] * len(own_sums)
    for b in reversed(range(len(own_sums))):
        came[b] = swap_ctx(other_sums[b])
    if plane_of(owners):
        own_final = scatter_sums(own_sums, came)
    else:
        own_final = lax.psum_scatter(own_sums[0] + came[0], "ep", scatter_dimension=0, tiled=True)
    other_final = swap_ctx(own_final)
    routed = jnp.where(core == 0, cat(own_final, other_final), cat(other_final, own_final))
    return routed, packed


def body(
    moe_rows,
    routes,
    route_gates,
    gate_weight,
    up_weight,
    down_weight,
    queries,
    latent_cache,
    cache_lengths,
):
    packed = attend_local(queries, latent_cache, cache_lengths)
    routed_output, packed = route_rows(
        moe_rows, routes, route_gates, gate_weight, up_weight, down_weight, packed
    )
    return (routed_output, join_cores(packed))


def solution(mesh):
    in_specs = (
        P("ep", None),
        P("ep", None),
        P("ep", None),
        P("ep", None, "ctx"),
        P("ep", None, "ctx"),
        P("ep", "ctx", None),
        P("ep", None, None),
        P("ep", "ctx", None),
        P("ep"),
    )
    out_specs = (P("ep", None), P("ep", "ctx", None))
    return jax.shard_map(body, mesh=mesh, in_specs=in_specs, out_specs=out_specs, check_vma=False)
```

time: 160 us -> 152 us (0.950)
  local copies, waits for them, and re-layouts: 14.3 us -> 5.41 us
  waiting for transfers between devices: 59.4 us -> 67 us
  matrix products: 4.16 us -> 0 us
  other arithmetic: 9.85 us -> 8.13 us
    ppermute x22, waiting for transfers between devices: 57.4 us -> 65 us  [send(): return lax.ppermute(x, 'ep', [(i, target(i)) for i in range(count)])]
    dot_general x2 -> x0, matrix products: 4.16 us -> none  [the longest x1 2.34 us: softmax_parts(): jnp.einsum('rhk,rlk->rhl', queries, cache, preferred_element_type=jnp.flo...]
    concatenate x8 -> x11, other arithmetic: 0.34 us -> 3.88 us  [cat(): return jnp.concatenate(pieces, axis=0)]
    unnamed x27 -> x50, local copies, waits for them, and re-layouts: 7.38 us -> 4.27 us
    concatenate x6 -> x0, local copies, waits for them, and re-layouts: 2.8 us -> none  [the longest x4 1.6 us: cat(): return jnp.concatenate(pieces, axis=0)]
    another operation x6, other arithmetic: 3.56 us -> 1.51 us
    pallas_call x1 -> x3, Pallas kernels: 40.4 us -> 40 us  [the longest x1 38.4 us: expert_sums(): pl.pallas_call(functools.partial(expert_kernel, (planes, group_count, exp...]
  transfers between devices with their start and end apart: 32 -> 31, of which waited for: 16 -> 20; matrix products, arithmetic and copies ran while one was open for 14% -> 5% of each run, Pallas kernels for 0% -> 1%
where the time goes in v3:
time: 152 us; the launch traced here: 151 us
  waiting for transfers between devices  67 us (44%)
  Pallas kernels  40 us (26%)
  starting transfers between devices  28.9 us (19%)
  other arithmetic  8.13 us (5%)
  local copies, waits for them, and re-layouts  5.41 us (4%)
  between operations  1.72 us (1%)
    ppermute x22, waiting for transfers between devices, send(): return lax.ppermute(x, 'ep', [(i, target(i)) for i in range(count)])  65 us
    pallas_call x1, Pallas kernels, expert_sums(): pl.pallas_call(functools.partial(expert_kernel, (planes, group_count, exp...  38.4 us
    ppermute x22, starting transfers between devices, send(): return lax.ppermute(x, 'ep', [(i, target(i)) for i in range(count)])  27.1 us
    unnamed x50, local copies, waits for them, and re-layouts  4.27 us
    concatenate x11, other arithmetic, cat(): return jnp.concatenate(pieces, axis=0)  3.88 us
  transfers between devices with their start and end apart: 31, of which 20 were waited for; matrix products, arithmetic and copies ran while one was open for 5% of the time, Pallas kernels for 1%

profile of v3, /device:TPU:0, one launch (start us, length us, event | category | flops | bytes accessed | tf_op | source)
XLA Modules:
  0.0 151.2 jit_solution(8735913631949776422)
XLA Ops:
  0.6 1.0 copy-done.11
  1.7 0.7 copy-done.17
  2.3 0.7 copy-done.18
  3.0 0.3 shard_map.105
  3.3 0.7 copy-done.14
  4.0 3.0 %collective-permute-start.1 = (bf16[32,3712]{1,0:T(8,128)(2,1)S(1)}, bf16[32,3712]{1,0:T(8,128)(2,1)S(1)}, u32[]{:S(2)}, u32[]{:S(2)}) collective-permute-start(bf16[32,3712]{1,0:T(8,128)(2,1)S(1)} %get-tuple-element.17.refs_0_), channel_id=1, source_target_pairs={{0,2},{1,3},{2,0},{3,1},{4,6},{5,7},{6,4},{7,5},{8,10},{9,11},{10,... | collective-permute-start | bytes 712712 | tf_op jit(solution)/shard_map/ppermute | solution.py:95
  7.0 1.5 collective-permute-start
  8.5 3.6 %collective-permute-start.3 = (bf16[32,3712]{1,0:T(8,128)(2,1)S(1)}, bf16[32,3712]{1,0:T(8,128)(2,1)S(1)}, u32[]{:S(2)}, u32[]{:S(2)}) collective-permute-start(bf16[32,3712]{1,0:T(8,128)(2,1)S(1)} %get-tuple-element.17.refs_0_), channel_id=1, source_target_pairs={{0,12},{1,13},{2,14},{3,15},{4,0},{5,1},{6,2},{7,3},{8,4},{9,5},{1... | collective-permute-start | bytes 712712 | tf_op jit(solution)/shard_map/ppermute | solution.py:95
  12.1 0.7 collective-permute-done.1.refs_2_
  12.8 1.4 collective-permute-done.refs_1_
  14.2 4.1 %collective-permute-done.3.refs_4_ = bf16[32,3712]{1,0:T(8,128)(2,1)S(1)} collective-permute-done((bf16[32,3712]{1,0:T(8,128)(2,1)S(1)}, bf16[32,3712]{1,0:T(8,128)(2,1)S(1)}, u32[]{:S(2)}, u32[]{:S(2)}) %collective-permute-start.3) | collective-permute-done | bytes 237600 | tf_op jit(solution)/shard_map/ppermute | solution.py:95
  18.3 4.2 %collective-permute-done.2.refs_3_ = bf16[32,3712]{1,0:T(8,128)(2,1)S(1)} collective-permute-done((bf16[32,3712]{1,0:T(8,128)(2,1)S(1)}, bf16[32,3712]{1,0:T(8,128)(2,1)S(1)}, u32[]{:S(2)}, u32[]{:S(2)}) %collective-permute-start.2) | collective-permute-done | bytes 237600 | tf_op jit(solution)/shard_map/ppermute | solution.py:95
  22.6 0.6 collective-permute-start.5
  23.2 0.7 collective-permute-start.6
  24.0 0.5 collective-permute-start.4
  24.5 11.9 %collective-permute-done.5.refs_6_ = bf16[80,3712]{1,0:T(8,128)(2,1)S(1)} collective-permute-done((bf16[80,3712]{1,0:T(8,128)(2,1)S(1)}, bf16[80,3712]{1,0:T(8,128)(2,1)S(1)}, u32[]{:S(2)}, u32[]{:S(2)}) %collective-permute-start.5) | collective-permute-done | bytes 593952 | tf_op jit(solution)/shard_map/ppermute | solution.py:95
  36.4 0.2 collective-permute-done.4.refs_5_
  36.7 1.6 %collective-permute-start.8 = (bf16[64,3712]{1,0:T(8,128)(2,1)S(1)}, bf16[64,3712]{1,0:T(8,128)(2,1)S(1)}, u32[]{:S(2)}, u32[]{:S(2)}) collective-permute-start(bf16[64,3712]{1,0:T(8,128)(2,1)S(1)} %get-tuple-element.50), channel_id=1, source_target_pairs={{0,2},{1,3},{2,0},{3,1},{4,6},{5,7},{6,4},{7,5},{8,10},{9,11},{10,... | collective-permute-start | bytes 1425416 | tf_op jit(solution)/shard_map/ppermute | solution.py:95
  38.3 0.5 collective-permute-start.7
  38.8 8.1 %collective-permute-done.8.refs_9_ = bf16[64,3712]{1,0:T(8,128)(2,1)S(1)} collective-permute-done((bf16[64,3712]{1,0:T(8,128)(2,1)S(1)}, bf16[64,3712]{1,0:T(8,128)(2,1)S(1)}, u32[]{:S(2)}, u32[]{:S(2)}) %collective-permute-start.8) | collective-permute-done | bytes 475168 | tf_op jit(solution)/shard_map/ppermute | solution.py:95
  47.0 0.4 collective-permute-start.9
  47.4 1.8 %collective-permute-done.7.refs_8_ = bf16[64,3712]{1,0:T(8,128)(2,1)S(1)} collective-permute-done((bf16[64,3712]{1,0:T(8,128)(2,1)S(1)}, bf16[64,3712]{1,0:T(8,128)(2,1)S(1)}, u32[]{:S(2)}, u32[]{:S(2)}) %collective-permute-start.7) | collective-permute-done | bytes 475168 | tf_op jit(solution)/shard_map/ppermute | solution.py:95
  49.3 0.7 collective-permute-start.10
  49.9 1.3 pad_maximum_fusion
  51.2 0.7 collective-permute-done.9.refs_10_
  51.9 2.3 %collective-permute-done.10.refs_11_ = bf16[16,3712]{1,0:T(8,128)(2,1)S(1)} collective-permute-done((bf16[16,3712]{1,0:T(8,128)(2,1)S(1)}, bf16[16,3712]{1,0:T(8,128)(2,1)S(1)}, u32[]{:S(2)}, u32[]{:S(2)}) %collective-permute-start.10) | collective-permute-done | bytes 118816 | tf_op jit(solution)/shard_map/ppermute | solution.py:95
  54.2 1.2 pad_maximum_fusion.1
  55.4 1.0 pad_maximum_fusion.2
  56.4 0.5 collective-permute-start.11
  57.6 0.9 copy-done.16
  58.5 1.4 shard_map.104
  60.0 38.4 %shard_map.106 = (bf16[160,3584]{1,0:T(8,128)(2,1)}, bf16[160,3584]{1,0:T(8,128)(2,1)}, bf16[160,3584]{1,0:T(8,128)(2,1)}, bf16[32,3584]{1,0:T(8,128)(2,1)S(1)},...) custom-call(s32[1]{0:T(128)} %bitcast.first_ref, ...), custom_call_target="tpu_custom_call" | custom-call | flops 11274289152 | bytes 88080384 | tf_op jit(solution)/shard_map/pallas_call | solution.py:409
  98.4 0.2 collective-permute-start.16
  98.6 0.4 collective-permute-start.17
  99.0 0.9 constant_dynamic-slice_fusion
  99.9 0.2 collective-permute-start.30
  100.0 0.4 collective-permute-start.14
  100.4 0.2 collective-permute-start.15
  100.6 1.3 collective-permute-done.17
  101.9 0.3 collective-permute-start.18
  102.3 1.1 collective-permute-start.22
  103.4 1.1 add_convert_fusion
  104.5 2.7 %collective-permute-done.18 = bf16[16,3584]{1,0:T(8,128)(2,1)S(1)} collective-permute-done((bf16[16,3584]{1,0:T(8,128)(2,1)S(1)}, bf16[16,3584]{1,0:T(8,128)(2,1)S(1)}, u32[]{:S(2)}, u32[]{:S(2)}) %collective-permute-start.18) | collective-permute-done | bytes 114720 | tf_op jit(solution)/shard_map/ppermute | solution.py:95
  107.4 1.3 collective-permute-start.19
  108.8 0.8 collective-permute-start.23
  109.7 10.4 %collective-permute-done.23 = bf16[64,3584]{1,0:T(8,128)(2,1)S(1)} collective-permute-done((bf16[64,3584]{1,0:T(8,128)(2,1)S(1)}, bf16[64,3584]{1,0:T(8,128)(2,1)S(1)}, u32[]{:S(2)}, u32[]{:S(2)}) %collective-permute-start.23) | collective-permute-done | bytes 458784 | tf_op jit(solution)/shard_map/ppermute | solution.py:95
  120.4 1.0 collective-permute-start.24
  121.6 1.5 collective-permute-start.20
  123.2 2.2 %collective-permute-start.28 = (bf16[32,3584]{1,0:T(8,128)(2,1)S(1)}, bf16[32,3584]{1,0:T(8,128)(2,1)S(1)}, u32[]{:S(2)}, u32[]{:S(2)}) collective-permute-start(bf16[32,3584]{1,0:T(8,128)(2,1)S(1)} %fusion.2), channel_id=1, source_target_pairs={{0,8},{1,9},{2,10},{3,11},{4,12},{5,13},{6,14},{7,15},{8,0},{9,1},... | collective-permute-start | bytes 688136 | tf_op jit(solution)/shard_map/ppermute | solution.py:95
  125.4 7.9 %collective-permute-done.24 = bf16[80,3584]{1,0:T(8,128)(2,1)S(1)} collective-permute-done((bf16[80,3584]{1,0:T(8,128)(2,1)S(1)}, bf16[80,3584]{1,0:T(8,128)(2,1)S(1)}, u32[]{:S(2)}, u32[]{:S(2)}) %collective-permute-start.24) | collective-permute-done | bytes 573472 | tf_op jit(solution)/shard_map/ppermute | solution.py:95
  133.4 0.9 collective-permute-done.20
  134.4 0.2 copy-done.22
  134.8 1.5 collective-permute-start.25
  136.3 0.8 collective-permute-start.21
  137.1 0.2 fusion.4
  137.3 3.5 %collective-permute-start.26 = (bf16[32,3584]{1,0:T(8,128)(2,1)S(1)}, bf16[32,3584]{1,0:T(8,128)(2,1)S(1)}, u32[]{:S(2)}, u32[]{:S(2)}) collective-permute-start(bf16[32,3584]{1,0:T(8,128)(2,1)S(1)} %get-tuple-element.30), channel_id=1, source_target_pairs={{0,12},{1,13},{2,14},{3,15},{4,0},{5,1},{6,2},{7,3},{8,4},{9,5},{1... | collective-permute-start | bytes 688136 | tf_op jit(solution)/shard_map/ppermute | solution.py:95
  141.0 1.4 collective-permute-done.21
  142.3 3.5 %collective-permute-done.26 = bf16[32,3584]{1,0:T(8,128)(2,1)S(1)} collective-permute-done((bf16[32,3584]{1,0:T(8,128)(2,1)S(1)}, bf16[32,3584]{1,0:T(8,128)(2,1)S(1)}, u32[]{:S(2)}, u32[]{:S(2)}) %collective-permute-start.26) | collective-permute-done | bytes 229408 | tf_op jit(solution)/shard_map/ppermute | solution.py:95
  145.8 2.8 %collective-permute-done.27 = bf16[32,3584]{1,0:T(8,128)(2,1)S(1)} collective-permute-done((bf16[32,3584]{1,0:T(8,128)(2,1)S(1)}, bf16[32,3584]{1,0:T(8,128)(2,1)S(1)}, u32[]{:S(2)}, u32[]{:S(2)}) %collective-permute-start.27) | collective-permute-done | bytes 229408 | tf_op jit(solution)/shard_map/ppermute | solution.py:95
  148.6 0.2 add_convert_fusion.1
  148.9 0.2 slice_reduce_fusion
  149.1 0.7 fusion.16
  149.8 0.6 collective-permute-done.29
  150.4 0.8 maximum_select_fusion
  (92 shorter events, 2.0 us)
Async XLA Ops:
  0.6 1.0 copy-start.11
  1.7 0.7 copy-start.17
  2.3 0.7 copy-start.18
  3.3 0.7 copy-start.14
  4.0 19.2 %copy-start.12 = (bf16[32,3712]{1,0:T(8,128)(2,1)}, bf16[32,3712]{1,0:T(8,128)(2,1)S(1)}, u32[]{:S(2)}) copy-start(bf16[32,3712]{1,0:T(8,128)(2,1)S(1)} %get-tuple-element.17.refs_0_) | copy-start | bytes 712708
  4.0 8.7 %collective-permute-start.1 = (bf16[32,3712]{1,0:T(8,128)(2,1)S(1)}, bf16[32,3712]{1,0:T(8,128)(2,1)S(1)}, u32[]{:S(2)}, u32[]{:S(2)}) collective-permute-start(bf16[32,3712]{1,0:T(8,128)(2,1)S(1)} %get-tuple-element.17.refs_0_), channel_id=1, source_target_pairs={{0,2},{1,3},{2,0},{3,1},{4,6},{5,7},{6,4},{7,5},{8,10},{9,11},{10,... | collective-permute-start | bytes 712712 | tf_op jit(solution)/shard_map/ppermute | solution.py:95
  7.0 7.2 %collective-permute-start = (bf16[32,3712]{1,0:T(8,128)(2,1)S(1)}, bf16[32,3712]{1,0:T(8,128)(2,1)S(1)}, u32[]{:S(2)}, u32[]{:S(2)}) collective-permute-start(bf16[32,3712]{1,0:T(8,128)(2,1)S(1)} %get-tuple-element.17.refs_0_), channel_id=1, source_target_pairs={{0,1},{1,0},{2,3},{3,2},{4,5},{5,4},{6,7},{7,6},{8,9},{9,8},{10,11... | collective-permute-start | bytes 712712 | tf_op jit(solution)/shard_map/ppermute | solution.py:95
  8.5 9.8 %collective-permute-start.3 = (bf16[32,3712]{1,0:T(8,128)(2,1)S(1)}, bf16[32,3712]{1,0:T(8,128)(2,1)S(1)}, u32[]{:S(2)}, u32[]{:S(2)}) collective-permute-start(bf16[32,3712]{1,0:T(8,128)(2,1)S(1)} %get-tuple-element.17.refs_0_), channel_id=1, source_target_pairs={{0,12},{1,13},{2,14},{3,15},{4,0},{5,1},{6,2},{7,3},{8,4},{9,5},{1... | collective-permute-start | bytes 712712 | tf_op jit(solution)/shard_map/ppermute | solution.py:95
  12.1 10.5 %collective-permute-start.2 = (bf16[32,3712]{1,0:T(8,128)(2,1)S(1)}, bf16[32,3712]{1,0:T(8,128)(2,1)S(1)}, u32[]{:S(2)}, u32[]{:S(2)}) collective-permute-start(bf16[32,3712]{1,0:T(8,128)(2,1)S(1)} %get-tuple-element.17.refs_0_), channel_id=1, source_target_pairs={{0,4},{1,5},{2,6},{3,7},{4,8},{5,9},{6,10},{7,11},{8,12},{9,13},{1... | collective-permute-start | bytes 712712 | tf_op jit(solution)/shard_map/ppermute | solution.py:95
  12.8 42.6 %copy-start.1 = (bf16[32,3712]{1,0:T(8,128)(2,1)}, bf16[32,3712]{1,0:T(8,128)(2,1)S(1)}, u32[]{:S(2)}) copy-start(bf16[32,3712]{1,0:T(8,128)(2,1)S(1)} %collective-permute-done.1.refs_2_) | copy-start | bytes 712708
  14.2 41.2 %copy-start.3 = (bf16[32,3712]{1,0:T(8,128)(2,1)}, bf16[32,3712]{1,0:T(8,128)(2,1)S(1)}, u32[]{:S(2)}) copy-start(bf16[32,3712]{1,0:T(8,128)(2,1)S(1)} %collective-permute-done.refs_1_) | copy-start | bytes 712708
  22.6 13.7 %collective-permute-start.5 = (bf16[80,3712]{1,0:T(8,128)(2,1)S(1)}, bf16[80,3712]{1,0:T(8,128)(2,1)S(1)}, u32[]{:S(2)}, u32[]{:S(2)}) collective-permute-start(bf16[80,3712]{1,0:T(8,128)(2,1)S(1)} %get-tuple-element.46), channel_id=1, source_target_pairs={{0,2},{1,3},{2,0},{3,1},{4,6},{5,7},{6,4},{7,5},{8,10},{9,11},{10,... | collective-permute-start | bytes 1781768 | tf_op jit(solution)/shard_map/ppermute | solution.py:95
  23.2 13.4 %collective-permute-start.6 = (bf16[32,3712]{1,0:T(8,128)(2,1)S(1)}, bf16[32,3712]{1,0:T(8,128)(2,1)S(1)}, u32[]{:S(2)}, u32[]{:S(2)}) collective-permute-start(bf16[32,3712]{1,0:T(8,128)(2,1)S(1)} %get-tuple-element.17.refs_0_), channel_id=1, source_target_pairs={{0,8},{1,9},{2,10},{3,11},{4,12},{5,13},{6,14},{7,15},{8,0},{9,1},... | collective-permute-start | bytes 712712 | tf_op jit(solution)/shard_map/ppermute | solution.py:95
  24.0 12.7 %collective-permute-start.4 = (bf16[80,3712]{1,0:T(8,128)(2,1)S(1)}, bf16[80,3712]{1,0:T(8,128)(2,1)S(1)}, u32[]{:S(2)}, u32[]{:S(2)}) collective-permute-start(bf16[80,3712]{1,0:T(8,128)(2,1)S(1)} %get-tuple-element.47), channel_id=1, source_target_pairs={{0,1},{1,0},{2,3},{3,2},{4,5},{5,4},{6,7},{7,6},{8,9},{9,8},{10,11... | collective-permute-start | bytes 1781768 | tf_op jit(solution)/shard_map/ppermute | solution.py:95
  36.4 13.5 %copy-start.19 = (bf16[80,3712]{1,0:T(8,128)(2,1)}, bf16[80,3712]{1,0:T(8,128)(2,1)S(1)}, u32[]{:S(2)}) copy-start(bf16[80,3712]{1,0:T(8,128)(2,1)S(1)} %collective-permute-done.5.refs_6_) | copy-start | bytes 1781764
  36.6 13.3 %copy-start.20 = (bf16[80,3712]{1,0:T(8,128)(2,1)}, bf16[80,3712]{1,0:T(8,128)(2,1)S(1)}, u32[]{:S(2)}) copy-start(bf16[80,3712]{1,0:T(8,128)(2,1)S(1)} %collective-permute-done.4.refs_5_) | copy-start | bytes 1781764
  36.7 10.2 %collective-permute-start.8 = (bf16[64,3712]{1,0:T(8,128)(2,1)S(1)}, bf16[64,3712]{1,0:T(8,128)(2,1)S(1)}, u32[]{:S(2)}, u32[]{:S(2)}) collective-permute-start(bf16[64,3712]{1,0:T(8,128)(2,1)S(1)} %get-tuple-element.50), channel_id=1, source_target_pairs={{0,2},{1,3},{2,0},{3,1},{4,6},{5,7},{6,4},{7,5},{8,10},{9,11},{10,... | collective-permute-start | bytes 1425416 | tf_op jit(solution)/shard_map/ppermute | solution.py:95
  38.3 10.9 %collective-permute-start.7 = (bf16[64,3712]{1,0:T(8,128)(2,1)S(1)}, bf16[64,3712]{1,0:T(8,128)(2,1)S(1)}, u32[]{:S(2)}, u32[]{:S(2)}) collective-permute-start(bf16[64,3712]{1,0:T(8,128)(2,1)S(1)} %get-tuple-element.51), channel_id=1, source_target_pairs={{0,1},{1,0},{2,3},{3,2},{4,5},{5,4},{6,7},{7,6},{8,9},{9,8},{10,11... | collective-permute-start | bytes 1425416 | tf_op jit(solution)/shard_map/ppermute | solution.py:95
  47.0 7.2 %copy-start.21 = (bf16[64,3712]{1,0:T(8,128)(2,1)}, bf16[64,3712]{1,0:T(8,128)(2,1)S(1)}, u32[]{:S(2)}) copy-start(bf16[64,3712]{1,0:T(8,128)(2,1)S(1)} %collective-permute-done.8.refs_9_) | copy-start | bytes 1425412
  47.0 4.9 %collective-permute-start.9 = (bf16[16,3712]{1,0:T(8,128)(2,1)S(1)}, bf16[16,3712]{1,0:T(8,128)(2,1)S(1)}, u32[]{:S(2)}, u32[]{:S(2)}) collective-permute-start(bf16[16,3712]{1,0:T(8,128)(2,1)S(1)} %slice.294), channel_id=1, source_target_pairs={{0,1},{1,0},{2,3},{3,2},{4,5},{5,4},{6,7},{7,6},{8,9},{9,8},{10,11... | collective-permute-start | bytes 356360 | tf_op jit(solution)/shard_map/ppermute | solution.py:95
  49.3 4.9 %collective-permute-start.10 = (bf16[16,3712]{1,0:T(8,128)(2,1)S(1)}, bf16[16,3712]{1,0:T(8,128)(2,1)S(1)}, u32[]{:S(2)}, u32[]{:S(2)}) collective-permute-start(bf16[16,3712]{1,0:T(8,128)(2,1)S(1)} %slice.295), channel_id=1, source_target_pairs={{0,2},{1,3},{2,0},{3,1},{4,6},{5,7},{6,4},{7,5},{8,10},{9,11},{10,... | collective-permute-start | bytes 356360 | tf_op jit(solution)/shard_map/ppermute | solution.py:95
  51.2 8.7 %collective-permute-start.12 = (bf16[192,3712]{1,0:T(8,128)(2,1)}, bf16[192,3712]{1,0:T(8,128)(2,1)}, u32[]{:S(2)}, u32[]{:S(2)}) collective-permute-start(bf16[192,3712]{1,0:T(8,128)(2,1)} %pad_maximum_fusion), channel_id=1, source_target_pairs={{0,16},{16,0},{1,17},{17,1},{2,18},{18,2},{3,19},{19,3},{4,20},{20... | collective-permute-start | bytes 4276232 | tf_op jit(solution)/shard_map/ppermute | solution.py:61
  51.9 3.5 %copy-start.7 = (bf16[16,3712]{1,0:T(8,128)(2,1)}, bf16[16,3712]{1,0:T(8,128)(2,1)S(1)}, u32[]{:S(2)}) copy-start(bf16[16,3712]{1,0:T(8,128)(2,1)S(1)} %collective-permute-done.9.refs_10_) | copy-start | bytes 356356
  54.2 1.2 copy-start.9
  54.2 3.4 %copy-start = (bf16[1,2048,576]{1,2,0:T(8,128)(2,1)S(1)}, bf16[1,2048,576]{1,2,0:T(8,128)(2,1)}, u32[]{:S(2)}) copy-start(bf16[1,2048,576]{1,2,0:T(8,128)(2,1)} %param.16) | copy-start | bytes 7077892
  55.4 4.6 %collective-permute-start.13 = (bf16[160,3712]{1,0:T(8,128)(2,1)}, bf16[160,3712]{1,0:T(8,128)(2,1)}, u32[]{:S(2)}, u32[]{:S(2)}) collective-permute-start(bf16[160,3712]{1,0:T(8,128)(2,1)} %pad_maximum_fusion.1), channel_id=1, source_target_pairs={{0,16},{16,0},{1,17},{17,1},{2,18},{18,2},{3,19},{19,3},{4,20},{20... | collective-permute-start | bytes 3563528 | tf_op jit(solution)/shard_map/ppermute | solution.py:61
  56.4 3.5 %collective-permute-start.11 = (bf16[128,3712]{1,0:T(8,128)(2,1)}, bf16[128,3712]{1,0:T(8,128)(2,1)}, u32[]{:S(2)}, u32[]{:S(2)}) collective-permute-start(bf16[128,3712]{1,0:T(8,128)(2,1)} %pad_maximum_fusion.2), channel_id=1, source_target_pairs={{0,16},{16,0},{1,17},{17,1},{2,18},{18,2},{3,19},{19,3},{4,20},{20... | collective-permute-start | bytes 2850824 | tf_op jit(solution)/shard_map/ppermute | solution.py:61
  57.6 0.9 copy-start.16
  58.5 1.5 copy-start.2
  58.5 1.5 copy-start.4
  58.5 1.5 copy-start.8
  58.5 1.5 copy-start.10
  58.5 1.5 copy-start.13
  58.5 1.5 copy-start.15
  59.9 38.5 %copy-start.5 = (f32[64,640]{1,0:T(8,128)}, f32[64,640]{1,0:T(8,128)S(1)}, u32[]{:S(2)}) copy-start(f32[64,640]{1,0:T(8,128)S(1)} %shard_map.104) | copy-start | bytes 491524
  98.4 8.9 %copy-start.23 = (bf16[160,3584]{1,0:T(8,128)(2,1)S(1)}, bf16[160,3584]{1,0:T(8,128)(2,1)}, u32[]{:S(2)}) copy-start(bf16[160,3584]{1,0:T(8,128)(2,1)} %get-tuple-element.23) | copy-start | bytes 3440644
  98.4 3.9 %collective-permute-start.16 = (bf16[160,3584]{1,0:T(8,128)(2,1)}, bf16[160,3584]{1,0:T(8,128)(2,1)S(1)}, u32[]{:S(2)}, u32[]{:S(2)}) collective-permute-start(bf16[160,3584]{1,0:T(8,128)(2,1)} %get-tuple-element.24), channel_id=1, source_target_pairs={{0,16},{16,0},{1,17},{17,1},{2,18},{18,2},{3,19},{19,3},{4,20},{20... | collective-permute-start | bytes 3440648 | tf_op jit(solution)/shard_map/ppermute | solution.py:61
  98.6 3.2 %collective-permute-start.17 = (bf16[32,3584]{1,0:T(8,128)(2,1)S(1)}, bf16[32,3584]{1,0:T(8,128)(2,1)S(1)}, u32[]{:S(2)}, u32[]{:S(2)}) collective-permute-start(bf16[32,3584]{1,0:T(8,128)(2,1)S(1)} %get-tuple-element.26), channel_id=1, source_target_pairs={{0,16},{16,0},{1,17},{17,1},{2,18},{18,2},{3,19},{19,3},{4,20},{20... | collective-permute-start | bytes 688136 | tf_op jit(solution)/shard_map/ppermute | solution.py:61
  99.9 40.8 %collective-permute-start.30 = (f32[1,32,640]{2,1,0:T(8,128)S(1)}, f32[1,32,640]{2,1,0:T(8,128)S(1)}, u32[]{:S(2)}, u32[]{:S(2)}) collective-permute-start(f32[1,32,640]{2,1,0:T(8,128)S(1)} %constant_dynamic-slice_fusion), channel_id=1, source_target_pairs={{0,16},{16,0},{1,17},{17,1},{2,18},{18,2},{3,19},{19,3},{4,20},{20... | collective-permute-start | bytes 245768 | tf_op jit(solution)/shard_map/ppermute | solution.py:61
  100.0 34.3 %collective-permute-start.14 = (bf16[160,3584]{1,0:T(8,128)(2,1)}, bf16[160,3584]{1,0:T(8,128)(2,1)S(1)}, u32[]{:S(2)}, u32[]{:S(2)}) collective-permute-start(bf16[160,3584]{1,0:T(8,128)(2,1)} %get-tuple-element.20), channel_id=1, source_target_pairs={{0,16},{16,0},{1,17},{17,1},{2,18},{18,2},{3,19},{19,3},{4,20},{20... | collective-permute-start | bytes 3440648 | tf_op jit(solution)/shard_map/ppermute | solution.py:61
  100.4 9.2 %collective-permute-start.15 = (bf16[160,3584]{1,0:T(8,128)(2,1)}, bf16[160,3584]{1,0:T(8,128)(2,1)S(1)}, u32[]{:S(2)}, u32[]{:S(2)}) collective-permute-start(bf16[160,3584]{1,0:T(8,128)(2,1)} %get-tuple-element.22), channel_id=1, source_target_pairs={{0,16},{16,0},{1,17},{17,1},{2,18},{18,2},{3,19},{19,3},{4,20},{20... | collective-permute-start | bytes 3440648 | tf_op jit(solution)/shard_map/ppermute | solution.py:61
  101.9 5.3 %collective-permute-start.18 = (bf16[16,3584]{1,0:T(8,128)(2,1)S(1)}, bf16[16,3584]{1,0:T(8,128)(2,1)S(1)}, u32[]{:S(2)}, u32[]{:S(2)}) collective-permute-start(bf16[16,3584]{1,0:T(8,128)(2,1)S(1)} %get-tuple-element.48), channel_id=1, source_target_pairs={{0,2},{1,3},{2,0},{3,1},{4,6},{5,7},{6,4},{7,5},{8,10},{9,11},{10,... | collective-permute-start | bytes 344072 | tf_op jit(solution)/shard_map/ppermute | solution.py:95
  102.3 5.0 %collective-permute-start.22 = (bf16[16,3584]{1,0:T(8,128)(2,1)S(1)}, bf16[16,3584]{1,0:T(8,128)(2,1)S(1)}, u32[]{:S(2)}, u32[]{:S(2)}) collective-permute-start(bf16[16,3584]{1,0:T(8,128)(2,1)S(1)} %get-tuple-element.49), channel_id=1, source_target_pairs={{0,1},{1,0},{2,3},{3,2},{4,5},{5,4},{6,7},{7,6},{8,9},{9,8},{10,11... | collective-permute-start | bytes 344072 | tf_op jit(solution)/shard_map/ppermute | solution.py:95
  107.4 2.2 %copy-start.24 = (bf16[160,3584]{1,0:T(8,128)(2,1)S(1)}, bf16[160,3584]{1,0:T(8,128)(2,1)}, u32[]{:S(2)}) copy-start(bf16[160,3584]{1,0:T(8,128)(2,1)} %get-tuple-element.21) | copy-start | bytes 3440644
  107.4 13.9 %collective-permute-start.19 = (bf16[64,3584]{1,0:T(8,128)(2,1)S(1)}, bf16[64,3584]{1,0:T(8,128)(2,1)S(1)}, u32[]{:S(2)}, u32[]{:S(2)}) collective-permute-start(bf16[64,3584]{1,0:T(8,128)(2,1)S(1)} %pad_maximum_fusion.9), channel_id=1, source_target_pairs={{0,1},{1,0},{2,3},{3,2},{4,5},{5,4},{6,7},{7,6},{8,9},{9,8},{10,11... | collective-permute-start | bytes 1376264 | tf_op jit(solution)/shard_map/ppermute | solution.py:95
  108.8 11.4 %collective-permute-start.23 = (bf16[64,3584]{1,0:T(8,128)(2,1)S(1)}, bf16[64,3584]{1,0:T(8,128)(2,1)S(1)}, u32[]{:S(2)}, u32[]{:S(2)}) collective-permute-start(bf16[64,3584]{1,0:T(8,128)(2,1)S(1)} %pad_maximum_fusion.10), channel_id=1, source_target_pairs={{0,2},{1,3},{2,0},{3,1},{4,6},{5,7},{6,4},{7,5},{8,10},{9,11},{10,... | collective-permute-start | bytes 1376264 | tf_op jit(solution)/shard_map/ppermute | solution.py:95
  120.4 12.9 %collective-permute-start.24 = (bf16[80,3584]{1,0:T(8,128)(2,1)S(1)}, bf16[80,3584]{1,0:T(8,128)(2,1)S(1)}, u32[]{:S(2)}, u32[]{:S(2)}) collective-permute-start(bf16[80,3584]{1,0:T(8,128)(2,1)S(1)} %pad_maximum_fusion.6), channel_id=1, source_target_pairs={{0,1},{1,0},{2,3},{3,2},{4,5},{5,4},{6,7},{7,6},{8,9},{9,8},{10,11... | collective-permute-start | bytes 1720328 | tf_op jit(solution)/shard_map/ppermute | solution.py:95
  121.6 12.7 %collective-permute-start.20 = (bf16[80,3584]{1,0:T(8,128)(2,1)S(1)}, bf16[80,3584]{1,0:T(8,128)(2,1)S(1)}, u32[]{:S(2)}, u32[]{:S(2)}) collective-permute-start(bf16[80,3584]{1,0:T(8,128)(2,1)S(1)} %fusion.13), channel_id=1, source_target_pairs={{0,2},{1,3},{2,0},{3,1},{4,6},{5,7},{6,4},{7,5},{8,10},{9,11},{10,... | collective-permute-start | bytes 1720328 | tf_op jit(solution)/shard_map/ppermute | solution.py:95
  123.2 17.8 %collective-permute-start.28 = (bf16[32,3584]{1,0:T(8,128)(2,1)S(1)}, bf16[32,3584]{1,0:T(8,128)(2,1)S(1)}, u32[]{:S(2)}, u32[]{:S(2)}) collective-permute-start(bf16[32,3584]{1,0:T(8,128)(2,1)S(1)} %fusion.2), channel_id=1, source_target_pairs={{0,8},{1,9},{2,10},{3,11},{4,12},{5,13},{6,14},{7,15},{8,0},{9,1},... | collective-permute-start | bytes 688136 | tf_op jit(solution)/shard_map/ppermute | solution.py:95
  133.4 1.3 copy-start.22
  134.8 6.2 %collective-permute-start.25 = (bf16[32,3584]{1,0:T(8,128)(2,1)S(1)}, bf16[32,3584]{1,0:T(8,128)(2,1)S(1)}, u32[]{:S(2)}, u32[]{:S(2)}) collective-permute-start(bf16[32,3584]{1,0:T(8,128)(2,1)S(1)} %pad_maximum_fusion.12), channel_id=1, source_target_pairs={{0,2},{1,3},{2,0},{3,1},{4,6},{5,7},{6,4},{7,5},{8,10},{9,11},{10,... | collective-permute-start | bytes 688136 | tf_op jit(solution)/shard_map/ppermute | solution.py:95
  136.3 4.5 %copy-start.6 = (f32[64,640]{1,0:T(8,128)S(1)}, f32[64,640]{1,0:T(8,128)}, u32[]{:S(2)}) copy-start(f32[64,640]{1,0:T(8,128)} %copy-done.5) | copy-start | bytes 491524
  136.3 6.1 %collective-permute-start.21 = (bf16[32,3584]{1,0:T(8,128)(2,1)S(1)}, bf16[32,3584]{1,0:T(8,128)(2,1)S(1)}, u32[]{:S(2)}, u32[]{:S(2)}) collective-permute-start(bf16[32,3584]{1,0:T(8,128)(2,1)S(1)} %pad_maximum_fusion.11), channel_id=1, source_target_pairs={{0,1},{1,0},{2,3},{3,2},{4,5},{5,4},{6,7},{7,6},{8,9},{9,8},{10,11... | collective-permute-start | bytes 688136 | tf_op jit(solution)/shard_map/ppermute | solution.py:95
  137.3 8.5 %collective-permute-start.26 = (bf16[32,3584]{1,0:T(8,128)(2,1)S(1)}, bf16[32,3584]{1,0:T(8,128)(2,1)S(1)}, u32[]{:S(2)}, u32[]{:S(2)}) collective-permute-start(bf16[32,3584]{1,0:T(8,128)(2,1)S(1)} %get-tuple-element.30), channel_id=1, source_target_pairs={{0,12},{1,13},{2,14},{3,15},{4,0},{5,1},{6,2},{7,3},{8,4},{9,5},{1... | collective-permute-start | bytes 688136 | tf_op jit(solution)/shard_map/ppermute | solution.py:95
  140.7 7.9 %collective-permute-start.27 = (bf16[32,3584]{1,0:T(8,128)(2,1)S(1)}, bf16[32,3584]{1,0:T(8,128)(2,1)S(1)}, u32[]{:S(2)}, u32[]{:S(2)}) collective-permute-start(bf16[32,3584]{1,0:T(8,128)(2,1)S(1)} %get-tuple-element.31), channel_id=1, source_target_pairs={{0,4},{1,5},{2,6},{3,7},{4,8},{5,9},{6,10},{7,11},{8,12},{9,13},{1... | collective-permute-start | bytes 688136 | tf_op jit(solution)/shard_map/ppermute | solution.py:95
  148.8 1.6 %collective-permute-start.29 = (bf16[32,3584]{1,0:T(8,128)(2,1)S(1)}, bf16[32,3584]{1,0:T(8,128)(2,1)S(1)}, u32[]{:S(2)}, u32[]{:S(2)}) collective-permute-start(bf16[32,3584]{1,0:T(8,128)(2,1)S(1)} %add_convert_fusion.1), channel_id=1, source_target_pairs={{0,16},{16,0},{1,17},{17,1},{2,18},{18,2},{3,19},{19,3},{4,20},{20... | collective-permute-start | bytes 688136 | tf_op jit(solution)/shard_map/ppermute | solution.py:61

commit v4 on v3

--- a/solution.py
+++ b/solution.py
@@ -11,73 +11,72 @@
 CAP = 8
 JOIN = 4
 COLS = 512
-VMEM_LIMIT = 51 * 1024 * 1024
+AHEAD = 2
+MORE = 2
+VMEM_LIMIT = 71 * 512 * 1024
 
 softmax_scale = 192.0 ** (-0.5)
 
 
-def attend_kernel(span_ref, queries_ref, cache_ref, out_ref):
+def attend_kernel(request, here_ref, lengths_ref, queries_ref, cache_ref, kept_ref, sent_ref, joined):
     heads, span = queries_ref.shape[0], cache_ref.shape[1]
+    share = heads // 2
+    core = here_ref[0]
     scores = (
         jnp.dot(queries_ref[...], cache_ref[...], preferred_element_type=jnp.float32)
         * softmax_scale
     )
-    usable = lax.broadcasted_iota(jnp.int32, (heads, span), 1) < span_ref[0]
+    positions = core * span + lax.broadcasted_iota(jnp.int32, (heads, span), 1)
+    usable = positions < lengths_ref[request]
     masked = jnp.where(usable, scores, -1e30)
     top = jnp.max(masked, axis=1, keepdims=True)
     weights = jnp.where(usable, jnp.exp(masked - top), 0.0)
     total = jnp.sum(weights, axis=1, keepdims=True)
-    out_ref[:, :LAT] = lax.dot_general(
+    joined[:, :LAT] = lax.dot_general(
         weights.astype(jnp.bfloat16),
         cache_ref[:LAT],
         (((1,), (1,)), ((), ())),
         preferred_element_type=jnp.float32,
     )
     lane = lax.broadcasted_iota(jnp.int32, (heads, 128), 1)
-    out_ref[:, LAT:] = jnp.where(lane == 0, top, total)
-
-
-def attend_part(queries, cache, span):
+    joined[:, LAT:] = jnp.where(lane == 0, top, total)
+    kept_ref[...] = joined[pl.ds(pl.multiple_of(core * share, share), share)]
+    sent_ref[...] = joined[pl.ds(pl.multiple_of((1 - core) * share, share), share)]
+
+
+def attend_part(queries, cache, lengths, request, here):
     heads, depth = queries.shape
+    part = jax.ShapeDtypeStruct((heads // 2, LAT + 128), jnp.float32)
     return pl.pallas_call(
-        attend_kernel,
-        out_shape=jax.ShapeDtypeStruct((heads, LAT + 128), jnp.float32),
-        in_specs=[
-            pl.BlockSpec(memory_space=pltpu.SMEM),
-            pl.BlockSpec(memory_space=pltpu.VMEM),
-            pl.BlockSpec(memory_space=pltpu.VMEM),
-        ],
-        out_specs=pl.BlockSpec(memory_space=pltpu.VMEM),
+        functools.partial(attend_kernel, request),
+        out_shape=(part, part),
+        in_specs=[pl.BlockSpec(memory_space=pltpu.SMEM)] * 2
+        + [pl.BlockSpec(memory_space=pltpu.VMEM)] * 2,
+        out_specs=(pl.BlockSpec(memory_space=pltpu.VMEM),) * 2,
+        scratch_shapes=[pltpu.VMEM((heads, LAT + 128), jnp.float32)],
         compiler_params=pltpu.CompilerParams(vmem_limit_bytes=16 * 1024 * 1024),
         cost_estimate=pl.CostEstimate(
             flops=2 * heads * cache.shape[0] * (depth + LAT),
             bytes_accessed=cache.size * 2,
             transcendentals=heads * cache.shape[0],
         ),
-    )(span, queries, cache.T)
+    )(here, lengths, queries, cache.T)
 
 
 def swap_ctx(x):
     return lax.ppermute(x, "ctx", [(0, 1), (1, 0)])
 
 
-def attend_local(queries, latent_cache, cache_lengths):
-    mine = lax.axis_index("ctx")
-    spans = jnp.clip(
-        cache_lengths - mine * latent_cache.shape[1], 0, latent_cache.shape[1]
-    ).astype(jnp.int32)
-    return jnp.stack(
-        [
-            attend_part(queries[r], latent_cache[r], spans[r : r + 1])
-            for r in range(queries.shape[0])
-        ]
-    )
-
-
-def join_cores(packed):
-    mine, share = lax.axis_index("ctx"), packed.shape[1] // 2
-    kept = lax.dynamic_slice_in_dim(packed, mine * share, share, 1)
-    other = swap_ctx(lax.dynamic_slice_in_dim(packed, (1 - mine) * share, share, 1))
+def attend_local(queries, latent_cache, cache_lengths, here):
+    parts = [
+        attend_part(queries[r], latent_cache[r], cache_lengths, r, here)
+        for r in range(queries.shape[0])
+    ]
+    return tuple(jnp.stack(half) for half in zip(*parts))
+
+
+def join_cores(kept, sent):
+    other = swap_ctx(sent)
     kept_top, other_top = kept[:, :, LAT : LAT + 1], other[:, :, LAT : LAT + 1]
     joined_top = jnp.maximum(kept_top, other_top)
     kept_factor = jnp.exp(kept_top - joined_top)
@@ -115,7 +114,7 @@
     return lax.optimization_barrier((x, other))[0]
 
 
-def gather_rows(rows):
+def gather_rows(rows, meanwhile):
     n = rows.shape[0]
     h = n // 2
     below, above = to_z(rows, 1), to_z(rows, 3)
@@ -123,11 +122,17 @@
     far = to_z(after(rows, below), 2)
     bx = to_x(cat(below, above, own_y[h:]))
     by = to_y(cat(below, above, own_x[:h]))
+    early = swap_ctx(cat(own_x, own_y, below, above))
+    result, done = meanwhile(above)
+    far = far + done
     cx = to_x(cat(far, by[h:n], by[n + h : 2 * n]))
     cy = to_y(cat(far, bx[:h], bx[n : n + h]))
+    middle = swap_ctx(cat(bx, by, far))
     dx = to_x(cy[h:n])
     dy = to_y(cx[:h])
-    return [rows, own_x, own_y, below, above, bx, by, far, cx, cy, dx, dy]
+    late = swap_ctx(cat(cx, cy))
+    own = [rows, own_x, own_y, below, above, bx, by, far, cx, cy, dx, dy]
+    return own, [early, middle, late, swap_ctx(cat(dx, dy))], result
 
 
 TAKEN = (
@@ -139,7 +144,7 @@
 OTHER = (
     ((0, 0, 2), (1, 0, 2), (1, 2, 4), (2, 9, 10), (2, 4, 5)),
     ((1, 4, 6), (2, 0, 2), (2, 5, 7), (3, 6, 7), (3, 2, 3)),
-    ((2, 10, 12), (3, 0, 2), (3, 4, 6), (3, 9, 10), (3, 8, 9)),
+    ((2, 10, 12), (3, 0, 2), (3, 4, 6), (4, 1, 2), (4, 0, 1)),
     ((1, 6, 8), (2, 2, 4), (2, 7, 9), (3, 7, 8), (3, 3, 4)),
 )
 PLACES = (
@@ -149,6 +154,7 @@
     ((0, 8, 10), (1, 2, 4), (1, 7, 9), (2, 9, 10), (2, 5, 6)),
 )
 BUNDLES = (10, 10, 10, 2)
+ORDER = (2, 1, 3, 0)
 
 
 def scatter_sums(kept, came):
@@ -195,32 +201,36 @@
     above = wide(to_z(narrow(share(0, 8, 10) + bx[n : 2 * n] + by[n : 2 * n]), 1))
     own_x = wide(to_x(narrow(share(0, 2, 3) + by[2 * n :], share(0, 3, 4))))
     own_y = wide(to_y(narrow(share(0, 4, 5), share(0, 5, 6) + bx[2 * n :])))
-    return narrow(share(0, 0, 2) + own_x + own_y + below + above + far)
-
-
-def expert_kernel(plan, first_ref, *refs):
+    others = lax.optimization_barrier(share(0, 0, 2) + below + above + far)
+    return narrow(others + own_x + own_y)
+
+
+def expert_kernel(plan, here_ref, *refs):
     planes, group_count, expert_count, width, top = plan
-    counts = (12, 4, 3) if planes else (1, 1, 3)
-    counts += (4, 4) if planes else (1, 1)
+    counts = (12, 5, 3, 3) if planes else (1, 1, 3, 3)
+    counts += (4, 4, 3) if planes else (1, 1, 3)
     parts, done = [], 0
     for count in counts:
         parts.append(refs[done : done + count])
         done += count
-    own, other, (gate_hbm, up_hbm, down_hbm), own_out, other_out = parts
-    slots, select, scales, gate_buf, up_buf, down_buf, staged, sems, in_sems, out_sems = refs[done:]
+    own, other, (gate_hbm, up_hbm, down_hbm), _, own_out, other_out = parts[:6]
+    gate_buf, up_buf, down_buf = parts[6]
+    slots, select, scales, staged, sems, in_sems, out_sems, *room = refs[done:]
+    sets = [[(ref, k) for ref in (gate_buf, up_buf, down_buf)] for k in range(gate_buf.shape[0])]
+    if room:
+        sets += [[(ref, k) for ref in room] for k in range(room[0].shape[0])]
     lanes = select.shape[2]
     half = lanes // 2
     piece = half // JOIN
     block = JOIN * CAP
     unit = piece // 2
-    depth = gate_buf.shape[0]
-
-    def loads(e):
-        slot = lax.rem(e, depth)
+    ahead, depth = gate_buf.shape[0], len(sets)
+
+    def loads(e, slot):
         return [
-            pltpu.make_async_copy(hbm.at[e], buf.at[slot], sems.at[k, slot])
-            for k, (hbm, buf) in enumerate(
-                ((gate_hbm, gate_buf), (up_hbm, up_buf), (down_hbm, down_buf))
+            pltpu.make_async_copy(hbm.at[e], ref.at[k], sems.at[i, slot])
+            for i, (hbm, (ref, k)) in enumerate(
+                zip((gate_hbm, up_hbm, down_hbm), sets[slot], strict=True)
             )
         ]
 
@@ -249,7 +259,7 @@
                 copies.append(
                     pltpu.make_async_copy(
                         side[b].at[pl.ds(f * unit, rows)],
-                        staged.at[group, pl.ds(at, rows)],
+                        staged.at[stage_of(group), pl.ds(at, rows)],
                         in_sems.at[len(copies) + 10 * group],
                     )
                 )
@@ -272,7 +282,7 @@
                 rows = (t - f) * unit
                 copies.append(
                     pltpu.make_async_copy(
-                        staged.at[group, pl.ds(at, rows), pl.ds(0, width)],
+                        staged.at[stage_of(group), pl.ds(at, rows), pl.ds(0, width)],
                         side[b].at[pl.ds(f * unit, rows)],
                         out_sems.at[len(copies) + 10 * group],
                     )
@@ -281,7 +291,7 @@
         return copies
 
     def stage_of(group):
-        return group if planes else 0
+        return ORDER.index(group) % 2 if planes else 0
 
     def sort_rows(group):
         copies = takes(group)
@@ -291,7 +301,7 @@
         for copy in copies:
             copy.wait()
         rows_ref = staged.at[stage_of(group)]
-        first = first_ref[0]
+        first = here_ref[1]
         named = rows_ref[:, width:].astype(jnp.float32).T
         ids = named[:top]
         gates = named[top : 2 * top] + named[2 * top : 3 * top] + named[3 * top : 4 * top]
@@ -330,26 +340,38 @@
             for e in range(expert_count):
                 slots[e, at, columns] = sorted_rows[e * block : (e + 1) * block]
 
-    def run_expert(e):
-        slot = lax.rem(e, depth)
-        gate_copy, up_copy, down_copy = loads(e)
+    def run_expert(e, slot):
+        copies = loads(e, slot)
+        (gate_buf, k), (up_buf, _), (down_buf, _) = sets[slot]
+
+        def arrived(copy):
+            pl.when(e >= ahead)(copy.wait)
+
+        def reload(i):
+            @pl.when(e + depth < expert_count)
+            def _():
+                loads(e + depth, slot)[i].start()
+
         rows = slots[e]
-        gate_copy.wait()
-        gate = jnp.dot(rows, gate_buf[slot], preferred_element_type=jnp.float32)
-        up_copy.wait()
-        up = jnp.dot(rows, up_buf[slot], preferred_element_type=jnp.float32)
+        arrived(copies[0])
+        gate = jnp.dot(rows, gate_buf[k], preferred_element_type=jnp.float32)
+        reload(0)
+        arrived(copies[1])
+        up = jnp.dot(rows, up_buf[k], preferred_element_type=jnp.float32)
+        reload(1)
         hidden = (gate / (1.0 + jnp.exp(-gate))) * up * scales[e][:, :1]
         hidden = hidden.astype(jnp.bfloat16)
-        down_copy.wait()
+        arrived(copies[2])
         for c in range(0, width, COLS):
             slots[e, :, c : c + COLS] = jnp.dot(
-                hidden, down_buf[slot, :, c : c + COLS], preferred_element_type=jnp.float32
+                hidden, down_buf[k, :, c : c + COLS], preferred_element_type=jnp.float32
             ).astype(jnp.bfloat16)
 
-        @pl.when(e + depth < expert_count)
-        def _():
-            for copy in loads(e + depth):
-                copy.start()
+        reload(2)
+
+    def run_experts(first):
+        for slot in range(depth):
+            run_expert(first * depth + slot, slot)
 
     def sum_rows(group):
         chosen = select[group]
@@ -370,71 +392,122 @@
     def each(count, work):
         lax.fori_loop(0, count, lambda i, _: (work(i), 0)[1], 0)
 
+    def start(copies):
+        for copy in copies:
+            copy.start()
+
+    def wait(copies):
+        for copy in copies:
+            copy.wait()
+
     if planes:
-        for group in range(group_count):
-            for copy in takes(group):
-                copy.start()
-    for e in range(min(depth, expert_count)):
-        for copy in loads(e):
-            copy.start()
+        for group in ORDER[:2]:
+            start(takes(group))
+    for e in range(ahead, depth):
+        start(loads(e, e))
     if planes:
-        for group in range(group_count):
+        for place, group in enumerate(ORDER):
             sort_rows(group)
+            if place + 2 < group_count:
+                start(takes(ORDER[place + 2]))
     else:
         each(group_count, sort_rows)
-    each(expert_count, run_expert)
+    each(expert_count // depth, run_experts)
     if planes:
-        for group in (2, 1, 3, 0):
+        for place, group in enumerate(ORDER):
+            if place >= 2:
+                wait(puts(ORDER[place - 2]))
             sum_rows(group)
-        for group in (2, 1, 3, 0):
-            for copy in puts(group):
-                copy.wait()
+        for group in ORDER[2:]:
+            wait(puts(group))
     else:
         each(group_count, sum_rows)
 
 
-def expert_sums(own, other, top, owners, first, gate_weight, up_weight, down_weight):
+def ahead_kernel(gate_hbm, up_hbm, down_hbm, _, __, gate_out, up_out, down_out, done_out, sems):
+    copies = [
+        pltpu.make_async_copy(hbm.at[e], out.at[e], sems.at[k, e])
+        for e in range(gate_out.shape[0])
+        for k, (hbm, out) in enumerate(
+            ((gate_hbm, gate_out), (up_hbm, up_out), (down_hbm, down_out))
+        )
+    ]
+    for copy in copies:
+        copy.start()
+    done_out[...] = jnp.zeros_like(done_out)
+    for copy in copies:
+        copy.wait()
+
+
+def weights_ahead(gate_weight, up_weight, down_weight, *follows):
+    depth = min(AHEAD, gate_weight.shape[0])
+    assert gate_weight.shape[0] % depth == 0
+    weights = [gate_weight, up_weight, down_weight]
+    return pl.pallas_call(
+        ahead_kernel,
+        out_shape=[pltpu.VMEM((depth,) + w.shape[1:], w.dtype) for w in weights]
+        + [jax.ShapeDtypeStruct(follows[0].shape, follows[0].dtype)],
+        in_specs=[pl.BlockSpec(memory_space=pl.ANY)] * 5,
+        out_specs=[pl.BlockSpec(memory_space=pltpu.VMEM)] * 4,
+        scratch_shapes=[pltpu.SemaphoreType.DMA((3, depth))],
+        compiler_params=pltpu.CompilerParams(vmem_limit_bytes=VMEM_LIMIT),
+        cost_estimate=pl.CostEstimate(
+            flops=0,
+            bytes_accessed=sum(2 * depth * w[0].size for w in weights),
+            transcendentals=0,
+        ),
+    )(*weights, *follows)
+
+
+def expert_sums(own, other, top, owners, here, gate_weight, up_weight, down_weight, ahead):
     expert_count, width, hidden = gate_weight.shape
     planes = plane_of(owners)
     group_count = owners // JOIN
     half = sum(x.shape[0] for x in own) // group_count
     slot_rows = group_count * JOIN * CAP
-    depth = min(3, expert_count)
+    more = MORE if expert_count % (AHEAD + MORE) == 0 else 0
+    depth = ahead[0].shape[0] + more
+    ahead = [pltpu.with_memory_space_constraint(w, pltpu.VMEM) for w in ahead]
     if planes:
         out_rows = [u * half // 8 for u in BUNDLES] * 2
     else:
         out_rows = [own[0].shape[0]] * 2
-    stages, copies = (group_count, 10 * group_count) if planes else (1, 2)
+    stages, copies = (2, 10 * group_count) if planes else (1, 2)
     weight_bytes = 3 * expert_count * width * hidden * 2
     sums = pl.pallas_call(
         functools.partial(expert_kernel, (planes, group_count, expert_count, width, top)),
-        out_shape=[jax.ShapeDtypeStruct((r, width), jnp.bfloat16) for r in out_rows],
+        out_shape=[jax.ShapeDtypeStruct((r, width), jnp.bfloat16) for r in out_rows]
+        + [pltpu.VMEM(w.shape, w.dtype) for w in ahead],
+        input_output_aliases={
+            1 + len(own) + len(other) + 3 + k: len(out_rows) + k for k in range(3)
+        },
         in_specs=[pl.BlockSpec(memory_space=pltpu.SMEM)]
-        + [pl.BlockSpec(memory_space=pl.ANY)] * (len(own) + len(other) + 3),
-        out_specs=[pl.BlockSpec(memory_space=pl.ANY)] * len(out_rows),
+        + [pl.BlockSpec(memory_space=pl.ANY)] * (len(own) + len(other) + 3)
+        + [pl.BlockSpec(memory_space=pltpu.VMEM)] * 3,
+        out_specs=[pl.BlockSpec(memory_space=pl.ANY)] * len(out_rows)
+        + [pl.BlockSpec(memory_space=pltpu.VMEM)] * 3,
         scratch_shapes=[
             pltpu.VMEM((expert_count, slot_rows, width), jnp.bfloat16),
             pltpu.VMEM((group_count, expert_count * JOIN * CAP, 2 * half), jnp.bfloat16),
             pltpu.VMEM((expert_count, slot_rows, 128), jnp.float32),
-            pltpu.VMEM((depth, width, hidden), jnp.bfloat16),
-            pltpu.VMEM((depth, width, hidden), jnp.bfloat16),
-            pltpu.VMEM((depth, hidden, width), jnp.bfloat16),
             pltpu.VMEM((stages, 2 * half, own[0].shape[1]), jnp.bfloat16),
             pltpu.SemaphoreType.DMA((3, depth)),
             pltpu.SemaphoreType.DMA((copies,)),
             pltpu.SemaphoreType.DMA((copies,)),
-        ],
+        ]
+        + [pltpu.VMEM((more,) + w.shape[1:], w.dtype) for w in ahead if more],
         compiler_params=pltpu.CompilerParams(vmem_limit_bytes=VMEM_LIMIT),
         cost_estimate=pl.CostEstimate(
             flops=slot_rows * weight_bytes,
             bytes_accessed=weight_bytes,
             transcendentals=expert_count * slot_rows * hidden,
         ),
-    )(first, *own, *other, gate_weight, up_weight, down_weight)
-    return sums[: len(sums) // 2], sums[len(sums) // 2 :]
-
-
-def ask_kernel(core_ref, rows_hbm, routes_hbm, gates_hbm, own_ref, other_ref, routes, gates, sems):
+    )(here, *own, *other, gate_weight, up_weight, down_weight, *ahead)
+    count = len(out_rows) // 2
+    return sums[:count], sums[count : 2 * count]
+
+
+def ask_kernel(here_ref, rows_hbm, routes_hbm, gates_hbm, own_ref, other_ref, routes, gates, asks, sems):
     width = rows_hbm.shape[1]
     half = rows_hbm.shape[0] // 2
     small = [
@@ -448,7 +521,7 @@
             sems.at[2 + k],
         )
         for k, (from_half, ref) in enumerate(
-            ((core_ref[0], own_ref), (1 - core_ref[0], other_ref))
+            ((here_ref[0], own_ref), (1 - here_ref[0], other_ref))
         )
     ]
     for copy in small + large:
@@ -465,14 +538,16 @@
     asked = jnp.concatenate(terms + [jnp.zeros((blank, 2 * half), jnp.float32)], axis=0).T
     asked = asked.astype(jnp.bfloat16)
     first, last = asked[:half], asked[half:]
-    mine = core_ref[0] == 0
+    mine = here_ref[0] == 0
     own_ref[:, width:] = jnp.where(mine, first, last)
-    other_ref[:, width:] = jnp.where(mine, last, first)
-    for copy in large:
+    asks[...] = jnp.where(mine, last, first)
+    last = pltpu.make_async_copy(asks, other_ref.at[:, pl.ds(width, 128)], sems.at[4])
+    last.start()
+    for copy in large + [last]:
         copy.wait()
 
 
-def ask(moe_rows, routes, route_gates, core):
+def ask(moe_rows, routes, route_gates, here):
     rows, width = moe_rows.shape
     half = jax.ShapeDtypeStruct((rows // 2, width + 128), jnp.bfloat16)
     return pl.pallas_call(
@@ -480,32 +555,58 @@
         out_shape=(half, half),
         in_specs=[pl.BlockSpec(memory_space=pltpu.SMEM)]
         + [pl.BlockSpec(memory_space=pl.ANY)] * 3,
-        out_specs=[pl.BlockSpec(memory_space=pltpu.VMEM)] * 2,
+        out_specs=[pl.BlockSpec(memory_space=pltpu.VMEM), pl.BlockSpec(memory_space=pl.ANY)],
         scratch_shapes=[
             pltpu.VMEM(routes.shape[::-1], jnp.int32),
             pltpu.VMEM(routes.shape[::-1], jnp.float32),
-            pltpu.SemaphoreType.DMA((4,)),
+            pltpu.VMEM((rows // 2, 128), jnp.bfloat16),
+            pltpu.SemaphoreType.DMA((5,)),
         ],
         compiler_params=pltpu.CompilerParams(vmem_limit_bytes=4 * 1024 * 1024),
-    )(core.astype(jnp.int32).reshape(1), moe_rows, routes.T, route_gates.T)
-
-
-def route_rows(moe_rows, routes, route_gates, gate_weight, up_weight, down_weight, packed):
+    )(
+        here,
+        *(pltpu.with_memory_space_constraint(x, pltpu.HBM) for x in (moe_rows, routes.T, route_gates.T)),
+    )
+
+
+def order_kernel(here_ref, own_ref, other_ref, out_ref):
+    half = own_ref.shape[0]
+    out_ref[pl.ds(pl.multiple_of(here_ref[0] * half, half), half)] = own_ref[...]
+    out_ref[pl.ds(pl.multiple_of((1 - here_ref[0]) * half, half), half)] = other_ref[...]
+
+
+def in_order(own, other, here):
+    return pl.pallas_call(
+        order_kernel,
+        out_shape=jax.ShapeDtypeStruct((2 * own.shape[0], own.shape[1]), own.dtype),
+        in_specs=[pl.BlockSpec(memory_space=pltpu.SMEM)]
+        + [pl.BlockSpec(memory_space=pltpu.VMEM)] * 2,
+        out_specs=pl.BlockSpec(memory_space=pltpu.VMEM),
+        compiler_params=pltpu.CompilerParams(vmem_limit_bytes=4 * 1024 * 1024),
+    )(here, own, other)
+
+
+def route_rows(moe_rows, routes, route_gates, gate_weight, up_weight, down_weight, attend):
     owners = lax.axis_size("ep")
     top = routes.shape[1]
     core, chip = lax.axis_index("ctx"), lax.axis_index("ep")
-    first = (chip * gate_weight.shape[0]).astype(jnp.int32).reshape(1)
-
-    mine, theirs = ask(moe_rows, routes, route_gates, core)
+    here = jnp.stack([core, chip * gate_weight.shape[0]]).astype(jnp.int32)
+
+    def meanwhile(follows):
+        packed = attend(here)
+        *ahead, done = weights_ahead(gate_weight, up_weight, down_weight, follows, packed[0])
+        return (ahead, packed), done
+
+    mine, theirs = ask(moe_rows, routes, route_gates, here)
     if plane_of(owners):
-        own = gather_rows(mine)
-        other = [theirs] + [swap_ctx(cat(*x)) for x in (own[1:5], own[5:8], own[8:])]
+        own, other, (ahead, packed) = gather_rows(mine, meanwhile)
+        other = [theirs] + other
     else:
         own = [lax.all_gather(mine, "ep", tiled=True)]
         other = [swap_ctx(own[0])]
-    first, packed = lax.optimization_barrier((first, packed))
+        ahead, packed = meanwhile(mine)[0]
     own_sums, other_sums = expert_sums(
-        own, other, top, owners, first, gate_weight, up_weight, down_weight
+        own, other, top, owners, here, gate_weight, up_weight, down_weight, ahead
     )
     came = [None] * len(own_sums)
     for b in reversed(range(len(own_sums))):
@@ -515,8 +616,7 @@
     else:
         own_final = lax.psum_scatter(own_sums[0] + came[0], "ep", scatter_dimension=0, tiled=True)
     other_final = swap_ctx(own_final)
-    routed = jnp.where(core == 0, cat(own_final, other_final), cat(other_final, own_final))
-    return routed, packed
+    return in_order(own_final, other_final, here), packed
 
 
 def body(
@@ -530,11 +630,11 @@
     latent_cache,
     cache_lengths,
 ):
-    packed = attend_local(queries, latent_cache, cache_lengths)
+    attend = functools.partial(attend_local, queries, latent_cache, cache_lengths)
     routed_output, packed = route_rows(
-        moe_rows, routes, route_gates, gate_weight, up_weight, down_weight, packed
-    )
-    return (routed_output, join_cores(packed))
+        moe_rows, routes, route_gates, gate_weight, up_weight, down_weight, attend
+    )
+    return (routed_output, join_cores(*packed))
 
 
 def solution(mesh):

time: 152 us -> 147 us (0.967)
  waiting for transfers between devices: 67 us -> 55.8 us
  Pallas kernels: 40 us -> 46.3 us
  starting transfers between devices: 28.9 us -> 33 us
  other arithmetic: 8.13 us -> 6.05 us
    ppermute x22, waiting for transfers between devices: 65 us -> 52.2 us  [send(): return lax.ppermute(x, 'ep', [(i, target(i)) for i in range(count)])]
    pallas_call x1 -> x3, Pallas kernels: 1.37 us -> 11.4 us  [the longest x1 8.09 us: weights_ahead(): pl.pallas_call(ahead_kernel, out_shape=[pltpu.VMEM((depth,) + w.shape[1:]...]
    pallas_call x1, Pallas kernels: 38.4 us -> 33.3 us  [expert_sums(): pl.pallas_call(functools.partial(expert_kernel, (planes, group_count, exp...]
    ppermute x22, starting transfers between devices: 27.1 us -> 30.6 us  [send(): return lax.ppermute(x, 'ep', [(i, target(i)) for i in range(count)])]
    concatenate x11 -> x12, other arithmetic: 3.88 us -> 0.62 us  [cat(): return jnp.concatenate(pieces, axis=0)]
    ppermute x9 -> x10, waiting for transfers between devices: 1.97 us -> 3.57 us  [swap_ctx(): return lax.ppermute(x, 'ctx', [(0, 1), (1, 0)])]
    unnamed x50 -> x54, local copies, waits for them, and re-layouts: 4.27 us -> 3.66 us
  transfers between devices with their start and end apart: 31 -> 32, of which waited for: 20 -> 19; matrix products, arithmetic and copies ran while one was open for 5% -> 4% of each run, Pallas kernels for 1% -> 29%
where the time goes in v4:
time: 147 us
  waiting for transfers between devices  55.8 us (38%)
  Pallas kernels  46.3 us (31%)
  starting transfers between devices  33 us (22%)
  other arithmetic  6.05 us (4%)
  local copies, waits for them, and re-layouts  3.91 us (3%)
  between operations  1.79 us (1%)
    ppermute x22, waiting for transfers between devices, send(): return lax.ppermute(x, 'ep', [(i, target(i)) for i in range(count)])  52.2 us
    pallas_call x1, Pallas kernels, expert_sums(): pl.pallas_call(functools.partial(expert_kernel, (planes, group_count, exp...  33.3 us
    ppermute x22, starting transfers between devices, send(): return lax.ppermute(x, 'ep', [(i, target(i)) for i in range(count)])  30.6 us
    pallas_call x1, Pallas kernels, weights_ahead(): pl.pallas_call(ahead_kernel, out_shape=[pltpu.VMEM((depth,) + w.shape[1:]...  8.09 us
    unnamed x54, local copies, waits for them, and re-layouts  3.66 us
    ppermute x10, waiting for transfers between devices, swap_ctx(): return lax.ppermute(x, 'ctx', [(0, 1), (1, 0)])  3.57 us
  transfers between devices with their start and end apart: 32, of which 19 were waited for; matrix products, arithmetic and copies ran while one was open for 4% of the time, Pallas kernels for 29%

profile of v4, /device:TPU:0, one launch (start us, length us, event | category | flops | bytes accessed | tf_op | source)
XLA Modules:
  0.0 146.9 jit_solution(13621490394712189387)
XLA Ops:
  0.7 1.7 %shard_map.104 = (bf16[32,3712]{1,0:T(8,128)(2,1)S(1)}, bf16[32,3712]{1,0:T(8,128)(2,1)S(1)}) custom-call(s32[2]{0:T(128)S(1)} %pad_add_fusion.here_ref, bf16[64,3584]{1,0:T(8,128)(2,1)} %rows_hbm.1, s32[8,64]{1,0:T(8,128)} %bitcast.17, f32[8,64]{1,0:T(8,128)} %bitcast.18), custom_call_target="tpu_custom_call" | custom-call | tf_op jit(solution)/shard_map/pallas_call | solution.py:553
  2.4 0.7 copy-done.4
  3.1 3.0 %collective-permute-start.1 = (bf16[32,3712]{1,0:T(8,128)(2,1)S(1)}, bf16[32,3712]{1,0:T(8,128)(2,1)S(1)}, u32[]{:S(2)}, u32[]{:S(2)}) collective-permute-start(bf16[32,3712]{1,0:T(8,128)(2,1)S(1)} %get-tuple-element.20.refs_0_), channel_id=1, source_target_pairs={{0,2},{1,3},{2,0},{3,1},{4,6},{5,7},{6,4},{7,5},{8,10},{9,11},{10,... | collective-permute-start | bytes 712712 | tf_op jit(solution)/shard_map/ppermute | solution.py:94
  6.1 1.5 %collective-permute-start = (bf16[32,3712]{1,0:T(8,128)(2,1)S(1)}, bf16[32,3712]{1,0:T(8,128)(2,1)S(1)}, u32[]{:S(2)}, u32[]{:S(2)}) collective-permute-start(bf16[32,3712]{1,0:T(8,128)(2,1)S(1)} %get-tuple-element.20.refs_0_), channel_id=1, source_target_pairs={{0,1},{1,0},{2,3},{3,2},{4,5},{5,4},{6,7},{7,6},{8,9},{9,8},{10,11... | collective-permute-start | bytes 712712 | tf_op jit(solution)/shard_map/ppermute | solution.py:94
  7.5 3.6 %collective-permute-start.3 = (bf16[32,3712]{1,0:T(8,128)(2,1)S(1)}, bf16[32,3712]{1,0:T(8,128)(2,1)S(1)}, u32[]{:S(2)}, u32[]{:S(2)}) collective-permute-start(bf16[32,3712]{1,0:T(8,128)(2,1)S(1)} %get-tuple-element.20.refs_0_), channel_id=1, source_target_pairs={{0,12},{1,13},{2,14},{3,15},{4,0},{5,1},{6,2},{7,3},{8,4},{9,5},{1... | collective-permute-start | bytes 712712 | tf_op jit(solution)/shard_map/ppermute | solution.py:94
  11.2 0.7 collective-permute-done.1.refs_2_
  11.8 1.4 collective-permute-done.refs_1_
  13.3 4.1 %collective-permute-done.3._.refs_4_ = bf16[32,3712]{1,0:T(8,128)(2,1)S(1)} collective-permute-done((bf16[32,3712]{1,0:T(8,128)(2,1)S(1)}, bf16[32,3712]{1,0:T(8,128)(2,1)S(1)}, u32[]{:S(2)}, u32[]{:S(2)}) %collective-permute-start.3) | collective-permute-done | bytes 237600 | tf_op jit(solution)/shard_map/ppermute | solution.py:94
  17.4 4.2 %collective-permute-done.2.refs_3_ = bf16[32,3712]{1,0:T(8,128)(2,1)S(1)} collective-permute-done((bf16[32,3712]{1,0:T(8,128)(2,1)S(1)}, bf16[32,3712]{1,0:T(8,128)(2,1)S(1)}, u32[]{:S(2)}, u32[]{:S(2)}) %collective-permute-start.2) | collective-permute-done | bytes 237600 | tf_op jit(solution)/shard_map/ppermute | solution.py:94
  21.7 0.6 collective-permute-start.5
  22.3 0.7 collective-permute-start.6
  23.7 1.9 %shard_map.105 = (f32[32,640]{1,0:T(8,128)S(1)}, f32[32,640]{1,0:T(8,128)S(1)}) custom-call(s32[2]{0:T(128)S(1)} %pad_add_fusion.here_ref, s32[1]{0:T(128)S(6)} %copy.21.lengths_ref, bf16[64,576]{1,0:T(8,128)(2,1)S(1)} %bitcast.15, bf16[576,2048]{1,0:T(8,128)(2,1)S(1)} %bitcast.12), custom_call_target="tpu_custom_call" | custom-call | flops 285212672 | bytes 2359296 | tf_op jit(solution)/shard_map/pallas_call | solution.py:50
  25.7 0.6 copy-done.1
  26.3 0.5 collective-permute-start.4
  26.8 8.1 %shard_map.106 = (bf16[2,3584,512]{2,1,0:T(8,128)(2,1)S(1)}, bf16[2,3584,512]{2,1,0:T(8,128)(2,1)S(1)}, bf16[2,512,3584]{2,1,0:T(8,128)(2,1)S(1)}, bf16[32,3712]{1,0:T(8,128)(2,1)}) custom-call(bf16[8,3584,512]{2,1,0:T(8,128)(2,1)} %refs_17_.1, bf16[8,3584,512]{2,1,0:T(8,128)(2,1)} %refs_18_.1, bf16[8,512,3584]{2,1,0:T(8,128)(2,1)} %refs_19_.1, ...), custom_call_target="tpu_custom_call" | custom-call | bytes 22020096 | tf_op jit(solution)/shard_map/pallas_call | solution.py:446
  34.9 1.0 add.135.refs_7_
  36.0 3.0 %collective-permute-done.4.refs_5_ = bf16[80,3712]{1,0:T(8,128)(2,1)S(1)} collective-permute-done((bf16[80,3712]{1,0:T(8,128)(2,1)S(1)}, bf16[80,3712]{1,0:T(8,128)(2,1)S(1)}, u32[]{:S(2)}, u32[]{:S(2)}) %collective-permute-start.4) | collective-permute-done | bytes 593952 | tf_op jit(solution)/shard_map/ppermute | solution.py:94
  39.0 2.1 %collective-permute-start.8 = (bf16[64,3712]{1,0:T(8,128)(2,1)S(1)}, bf16[64,3712]{1,0:T(8,128)(2,1)S(1)}, u32[]{:S(2)}, u32[]{:S(2)}) collective-permute-start(bf16[64,3712]{1,0:T(8,128)(2,1)S(1)} %get-tuple-element.58), channel_id=1, source_target_pairs={{0,2},{1,3},{2,0},{3,1},{4,6},{5,7},{6,4},{7,5},{8,10},{9,11},{10,... | collective-permute-start | bytes 1425416 | tf_op jit(solution)/shard_map/ppermute | solution.py:94
  41.2 0.5 collective-permute-start.7
  41.9 0.2 copy-done.9
  42.2 0.4 collective-permute-start.11
  42.6 5.7 %collective-permute-done.8.refs_9_ = bf16[64,3712]{1,0:T(8,128)(2,1)S(1)} collective-permute-done((bf16[64,3712]{1,0:T(8,128)(2,1)S(1)}, bf16[64,3712]{1,0:T(8,128)(2,1)S(1)}, u32[]{:S(2)}, u32[]{:S(2)}) %collective-permute-start.8) | collective-permute-done | bytes 475168 | tf_op jit(solution)/shard_map/ppermute | solution.py:94
  48.3 1.5 %collective-permute-done.7.refs_8_ = bf16[64,3712]{1,0:T(8,128)(2,1)S(1)} collective-permute-done((bf16[64,3712]{1,0:T(8,128)(2,1)S(1)}, bf16[64,3712]{1,0:T(8,128)(2,1)S(1)}, u32[]{:S(2)}, u32[]{:S(2)}) %collective-permute-start.7) | collective-permute-done | bytes 475168 | tf_op jit(solution)/shard_map/ppermute | solution.py:94
  50.0 0.6 collective-permute-start.9
  50.6 0.9 collective-permute-start.10
  51.5 4.2 %collective-permute-done.9.refs_10_ = bf16[16,3712]{1,0:T(8,128)(2,1)S(1)} collective-permute-done((bf16[16,3712]{1,0:T(8,128)(2,1)S(1)}, bf16[16,3712]{1,0:T(8,128)(2,1)S(1)}, u32[]{:S(2)}, u32[]{:S(2)}) %collective-permute-start.9) | collective-permute-done | bytes 118816 | tf_op jit(solution)/shard_map/ppermute | solution.py:94
  55.7 0.3 collective-permute-done.10.refs_11_
  56.1 0.5 collective-permute-start.31
  56.6 1.0 collective-permute-done.14.refs_16_
  57.7 0.6 copy-done.26
  58.3 0.3 copy-done.23
  58.6 0.5 copy-done.18
  59.1 33.3 %shard_map.107 = (bf16[160,3584]{1,0:T(8,128)(2,1)}, bf16[160,3584]{1,0:T(8,128)(2,1)}, bf16[160,3584]{1,0:T(8,128)(2,1)}, bf16[32,3584]{1,0:T(8,128)(2,1)}, bf1...) custom-call(s32[2]{0:T(128)} %copy-done.6, ...), custom_call_target="tpu_custom_call", output_to_operand_aliasing={{8}: (21, {}), {9}: (22, {}), {10}: (23, {})} | custom-call | flops 11274289152 | bytes 88080384 | tf_op jit(solution)/shard_map/pallas_call | solution.py:477
  92.4 0.2 collective-permute-start.17
  92.8 0.4 collective-permute-start.18
  93.3 0.2 collective-permute-start.15
  93.5 0.4 collective-permute-start.16
  93.8 2.0 %collective-permute-done.18 = bf16[32,3584]{1,0:T(8,128)(2,1)S(1)} collective-permute-done((bf16[32,3584]{1,0:T(8,128)(2,1)}, bf16[32,3584]{1,0:T(8,128)(2,1)S(1)}, u32[]{:S(2)}, u32[]{:S(2)}) %collective-permute-start.18) | collective-permute-done | bytes 229408 | tf_op jit(solution)/shard_map/ppermute | solution.py:67
  95.8 1.0 add_convert_fusion.9
  96.8 0.9 collective-permute-start.22
  97.7 1.5 %collective-permute-start.19 = (bf16[16,3584]{1,0:T(8,128)(2,1)S(1)}, bf16[16,3584]{1,0:T(8,128)(2,1)S(1)}, u32[]{:S(2)}, u32[]{:S(2)}) collective-permute-start(bf16[16,3584]{1,0:T(8,128)(2,1)S(1)} %get-tuple-element.57), channel_id=1, source_target_pairs={{0,1},{1,0},{2,3},{3,2},{4,5},{5,4},{6,7},{7,6},{8,9},{9,8},{10,11... | collective-permute-start | bytes 344072 | tf_op jit(solution)/shard_map/ppermute | solution.py:94
  99.2 1.1 add_convert_fusion
  100.3 1.8 %collective-permute-done.22 = bf16[16,3584]{1,0:T(8,128)(2,1)S(1)} collective-permute-done((bf16[16,3584]{1,0:T(8,128)(2,1)S(1)}, bf16[16,3584]{1,0:T(8,128)(2,1)S(1)}, u32[]{:S(2)}, u32[]{:S(2)}) %collective-permute-start.22) | collective-permute-done | bytes 114720 | tf_op jit(solution)/shard_map/ppermute | solution.py:94
  102.1 0.6 collective-permute-done.19
  102.8 1.5 %collective-permute-start.23 = (bf16[64,3584]{1,0:T(8,128)(2,1)S(1)}, bf16[64,3584]{1,0:T(8,128)(2,1)S(1)}, u32[]{:S(2)}, u32[]{:S(2)}) collective-permute-start(bf16[64,3584]{1,0:T(8,128)(2,1)S(1)} %pad_maximum_fusion.10), channel_id=1, source_target_pairs={{0,1},{1,0},{2,3},{3,2},{4,5},{5,4},{6,7},{7,6},{8,9},{9,8},{10,11... | collective-permute-start | bytes 1376264 | tf_op jit(solution)/shard_map/ppermute | solution.py:94
  104.5 1.3 collective-permute-start.20
  105.8 9.8 %collective-permute-done.20 = bf16[64,3584]{1,0:T(8,128)(2,1)S(1)} collective-permute-done((bf16[64,3584]{1,0:T(8,128)(2,1)S(1)}, bf16[64,3584]{1,0:T(8,128)(2,1)S(1)}, u32[]{:S(2)}, u32[]{:S(2)}) %collective-permute-start.20) | collective-permute-done | bytes 458784 | tf_op jit(solution)/shard_map/ppermute | solution.py:94
  115.9 0.6 collective-permute-start.21
  116.7 1.3 collective-permute-start.24
  118.1 2.9 %collective-permute-start.27 = (bf16[32,3584]{1,0:T(8,128)(2,1)S(1)}, bf16[32,3584]{1,0:T(8,128)(2,1)S(1)}, u32[]{:S(2)}, u32[]{:S(2)}) collective-permute-start(bf16[32,3584]{1,0:T(8,128)(2,1)S(1)} %fusion.2), channel_id=1, source_target_pairs={{0,8},{1,9},{2,10},{3,11},{4,12},{5,13},{6,14},{7,15},{8,0},{9,1},... | collective-permute-start | bytes 688136 | tf_op jit(solution)/shard_map/ppermute | solution.py:94
  121.0 7.6 %collective-permute-done.21 = bf16[80,3584]{1,0:T(8,128)(2,1)S(1)} collective-permute-done((bf16[80,3584]{1,0:T(8,128)(2,1)S(1)}, bf16[80,3584]{1,0:T(8,128)(2,1)S(1)}, u32[]{:S(2)}, u32[]{:S(2)}) %collective-permute-start.21) | collective-permute-done | bytes 573472 | tf_op jit(solution)/shard_map/ppermute | solution.py:94
  128.7 0.5 collective-permute-done.24
  129.3 0.7 copy-done.19
  130.1 1.3 collective-permute-start.29
  131.4 0.2 fusion.4
  131.6 4.1 %collective-permute-start.25 = (bf16[32,3584]{1,0:T(8,128)(2,1)S(1)}, bf16[32,3584]{1,0:T(8,128)(2,1)S(1)}, u32[]{:S(2)}, u32[]{:S(2)}) collective-permute-start(bf16[32,3584]{1,0:T(8,128)(2,1)S(1)} %get-tuple-element.38), channel_id=1, source_target_pairs={{0,12},{1,13},{2,14},{3,15},{4,0},{5,1},{6,2},{7,3},{8,4},{9,5},{1... | collective-permute-start | bytes 688136 | tf_op jit(solution)/shard_map/ppermute | solution.py:94
  135.7 1.3 collective-permute-start.28
  137.0 2.9 %collective-permute-done.25 = bf16[32,3584]{1,0:T(8,128)(2,1)S(1)} collective-permute-done((bf16[32,3584]{1,0:T(8,128)(2,1)S(1)}, bf16[32,3584]{1,0:T(8,128)(2,1)S(1)}, u32[]{:S(2)}, u32[]{:S(2)}) %collective-permute-start.25) | collective-permute-done | bytes 229408 | tf_op jit(solution)/shard_map/ppermute | solution.py:94
  139.9 3.9 %collective-permute-done.26 = bf16[32,3584]{1,0:T(8,128)(2,1)S(1)} collective-permute-done((bf16[32,3584]{1,0:T(8,128)(2,1)S(1)}, bf16[32,3584]{1,0:T(8,128)(2,1)S(1)}, u32[]{:S(2)}, u32[]{:S(2)}) %collective-permute-start.26) | collective-permute-done | bytes 229408 | tf_op jit(solution)/shard_map/ppermute | solution.py:94
  143.8 0.1 convert_add_fusion
  144.1 0.2 slice_reduce_fusion
  144.3 0.7 fusion.16
  145.0 0.6 collective-permute-done.30.other_ref
  145.6 1.3 shard_map.108
  (102 shorter events, 2.5 us)
Async XLA Ops:
  0.7 23.0 %copy-start.6 = (s32[2]{0:T(128)}, s32[2]{0:T(128)S(1)}, u32[]{:S(2)}) copy-start(s32[2]{0:T(128)S(1)} %pad_add_fusion.here_ref) | copy-start | bytes 28
  0.7 23.0 %copy-start.5 = (bf16[1,64,576]{2,1,0:T(8,128)(2,1)S(1)}, bf16[1,64,576]{2,1,0:T(8,128)(2,1)}, u32[]{:S(2)}) copy-start(bf16[1,64,576]{2,1,0:T(8,128)(2,1)} %param.15) | copy-start | bytes 221188
  2.4 0.7 copy-start.4
  3.1 19.2 %copy-start.3 = (bf16[32,3712]{1,0:T(8,128)(2,1)}, bf16[32,3712]{1,0:T(8,128)(2,1)S(1)}, u32[]{:S(2)}) copy-start(bf16[32,3712]{1,0:T(8,128)(2,1)S(1)} %get-tuple-element.20.refs_0_) | copy-start | bytes 712708
  3.1 20.6 %copy-start = (bf16[1,2048,576]{1,2,0:T(8,128)(2,1)S(1)}, bf16[1,2048,576]{1,2,0:T(8,128)(2,1)}, u32[]{:S(2)}) copy-start(bf16[1,2048,576]{1,2,0:T(8,128)(2,1)} %param.16) | copy-start | bytes 7077892
  3.1 8.7 %collective-permute-start.1 = (bf16[32,3712]{1,0:T(8,128)(2,1)S(1)}, bf16[32,3712]{1,0:T(8,128)(2,1)S(1)}, u32[]{:S(2)}, u32[]{:S(2)}) collective-permute-start(bf16[32,3712]{1,0:T(8,128)(2,1)S(1)} %get-tuple-element.20.refs_0_), channel_id=1, source_target_pairs={{0,2},{1,3},{2,0},{3,1},{4,6},{5,7},{6,4},{7,5},{8,10},{9,11},{10,... | collective-permute-start | bytes 712712 | tf_op jit(solution)/shard_map/ppermute | solution.py:94
  6.1 7.2 %collective-permute-start = (bf16[32,3712]{1,0:T(8,128)(2,1)S(1)}, bf16[32,3712]{1,0:T(8,128)(2,1)S(1)}, u32[]{:S(2)}, u32[]{:S(2)}) collective-permute-start(bf16[32,3712]{1,0:T(8,128)(2,1)S(1)} %get-tuple-element.20.refs_0_), channel_id=1, source_target_pairs={{0,1},{1,0},{2,3},{3,2},{4,5},{5,4},{6,7},{7,6},{8,9},{9,8},{10,11... | collective-permute-start | bytes 712712 | tf_op jit(solution)/shard_map/ppermute | solution.py:94
  7.5 9.8 %collective-permute-start.3 = (bf16[32,3712]{1,0:T(8,128)(2,1)S(1)}, bf16[32,3712]{1,0:T(8,128)(2,1)S(1)}, u32[]{:S(2)}, u32[]{:S(2)}) collective-permute-start(bf16[32,3712]{1,0:T(8,128)(2,1)S(1)} %get-tuple-element.20.refs_0_), channel_id=1, source_target_pairs={{0,12},{1,13},{2,14},{3,15},{4,0},{5,1},{6,2},{7,3},{8,4},{9,5},{1... | collective-permute-start | bytes 712712 | tf_op jit(solution)/shard_map/ppermute | solution.py:94
  11.2 10.5 %collective-permute-start.2 = (bf16[32,3712]{1,0:T(8,128)(2,1)S(1)}, bf16[32,3712]{1,0:T(8,128)(2,1)S(1)}, u32[]{:S(2)}, u32[]{:S(2)}) collective-permute-start(bf16[32,3712]{1,0:T(8,128)(2,1)S(1)} %get-tuple-element.20.refs_0_), channel_id=1, source_target_pairs={{0,4},{1,5},{2,6},{3,7},{4,8},{5,9},{6,10},{7,11},{8,12},{9,13},{1... | collective-permute-start | bytes 712712 | tf_op jit(solution)/shard_map/ppermute | solution.py:94
  11.8 30.1 %copy-start.16 = (bf16[32,3712]{1,0:T(8,128)(2,1)}, bf16[32,3712]{1,0:T(8,128)(2,1)S(1)}, u32[]{:S(2)}) copy-start(bf16[32,3712]{1,0:T(8,128)(2,1)S(1)} %collective-permute-done.1.refs_2_) | copy-start | bytes 712708
  13.3 28.6 %copy-start.17 = (bf16[32,3712]{1,0:T(8,128)(2,1)}, bf16[32,3712]{1,0:T(8,128)(2,1)S(1)}, u32[]{:S(2)}) copy-start(bf16[32,3712]{1,0:T(8,128)(2,1)S(1)} %collective-permute-done.refs_1_) | copy-start | bytes 712708
  17.4 8.3 %copy-start.8 = (bf16[32,3712]{1,0:T(8,128)(2,1)}, bf16[32,3712]{1,0:T(8,128)(2,1)S(1)}, u32[]{:S(2)}) copy-start(bf16[32,3712]{1,0:T(8,128)(2,1)S(1)} %collective-permute-done.3._.refs_4_) | copy-start | bytes 712708
  21.6 20.3 %copy-start.15 = (bf16[32,3712]{1,0:T(8,128)(2,1)}, bf16[32,3712]{1,0:T(8,128)(2,1)S(1)}, u32[]{:S(2)}) copy-start(bf16[32,3712]{1,0:T(8,128)(2,1)S(1)} %collective-permute-done.2.refs_3_) | copy-start | bytes 712708
  21.7 14.2 %collective-permute-start.5 = (bf16[80,3712]{1,0:T(8,128)(2,1)S(1)}, bf16[80,3712]{1,0:T(8,128)(2,1)S(1)}, u32[]{:S(2)}, u32[]{:S(2)}) collective-permute-start(bf16[80,3712]{1,0:T(8,128)(2,1)S(1)} %get-tuple-element.54), channel_id=1, source_target_pairs={{0,2},{1,3},{2,0},{3,1},{4,6},{5,7},{6,4},{7,5},{8,10},{9,11},{10,... | collective-permute-start | bytes 1781768 | tf_op jit(solution)/shard_map/ppermute | solution.py:94
  22.3 12.6 %collective-permute-start.6 = (bf16[32,3712]{1,0:T(8,128)(2,1)S(1)}, bf16[32,3712]{1,0:T(8,128)(2,1)S(1)}, u32[]{:S(2)}, u32[]{:S(2)}) collective-permute-start(bf16[32,3712]{1,0:T(8,128)(2,1)S(1)} %get-tuple-element.20.refs_0_), channel_id=1, source_target_pairs={{0,8},{1,9},{2,10},{3,11},{4,12},{5,13},{6,14},{7,15},{8,0},{9,1},... | collective-permute-start | bytes 712712 | tf_op jit(solution)/shard_map/ppermute | solution.py:94
  25.7 0.6 copy-start.1
  26.3 12.6 %collective-permute-start.4 = (bf16[80,3712]{1,0:T(8,128)(2,1)S(1)}, bf16[80,3712]{1,0:T(8,128)(2,1)S(1)}, u32[]{:S(2)}, u32[]{:S(2)}) collective-permute-start(bf16[80,3712]{1,0:T(8,128)(2,1)S(1)} %get-tuple-element.55), channel_id=1, source_target_pairs={{0,1},{1,0},{2,3},{3,2},{4,5},{5,4},{6,7},{7,6},{8,9},{9,8},{10,11... | collective-permute-start | bytes 1781768 | tf_op jit(solution)/shard_map/ppermute | solution.py:94
  35.9 5.8 %copy-start.10 = (bf16[32,3712]{1,0:T(8,128)(2,1)}, bf16[32,3712]{1,0:T(8,128)(2,1)S(1)}, u32[]{:S(2)}) copy-start(bf16[32,3712]{1,0:T(8,128)(2,1)S(1)} %add.135.refs_7_) | copy-start | bytes 712708
  36.0 5.7 %copy-start.11 = (bf16[80,3712]{1,0:T(8,128)(2,1)}, bf16[80,3712]{1,0:T(8,128)(2,1)S(1)}, u32[]{:S(2)}) copy-start(bf16[80,3712]{1,0:T(8,128)(2,1)S(1)} %collective-permute-done.5.refs_6_) | copy-start | bytes 1781764
  38.9 2.9 %copy-start.12 = (bf16[80,3712]{1,0:T(8,128)(2,1)}, bf16[80,3712]{1,0:T(8,128)(2,1)S(1)}, u32[]{:S(2)}) copy-start(bf16[80,3712]{1,0:T(8,128)(2,1)S(1)} %collective-permute-done.4.refs_5_) | copy-start | bytes 1781764
  39.0 9.2 %collective-permute-start.8 = (bf16[64,3712]{1,0:T(8,128)(2,1)S(1)}, bf16[64,3712]{1,0:T(8,128)(2,1)S(1)}, u32[]{:S(2)}, u32[]{:S(2)}) collective-permute-start(bf16[64,3712]{1,0:T(8,128)(2,1)S(1)} %get-tuple-element.58), channel_id=1, source_target_pairs={{0,2},{1,3},{2,0},{3,1},{4,6},{5,7},{6,4},{7,5},{8,10},{9,11},{10,... | collective-permute-start | bytes 1425416 | tf_op jit(solution)/shard_map/ppermute | solution.py:94
  41.2 0.9 copy-start.9
  41.2 8.7 %collective-permute-start.7 = (bf16[64,3712]{1,0:T(8,128)(2,1)S(1)}, bf16[64,3712]{1,0:T(8,128)(2,1)S(1)}, u32[]{:S(2)}, u32[]{:S(2)}) collective-permute-start(bf16[64,3712]{1,0:T(8,128)(2,1)S(1)} %get-tuple-element.59), channel_id=1, source_target_pairs={{0,1},{1,0},{2,3},{3,2},{4,5},{5,4},{6,7},{7,6},{8,9},{9,8},{10,11... | collective-permute-start | bytes 1425416 | tf_op jit(solution)/shard_map/ppermute | solution.py:94
  41.8 15.8 %collective-permute-start.12 = (bf16[192,3712]{1,0:T(8,128)(2,1)S(1)}, bf16[192,3712]{1,0:T(8,128)(2,1)S(1)}, u32[]{:S(2)}, u32[]{:S(2)}) collective-permute-start(bf16[192,3712]{1,0:T(8,128)(2,1)S(1)} %pad_maximum_fusion), channel_id=1, source_target_pairs={{0,16},{16,0},{1,17},{17,1},{2,18},{18,2},{3,19},{19,3},{4,20},{20... | collective-permute-start | bytes 4276232 | tf_op jit(solution)/shard_map/ppermute | solution.py:67
  42.2 14.4 %collective-permute-start.11 = (bf16[128,3712]{1,0:T(8,128)(2,1)S(1)}, bf16[128,3712]{1,0:T(8,128)(2,1)S(1)}, u32[]{:S(2)}, u32[]{:S(2)}) collective-permute-start(bf16[128,3712]{1,0:T(8,128)(2,1)S(1)} %pad_maximum_fusion.1), channel_id=1, source_target_pairs={{0,16},{16,0},{1,17},{17,1},{2,18},{18,2},{3,19},{19,3},{4,20},{20... | collective-permute-start | bytes 2850824 | tf_op jit(solution)/shard_map/ppermute | solution.py:67
  48.3 2.3 %copy-start.13 = (bf16[64,3712]{1,0:T(8,128)(2,1)}, bf16[64,3712]{1,0:T(8,128)(2,1)S(1)}, u32[]{:S(2)}) copy-start(bf16[64,3712]{1,0:T(8,128)(2,1)S(1)} %collective-permute-done.8.refs_9_) | copy-start | bytes 1425412
  49.8 0.8 copy-start.14
  49.9 7.7 %collective-permute-start.13 = (bf16[128,3712]{1,0:T(8,128)(2,1)S(1)}, bf16[128,3712]{1,0:T(8,128)(2,1)S(1)}, u32[]{:S(2)}, u32[]{:S(2)}) collective-permute-start(bf16[128,3712]{1,0:T(8,128)(2,1)S(1)} %pad_maximum_fusion.2), channel_id=1, source_target_pairs={{0,16},{16,0},{1,17},{17,1},{2,18},{18,2},{3,19},{19,3},{4,20},{20... | collective-permute-start | bytes 2850824 | tf_op jit(solution)/shard_map/ppermute | solution.py:67
  50.0 5.7 %collective-permute-start.9 = (bf16[16,3712]{1,0:T(8,128)(2,1)S(1)}, bf16[16,3712]{1,0:T(8,128)(2,1)S(1)}, u32[]{:S(2)}, u32[]{:S(2)}) collective-permute-start(bf16[16,3712]{1,0:T(8,128)(2,1)S(1)} %slice.294), channel_id=1, source_target_pairs={{0,1},{1,0},{2,3},{3,2},{4,5},{5,4},{6,7},{7,6},{8,9},{9,8},{10,11... | collective-permute-start | bytes 356360 | tf_op jit(solution)/shard_map/ppermute | solution.py:94
  50.6 5.4 %collective-permute-start.10 = (bf16[16,3712]{1,0:T(8,128)(2,1)S(1)}, bf16[16,3712]{1,0:T(8,128)(2,1)S(1)}, u32[]{:S(2)}, u32[]{:S(2)}) collective-permute-start(bf16[16,3712]{1,0:T(8,128)(2,1)S(1)} %slice.295), channel_id=1, source_target_pairs={{0,2},{1,3},{2,0},{3,1},{4,6},{5,7},{6,4},{7,5},{8,10},{9,11},{10,... | collective-permute-start | bytes 356360 | tf_op jit(solution)/shard_map/ppermute | solution.py:94
  55.7 2.0 %copy-start.24 = (bf16[16,3712]{1,0:T(8,128)(2,1)}, bf16[16,3712]{1,0:T(8,128)(2,1)S(1)}, u32[]{:S(2)}) copy-start(bf16[16,3712]{1,0:T(8,128)(2,1)S(1)} %collective-permute-done.9.refs_10_) | copy-start | bytes 356356
  56.0 1.6 %copy-start.25 = (bf16[16,3712]{1,0:T(8,128)(2,1)}, bf16[16,3712]{1,0:T(8,128)(2,1)S(1)}, u32[]{:S(2)}) copy-start(bf16[16,3712]{1,0:T(8,128)(2,1)S(1)} %collective-permute-done.10.refs_11_) | copy-start | bytes 356356
  56.1 1.6 %collective-permute-start.14 = (bf16[32,3712]{1,0:T(8,128)(2,1)S(1)}, bf16[32,3712]{1,0:T(8,128)(2,1)S(1)}, u32[]{:S(2)}, u32[]{:S(2)}) collective-permute-start(bf16[32,3712]{1,0:T(8,128)(2,1)S(1)} %pad_maximum_fusion.11), channel_id=1, source_target_pairs={{0,16},{16,0},{1,17},{17,1},{2,18},{18,2},{3,19},{19,3},{4,20},{20... | collective-permute-start | bytes 712712 | tf_op jit(solution)/shard_map/ppermute | solution.py:67
  56.1 36.5 %collective-permute-start.31 = (f32[1,32,640]{2,1,0:T(8,128)S(1)}, f32[1,32,640]{2,1,0:T(8,128)S(1)}, u32[]{:S(2)}, u32[]{:S(2)}) collective-permute-start(f32[1,32,640]{2,1,0:T(8,128)S(1)} %bitcast.16), channel_id=1, source_target_pairs={{0,16},{16,0},{1,17},{17,1},{2,18},{18,2},{3,19},{19,3},{4,20},{20... | collective-permute-start | bytes 245768 | tf_op jit(solution)/shard_map/ppermute | solution.py:67
  56.6 1.0 copy-start.22
  57.6 0.7 copy-start.26
  57.6 1.0 copy-start.23
  57.6 1.5 copy-start.18
  59.1 33.5 %copy-start.2 = (f32[32,640]{1,0:T(8,128)S(1)}, f32[32,640]{1,0:T(8,128)}, u32[]{:S(2)}) copy-start(f32[32,640]{1,0:T(8,128)} %copy-done.1) | copy-start | bytes 245764
  92.4 10.2 %copy-start.20 = (bf16[160,3584]{1,0:T(8,128)(2,1)S(1)}, bf16[160,3584]{1,0:T(8,128)(2,1)}, u32[]{:S(2)}) copy-start(bf16[160,3584]{1,0:T(8,128)(2,1)} %get-tuple-element.31) | copy-start | bytes 3440644
  92.4 6.8 %collective-permute-start.17 = (bf16[160,3584]{1,0:T(8,128)(2,1)}, bf16[160,3584]{1,0:T(8,128)(2,1)S(1)}, u32[]{:S(2)}, u32[]{:S(2)}) collective-permute-start(bf16[160,3584]{1,0:T(8,128)(2,1)} %get-tuple-element.32), channel_id=1, source_target_pairs={{0,16},{16,0},{1,17},{17,1},{2,18},{18,2},{3,19},{19,3},{4,20},{20... | collective-permute-start | bytes 3440648 | tf_op jit(solution)/shard_map/ppermute | solution.py:67
  92.8 3.1 %collective-permute-start.18 = (bf16[32,3584]{1,0:T(8,128)(2,1)}, bf16[32,3584]{1,0:T(8,128)(2,1)S(1)}, u32[]{:S(2)}, u32[]{:S(2)}) collective-permute-start(bf16[32,3584]{1,0:T(8,128)(2,1)} %get-tuple-element.34), channel_id=1, source_target_pairs={{0,16},{16,0},{1,17},{17,1},{2,18},{18,2},{3,19},{19,3},{4,20},{20... | collective-permute-start | bytes 688136 | tf_op jit(solution)/shard_map/ppermute | solution.py:67
  93.3 36.0 %collective-permute-start.15 = (bf16[160,3584]{1,0:T(8,128)(2,1)}, bf16[160,3584]{1,0:T(8,128)(2,1)S(1)}, u32[]{:S(2)}, u32[]{:S(2)}) collective-permute-start(bf16[160,3584]{1,0:T(8,128)(2,1)} %get-tuple-element.28), channel_id=1, source_target_pairs={{0,16},{16,0},{1,17},{17,1},{2,18},{18,2},{3,19},{19,3},{4,20},{20... | collective-permute-start | bytes 3440648 | tf_op jit(solution)/shard_map/ppermute | solution.py:67
  93.5 12.2 %collective-permute-start.16 = (bf16[160,3584]{1,0:T(8,128)(2,1)}, bf16[160,3584]{1,0:T(8,128)(2,1)S(1)}, u32[]{:S(2)}, u32[]{:S(2)}) collective-permute-start(bf16[160,3584]{1,0:T(8,128)(2,1)} %get-tuple-element.30), channel_id=1, source_target_pairs={{0,16},{16,0},{1,17},{17,1},{2,18},{18,2},{3,19},{19,3},{4,20},{20... | collective-permute-start | bytes 3440648 | tf_op jit(solution)/shard_map/ppermute | solution.py:67
  96.8 5.3 %collective-permute-start.22 = (bf16[16,3584]{1,0:T(8,128)(2,1)S(1)}, bf16[16,3584]{1,0:T(8,128)(2,1)S(1)}, u32[]{:S(2)}, u32[]{:S(2)}) collective-permute-start(bf16[16,3584]{1,0:T(8,128)(2,1)S(1)} %get-tuple-element.56), channel_id=1, source_target_pairs={{0,2},{1,3},{2,0},{3,1},{4,6},{5,7},{6,4},{7,5},{8,10},{9,11},{10,... | collective-permute-start | bytes 344072 | tf_op jit(solution)/shard_map/ppermute | solution.py:94
  97.7 4.9 %collective-permute-start.19 = (bf16[16,3584]{1,0:T(8,128)(2,1)S(1)}, bf16[16,3584]{1,0:T(8,128)(2,1)S(1)}, u32[]{:S(2)}, u32[]{:S(2)}) collective-permute-start(bf16[16,3584]{1,0:T(8,128)(2,1)S(1)} %get-tuple-element.57), channel_id=1, source_target_pairs={{0,1},{1,0},{2,3},{3,2},{4,5},{5,4},{6,7},{7,6},{8,9},{9,8},{10,11... | collective-permute-start | bytes 344072 | tf_op jit(solution)/shard_map/ppermute | solution.py:94
  102.8 3.0 %copy-start.21 = (bf16[160,3584]{1,0:T(8,128)(2,1)S(1)}, bf16[160,3584]{1,0:T(8,128)(2,1)}, u32[]{:S(2)}) copy-start(bf16[160,3584]{1,0:T(8,128)(2,1)} %get-tuple-element.29) | copy-start | bytes 3440644
  102.8 13.7 %collective-permute-start.23 = (bf16[64,3584]{1,0:T(8,128)(2,1)S(1)}, bf16[64,3584]{1,0:T(8,128)(2,1)S(1)}, u32[]{:S(2)}, u32[]{:S(2)}) collective-permute-start(bf16[64,3584]{1,0:T(8,128)(2,1)S(1)} %pad_maximum_fusion.10), channel_id=1, source_target_pairs={{0,1},{1,0},{2,3},{3,2},{4,5},{5,4},{6,7},{7,6},{8,9},{9,8},{10,11... | collective-permute-start | bytes 1376264 | tf_op jit(solution)/shard_map/ppermute | solution.py:94
  104.5 11.2 %collective-permute-start.20 = (bf16[64,3584]{1,0:T(8,128)(2,1)S(1)}, bf16[64,3584]{1,0:T(8,128)(2,1)S(1)}, u32[]{:S(2)}, u32[]{:S(2)}) collective-permute-start(bf16[64,3584]{1,0:T(8,128)(2,1)S(1)} %pad_maximum_fusion.9), channel_id=1, source_target_pairs={{0,2},{1,3},{2,0},{3,1},{4,6},{5,7},{6,4},{7,5},{8,10},{9,11},{10,... | collective-permute-start | bytes 1376264 | tf_op jit(solution)/shard_map/ppermute | solution.py:94
  115.9 12.7 %collective-permute-start.21 = (bf16[80,3584]{1,0:T(8,128)(2,1)S(1)}, bf16[80,3584]{1,0:T(8,128)(2,1)S(1)}, u32[]{:S(2)}, u32[]{:S(2)}) collective-permute-start(bf16[80,3584]{1,0:T(8,128)(2,1)S(1)} %pad_maximum_fusion.6), channel_id=1, source_target_pairs={{0,1},{1,0},{2,3},{3,2},{4,5},{5,4},{6,7},{7,6},{8,9},{9,8},{10,11... | collective-permute-start | bytes 1720328 | tf_op jit(solution)/shard_map/ppermute | solution.py:94
  116.7 12.5 %collective-permute-start.24 = (bf16[80,3584]{1,0:T(8,128)(2,1)S(1)}, bf16[80,3584]{1,0:T(8,128)(2,1)S(1)}, u32[]{:S(2)}, u32[]{:S(2)}) collective-permute-start(bf16[80,3584]{1,0:T(8,128)(2,1)S(1)} %fusion.13), channel_id=1, source_target_pairs={{0,2},{1,3},{2,0},{3,1},{4,6},{5,7},{6,4},{7,5},{8,10},{9,11},{10,... | collective-permute-start | bytes 1720328 | tf_op jit(solution)/shard_map/ppermute | solution.py:94
  118.1 18.9 %collective-permute-start.27 = (bf16[32,3584]{1,0:T(8,128)(2,1)S(1)}, bf16[32,3584]{1,0:T(8,128)(2,1)S(1)}, u32[]{:S(2)}, u32[]{:S(2)}) collective-permute-start(bf16[32,3584]{1,0:T(8,128)(2,1)S(1)} %fusion.2), channel_id=1, source_target_pairs={{0,8},{1,9},{2,10},{3,11},{4,12},{5,13},{6,14},{7,15},{8,0},{9,1},... | collective-permute-start | bytes 688136 | tf_op jit(solution)/shard_map/ppermute | solution.py:94
  128.7 1.3 copy-start.19
  130.1 13.8 %collective-permute-start.29 = (bf16[32,3584]{1,0:T(8,128)(2,1)S(1)}, bf16[32,3584]{1,0:T(8,128)(2,1)S(1)}, u32[]{:S(2)}, u32[]{:S(2)}) collective-permute-start(bf16[32,3584]{1,0:T(8,128)(2,1)S(1)} %pad_maximum_fusion.13), channel_id=1, source_target_pairs={{0,2},{1,3},{2,0},{3,1},{4,6},{5,7},{6,4},{7,5},{8,10},{9,11},{10,... | collective-permute-start | bytes 688136 | tf_op jit(solution)/shard_map/ppermute | solution.py:94
  131.6 8.3 %collective-permute-start.25 = (bf16[32,3584]{1,0:T(8,128)(2,1)S(1)}, bf16[32,3584]{1,0:T(8,128)(2,1)S(1)}, u32[]{:S(2)}, u32[]{:S(2)}) collective-permute-start(bf16[32,3584]{1,0:T(8,128)(2,1)S(1)} %get-tuple-element.38), channel_id=1, source_target_pairs={{0,12},{1,13},{2,14},{3,15},{4,0},{5,1},{6,2},{7,3},{8,4},{9,5},{1... | collective-permute-start | bytes 688136 | tf_op jit(solution)/shard_map/ppermute | solution.py:94
  135.7 8.1 %collective-permute-start.26 = (bf16[32,3584]{1,0:T(8,128)(2,1)S(1)}, bf16[32,3584]{1,0:T(8,128)(2,1)S(1)}, u32[]{:S(2)}, u32[]{:S(2)}) collective-permute-start(bf16[32,3584]{1,0:T(8,128)(2,1)S(1)} %get-tuple-element.39), channel_id=1, source_target_pairs={{0,4},{1,5},{2,6},{3,7},{4,8},{5,9},{6,10},{7,11},{8,12},{9,13},{1... | collective-permute-start | bytes 688136 | tf_op jit(solution)/shard_map/ppermute | solution.py:94
  135.7 9.9 %copy-start.7 = (s32[2]{0:T(128)S(1)}, s32[2]{0:T(128)}, u32[]{:S(2)}) copy-start(s32[2]{0:T(128)} %copy-done.6) | copy-start | bytes 28
  135.7 8.2 %collective-permute-start.28 = (bf16[32,3584]{1,0:T(8,128)(2,1)S(1)}, bf16[32,3584]{1,0:T(8,128)(2,1)S(1)}, u32[]{:S(2)}, u32[]{:S(2)}) collective-permute-start(bf16[32,3584]{1,0:T(8,128)(2,1)S(1)} %pad_maximum_fusion.12), channel_id=1, source_target_pairs={{0,1},{1,0},{2,3},{3,2},{4,5},{5,4},{6,7},{7,6},{8,9},{9,8},{10,11... | collective-permute-start | bytes 688136 | tf_op jit(solution)/shard_map/ppermute | solution.py:94
  144.0 1.6 %collective-permute-start.30 = (bf16[32,3584]{1,0:T(8,128)(2,1)S(1)}, bf16[32,3584]{1,0:T(8,128)(2,1)S(1)}, u32[]{:S(2)}, u32[]{:S(2)}) collective-permute-start(bf16[32,3584]{1,0:T(8,128)(2,1)S(1)} %add_convert_fusion.1.own_ref), channel_id=1, source_target_pairs={{0,16},{16,0},{1,17},{17,1},{2,18},{18,2},{3,19},{19,3},{4,20},{20... | collective-permute-start | bytes 688136 | tf_op jit(solution)/shard_map/ppermute | solution.py:67

commit v5 on v4

--- a/solution.py
+++ b/solution.py
@@ -11,14 +11,15 @@
 CAP = 8
 JOIN = 4
 COLS = 512
-AHEAD = 2
-MORE = 2
-VMEM_LIMIT = 71 * 512 * 1024
+AHEAD = 3
+MORE = 1
+VMEM_LIMIT = 55 * 512 * 1024
 
 softmax_scale = 192.0 ** (-0.5)
 
 
-def attend_kernel(request, here_ref, lengths_ref, queries_ref, cache_ref, kept_ref, sent_ref, joined):
+def attend_kernel(request, here_ref, lengths_ref, queries_ref, cache_ref, kept_ref, sent_ref, zeros_ref, joined):
+    zeros_ref[...] = jnp.zeros_like(zeros_ref)
     heads, span = queries_ref.shape[0], cache_ref.shape[1]
     share = heads // 2
     core = here_ref[0]
@@ -44,15 +45,15 @@
     sent_ref[...] = joined[pl.ds(pl.multiple_of((1 - core) * share, share), share)]
 
 
-def attend_part(queries, cache, lengths, request, here):
+def attend_part(queries, cache, lengths, request, here, like):
     heads, depth = queries.shape
     part = jax.ShapeDtypeStruct((heads // 2, LAT + 128), jnp.float32)
     return pl.pallas_call(
         functools.partial(attend_kernel, request),
-        out_shape=(part, part),
+        out_shape=(part, part, jax.ShapeDtypeStruct(like.shape, like.dtype)),
         in_specs=[pl.BlockSpec(memory_space=pltpu.SMEM)] * 2
         + [pl.BlockSpec(memory_space=pltpu.VMEM)] * 2,
-        out_specs=(pl.BlockSpec(memory_space=pltpu.VMEM),) * 2,
+        out_specs=(pl.BlockSpec(memory_space=pltpu.VMEM),) * 3,
         scratch_shapes=[pltpu.VMEM((heads, LAT + 128), jnp.float32)],
         compiler_params=pltpu.CompilerParams(vmem_limit_bytes=16 * 1024 * 1024),
         cost_estimate=pl.CostEstimate(
@@ -67,12 +68,13 @@
     return lax.ppermute(x, "ctx", [(0, 1), (1, 0)])
 
 
-def attend_local(queries, latent_cache, cache_lengths, here):
+def attend_local(queries, latent_cache, cache_lengths, here, like):
     parts = [
-        attend_part(queries[r], latent_cache[r], cache_lengths, r, here)
+        attend_part(queries[r], latent_cache[r], cache_lengths, r, here, like)
         for r in range(queries.shape[0])
     ]
-    return tuple(jnp.stack(half) for half in zip(*parts))
+    kept, sent, zeros = zip(*parts)
+    return (jnp.stack(kept), jnp.stack(sent)), zeros[-1]
 
 
 def join_cores(kept, sent):
@@ -120,10 +122,10 @@
     below, above = to_z(rows, 1), to_z(rows, 3)
     own_x, own_y = to_x(rows), to_y(rows)
     far = to_z(after(rows, below), 2)
-    bx = to_x(cat(below, above, own_y[h:]))
-    by = to_y(cat(below, above, own_x[:h]))
+    result, begun, done = meanwhile(above)
+    bx = to_x(cat(below, above + begun, own_y[h:]))
+    by = to_y(cat(below, above + begun, own_x[:h]))
     early = swap_ctx(cat(own_x, own_y, below, above))
-    result, done = meanwhile(above)
     far = far + done
     cx = to_x(cat(far, by[h:n], by[n + h : 2 * n]))
     cy = to_y(cat(far, bx[:h], bx[n : n + h]))
@@ -154,7 +156,6 @@
     ((0, 8, 10), (1, 2, 4), (1, 7, 9), (2, 9, 10), (2, 5, 6)),
 )
 BUNDLES = (10, 10, 10, 2)
-ORDER = (2, 1, 3, 0)
 
 
 def scatter_sums(kept, came):
@@ -259,7 +260,7 @@
                 copies.append(
                     pltpu.make_async_copy(
                         side[b].at[pl.ds(f * unit, rows)],
-                        staged.at[stage_of(group), pl.ds(at, rows)],
+                        staged.at[group, pl.ds(at, rows)],
                         in_sems.at[len(copies) + 10 * group],
                     )
                 )
@@ -282,7 +283,7 @@
                 rows = (t - f) * unit
                 copies.append(
                     pltpu.make_async_copy(
-                        staged.at[stage_of(group), pl.ds(at, rows), pl.ds(0, width)],
+                        staged.at[group, pl.ds(at, rows), pl.ds(0, width)],
                         side[b].at[pl.ds(f * unit, rows)],
                         out_sems.at[len(copies) + 10 * group],
                     )
@@ -291,7 +292,7 @@
         return copies
 
     def stage_of(group):
-        return ORDER.index(group) % 2 if planes else 0
+        return group if planes else 0
 
     def sort_rows(group):
         copies = takes(group)
@@ -392,34 +393,25 @@
     def each(count, work):
         lax.fori_loop(0, count, lambda i, _: (work(i), 0)[1], 0)
 
-    def start(copies):
-        for copy in copies:
+    if planes:
+        for group in range(group_count):
+            for copy in takes(group):
+                copy.start()
+    for e in range(ahead, depth):
+        for copy in loads(e, e):
             copy.start()
-
-    def wait(copies):
-        for copy in copies:
-            copy.wait()
-
     if planes:
-        for group in ORDER[:2]:
-            start(takes(group))
-    for e in range(ahead, depth):
-        start(loads(e, e))
-    if planes:
-        for place, group in enumerate(ORDER):
+        for group in range(group_count):
             sort_rows(group)
-            if place + 2 < group_count:
-                start(takes(ORDER[place + 2]))
     else:
         each(group_count, sort_rows)
     each(expert_count // depth, run_experts)
     if planes:
-        for place, group in enumerate(ORDER):
-            if place >= 2:
-                wait(puts(ORDER[place - 2]))
+        for group in (2, 1, 3, 0):
             sum_rows(group)
-        for group in ORDER[2:]:
-            wait(puts(group))
+        for group in (2, 1, 3, 0):
+            for copy in puts(group):
+                copy.wait()
     else:
         each(group_count, sum_rows)
 
@@ -440,8 +432,7 @@
 
 
 def weights_ahead(gate_weight, up_weight, down_weight, *follows):
-    depth = min(AHEAD, gate_weight.shape[0])
-    assert gate_weight.shape[0] % depth == 0
+    depth = AHEAD if gate_weight.shape[0] % (AHEAD + MORE) == 0 else 1
     weights = [gate_weight, up_weight, down_weight]
     return pl.pallas_call(
         ahead_kernel,
@@ -472,7 +463,7 @@
         out_rows = [u * half // 8 for u in BUNDLES] * 2
     else:
         out_rows = [own[0].shape[0]] * 2
-    stages, copies = (2, 10 * group_count) if planes else (1, 2)
+    stages, copies = (group_count, 10 * group_count) if planes else (1, 2)
     weight_bytes = 3 * expert_count * width * hidden * 2
     sums = pl.pallas_call(
         functools.partial(expert_kernel, (planes, group_count, expert_count, width, top)),
@@ -593,9 +584,9 @@
     here = jnp.stack([core, chip * gate_weight.shape[0]]).astype(jnp.int32)
 
     def meanwhile(follows):
-        packed = attend(here)
+        packed, begun = attend(here, follows)
         *ahead, done = weights_ahead(gate_weight, up_weight, down_weight, follows, packed[0])
-        return (ahead, packed), done
+        return (ahead, packed), begun, done
 
     mine, theirs = ask(moe_rows, routes, route_gates, here)
     if plane_of(owners):

time: 147 us -> 139 us (0.946)
  waiting for transfers between devices: 55.8 us -> 48.9 us
  Pallas kernels: 46.3 us -> 43.8 us
  local copies, waits for them, and re-layouts: 3.91 us -> 5.77 us
    ppermute x22, waiting for transfers between devices: 52.2 us -> 45.3 us  [send(): return lax.ppermute(x, 'ep', [(i, target(i)) for i in range(count)])]
    pallas_call x1, Pallas kernels: 33.3 us -> 27.6 us  [expert_sums(): pl.pallas_call(functools.partial(expert_kernel, (planes, group_count, exp...]
    pallas_call x1, Pallas kernels: 8.09 us -> 11.2 us  [weights_ahead(): pl.pallas_call(ahead_kernel, out_shape=[pltpu.VMEM((depth,) + w.shape[1:]...]
    unnamed x54, local copies, waits for them, and re-layouts: 3.66 us -> 5.52 us
  transfers between devices with their start and end apart: 32 -> 32, of which waited for: 19 -> 16; matrix products, arithmetic and copies ran while one was open for 4% -> 4% of each run, Pallas kernels for 29% -> 29%
where the time goes in v5:
time: 139 us
  waiting for transfers between devices  48.9 us (35%)
  Pallas kernels  43.8 us (32%)
  starting transfers between devices  32.4 us (23%)
  other arithmetic  6.12 us (4%)
  local copies, waits for them, and re-layouts  5.77 us (4%)
  between operations  1.84 us (1%)
    ppermute x22, waiting for transfers between devices, send(): return lax.ppermute(x, 'ep', [(i, target(i)) for i in range(count)])  45.3 us
    ppermute x22, starting transfers between devices, send(): return lax.ppermute(x, 'ep', [(i, target(i)) for i in range(count)])  29.8 us
    pallas_call x1, Pallas kernels, expert_sums(): pl.pallas_call(functools.partial(expert_kernel, (planes, group_count, exp...  27.6 us
    pallas_call x1, Pallas kernels, weights_ahead(): pl.pallas_call(ahead_kernel, out_shape=[pltpu.VMEM((depth,) + w.shape[1:]...  11.2 us
    unnamed x54, local copies, waits for them, and re-layouts  5.52 us
    ppermute x10, waiting for transfers between devices, swap_ctx(): return lax.ppermute(x, 'ctx', [(0, 1), (1, 0)])  3.57 us
  transfers between devices with their start and end apart: 32, of which 16 were waited for; matrix products, arithmetic and copies ran while one was open for 4% of the time, Pallas kernels for 29%

profile of v5, /device:TPU:0, one launch (start us, length us, event | category | flops | bytes accessed | tf_op | source)
XLA Modules:
  0.0 138.7 jit_solution(4437758298581950852)
XLA Ops:
  0.7 1.7 %shard_map.104 = (bf16[32,3712]{1,0:T(8,128)(2,1)S(1)}, bf16[32,3712]{1,0:T(8,128)(2,1)S(1)}) custom-call(s32[2]{0:T(128)S(1)} %pad_add_fusion.here_ref, bf16[64,3584]{1,0:T(8,128)(2,1)} %rows_hbm.1, s32[8,64]{1,0:T(8,128)} %bitcast.17, f32[8,64]{1,0:T(8,128)} %bitcast.18), custom_call_target="tpu_custom_call" | custom-call | tf_op jit(solution)/shard_map/pallas_call | solution.py:544
  2.4 0.7 copy-done.4
  3.1 3.0 %collective-permute-start.1 = (bf16[32,3712]{1,0:T(8,128)(2,1)S(1)}, bf16[32,3712]{1,0:T(8,128)(2,1)S(1)}, u32[]{:S(2)}, u32[]{:S(2)}) collective-permute-start(bf16[32,3712]{1,0:T(8,128)(2,1)S(1)} %get-tuple-element.22.refs_0_), channel_id=1, source_target_pairs={{0,2},{1,3},{2,0},{3,1},{4,6},{5,7},{6,4},{7,5},{8,10},{9,11},{10,... | collective-permute-start | bytes 712712 | tf_op jit(solution)/shard_map/ppermute | solution.py:96
  6.1 1.5 %collective-permute-start = (bf16[32,3712]{1,0:T(8,128)(2,1)S(1)}, bf16[32,3712]{1,0:T(8,128)(2,1)S(1)}, u32[]{:S(2)}, u32[]{:S(2)}) collective-permute-start(bf16[32,3712]{1,0:T(8,128)(2,1)S(1)} %get-tuple-element.22.refs_0_), channel_id=1, source_target_pairs={{0,1},{1,0},{2,3},{3,2},{4,5},{5,4},{6,7},{7,6},{8,9},{9,8},{10,11... | collective-permute-start | bytes 712712 | tf_op jit(solution)/shard_map/ppermute | solution.py:96
  7.5 3.6 %collective-permute-start.3 = (bf16[32,3712]{1,0:T(8,128)(2,1)S(1)}, bf16[32,3712]{1,0:T(8,128)(2,1)S(1)}, u32[]{:S(2)}, u32[]{:S(2)}) collective-permute-start(bf16[32,3712]{1,0:T(8,128)(2,1)S(1)} %get-tuple-element.22.refs_0_), channel_id=1, source_target_pairs={{0,12},{1,13},{2,14},{3,15},{4,0},{5,1},{6,2},{7,3},{8,4},{9,5},{1... | collective-permute-start | bytes 712712 | tf_op jit(solution)/shard_map/ppermute | solution.py:96
  11.8 1.7 %copy-done = bf16[1,2048,576]{1,2,0:T(8,128)(2,1)S(1)} copy-done((bf16[1,2048,576]{1,2,0:T(8,128)(2,1)S(1)}, bf16[1,2048,576]{1,2,0:T(8,128)(2,1)}, u32[]{:S(2)}) %copy-start) | copy-done | bytes 2359320
  13.5 0.9 copy-done.5
  14.4 1.9 %shard_map.105 = (f32[32,640]{1,0:T(8,128)S(1)}, f32[32,640]{1,0:T(8,128)S(1)}, bf16[32,3712]{1,0:T(8,128)(2,1)S(1)}) custom-call(s32[2]{0:T(128)S(1)} %pad_add_fusion.here_ref, s32[1]{0:T(128)S(6)} %copy.21.lengths_ref, bf16[64,576]{1,0:T(8,128)(2,1)S(1)} %bitcast.15, bf16[576,2048]{1,0:T(8,128)(2,1)S(1)} %bitcast.12), custom_call_target="tpu_custom_call" | custom-call | flops 285212672 | bytes 2359296 | tf_op jit(solution)/shard_map/pallas_call | solution.py:51
  16.4 1.0 collective-permute-done.3._.refs_4_
  17.5 4.2 %collective-permute-done.2.refs_3_ = bf16[32,3712]{1,0:T(8,128)(2,1)S(1)} collective-permute-done((bf16[32,3712]{1,0:T(8,128)(2,1)S(1)}, bf16[32,3712]{1,0:T(8,128)(2,1)S(1)}, u32[]{:S(2)}, u32[]{:S(2)}) %collective-permute-start.2) | collective-permute-done | bytes 237600 | tf_op jit(solution)/shard_map/ppermute | solution.py:96
  21.7 0.6 collective-permute-start.5
  22.3 0.7 collective-permute-start.6
  23.0 0.5 collective-permute-start.4
  23.6 11.2 %shard_map.106 = (bf16[3,3584,512]{2,1,0:T(8,128)(2,1)S(1)}, bf16[3,3584,512]{2,1,0:T(8,128)(2,1)S(1)}, bf16[3,512,3584]{2,1,0:T(8,128)(2,1)S(1)}, bf16[32,3712]{1,0:T(8,128)(2,1)}) custom-call(bf16[8,3584,512]{2,1,0:T(8,128)(2,1)} %refs_17_.1, bf16[8,3584,512]{2,1,0:T(8,128)(2,1)} %refs_18_.1, bf16[8,512,3584]{2,1,0:T(8,128)(2,1)} %refs_19_.1, ...), custom_call_target="tpu_custom_call" | custom-call | bytes 33030144 | tf_op jit(solution)/shard_map/pallas_call | solution.py:437
  34.8 1.0 add.140.refs_7_
  36.0 1.6 %collective-permute-start.8 = (bf16[64,3712]{1,0:T(8,128)(2,1)S(1)}, bf16[64,3712]{1,0:T(8,128)(2,1)S(1)}, u32[]{:S(2)}, u32[]{:S(2)}) collective-permute-start(bf16[64,3712]{1,0:T(8,128)(2,1)S(1)} %get-tuple-element.60), channel_id=1, source_target_pairs={{0,2},{1,3},{2,0},{3,1},{4,6},{5,7},{6,4},{7,5},{8,10},{9,11},{10,... | collective-permute-start | bytes 1425416 | tf_op jit(solution)/shard_map/ppermute | solution.py:96
  37.6 1.5 %collective-permute-start.7 = (bf16[64,3712]{1,0:T(8,128)(2,1)S(1)}, bf16[64,3712]{1,0:T(8,128)(2,1)S(1)}, u32[]{:S(2)}, u32[]{:S(2)}) collective-permute-start(bf16[64,3712]{1,0:T(8,128)(2,1)S(1)} %get-tuple-element.61), channel_id=1, source_target_pairs={{0,1},{1,0},{2,3},{3,2},{4,5},{5,4},{6,7},{7,6},{8,9},{9,8},{10,11... | collective-permute-start | bytes 1425416 | tf_op jit(solution)/shard_map/ppermute | solution.py:96
  39.1 0.1 pad_maximum_fusion
  39.5 0.5 collective-permute-start.11
  40.0 6.9 %collective-permute-done.8.refs_9_ = bf16[64,3712]{1,0:T(8,128)(2,1)S(1)} collective-permute-done((bf16[64,3712]{1,0:T(8,128)(2,1)S(1)}, bf16[64,3712]{1,0:T(8,128)(2,1)S(1)}, u32[]{:S(2)}, u32[]{:S(2)}) %collective-permute-start.8) | collective-permute-done | bytes 475168 | tf_op jit(solution)/shard_map/ppermute | solution.py:96
  46.9 1.2 collective-permute-done.7.refs_8_
  48.3 0.6 collective-permute-start.9
  49.0 0.6 collective-permute-start.10
  49.5 4.5 %collective-permute-done.9.refs_10_ = bf16[16,3712]{1,0:T(8,128)(2,1)S(1)} collective-permute-done((bf16[16,3712]{1,0:T(8,128)(2,1)S(1)}, bf16[16,3712]{1,0:T(8,128)(2,1)S(1)}, u32[]{:S(2)}, u32[]{:S(2)}) %collective-permute-start.9) | collective-permute-done | bytes 118816 | tf_op jit(solution)/shard_map/ppermute | solution.py:96
  54.0 0.3 collective-permute-done.10.refs_11_
  54.5 0.5 collective-permute-start.31
  55.0 1.0 collective-permute-done.14.refs_16_
  56.0 0.9 copy-done.23
  57.0 0.5 copy-done.18
  57.5 27.6 %shard_map.107 = (bf16[160,3584]{1,0:T(8,128)(2,1)}, bf16[160,3584]{1,0:T(8,128)(2,1)}, bf16[160,3584]{1,0:T(8,128)(2,1)}, bf16[32,3584]{1,0:T(8,128)(2,1)}, bf1...) custom-call(s32[2]{0:T(128)} %copy-done.6, ...), custom_call_target="tpu_custom_call", output_to_operand_aliasing={{8}: (21, {}), {9}: (22, {}), {10}: (23, {})} | custom-call | flops 11274289152 | bytes 88080384 | tf_op jit(solution)/shard_map/pallas_call | solution.py:468
  85.1 0.2 collective-permute-start.17
  85.3 0.1 fusion.18
  85.4 0.4 collective-permute-start.18
  85.9 0.2 collective-permute-start.15
  86.2 0.4 collective-permute-start.16
  86.5 2.0 %collective-permute-done.18 = bf16[32,3584]{1,0:T(8,128)(2,1)S(1)} collective-permute-done((bf16[32,3584]{1,0:T(8,128)(2,1)}, bf16[32,3584]{1,0:T(8,128)(2,1)S(1)}, u32[]{:S(2)}, u32[]{:S(2)}) %collective-permute-start.18) | collective-permute-done | bytes 229408 | tf_op jit(solution)/shard_map/ppermute | solution.py:68
  88.5 1.0 add_convert_fusion.9
  89.5 0.6 collective-permute-start.22
  90.1 1.5 %collective-permute-start.19 = (bf16[16,3584]{1,0:T(8,128)(2,1)S(1)}, bf16[16,3584]{1,0:T(8,128)(2,1)S(1)}, u32[]{:S(2)}, u32[]{:S(2)}) collective-permute-start(bf16[16,3584]{1,0:T(8,128)(2,1)S(1)} %get-tuple-element.59), channel_id=1, source_target_pairs={{0,1},{1,0},{2,3},{3,2},{4,5},{5,4},{6,7},{7,6},{8,9},{9,8},{10,11... | collective-permute-start | bytes 344072 | tf_op jit(solution)/shard_map/ppermute | solution.py:96
  91.6 1.1 add_convert_fusion
  92.6 2.1 %collective-permute-done.22 = bf16[16,3584]{1,0:T(8,128)(2,1)S(1)} collective-permute-done((bf16[16,3584]{1,0:T(8,128)(2,1)S(1)}, bf16[16,3584]{1,0:T(8,128)(2,1)S(1)}, u32[]{:S(2)}, u32[]{:S(2)}) %collective-permute-start.22) | collective-permute-done | bytes 114720 | tf_op jit(solution)/shard_map/ppermute | solution.py:96
  94.8 0.2 collective-permute-done.19
  95.0 0.1 add_convert_fusion.8
  95.2 1.6 %collective-permute-start.23 = (bf16[64,3584]{1,0:T(8,128)(2,1)S(1)}, bf16[64,3584]{1,0:T(8,128)(2,1)S(1)}, u32[]{:S(2)}, u32[]{:S(2)}) collective-permute-start(bf16[64,3584]{1,0:T(8,128)(2,1)S(1)} %pad_maximum_fusion.10), channel_id=1, source_target_pairs={{0,1},{1,0},{2,3},{3,2},{4,5},{5,4},{6,7},{7,6},{8,9},{9,8},{10,11... | collective-permute-start | bytes 1376264 | tf_op jit(solution)/shard_map/ppermute | solution.py:96
  96.8 1.6 %collective-permute-start.20 = (bf16[64,3584]{1,0:T(8,128)(2,1)S(1)}, bf16[64,3584]{1,0:T(8,128)(2,1)S(1)}, u32[]{:S(2)}, u32[]{:S(2)}) collective-permute-start(bf16[64,3584]{1,0:T(8,128)(2,1)S(1)} %pad_maximum_fusion.9), channel_id=1, source_target_pairs={{0,2},{1,3},{2,0},{3,1},{4,6},{5,7},{6,4},{7,5},{8,10},{9,11},{10,... | collective-permute-start | bytes 1376264 | tf_op jit(solution)/shard_map/ppermute | solution.py:96
  98.5 9.6 %collective-permute-done.20 = bf16[64,3584]{1,0:T(8,128)(2,1)S(1)} collective-permute-done((bf16[64,3584]{1,0:T(8,128)(2,1)S(1)}, bf16[64,3584]{1,0:T(8,128)(2,1)S(1)}, u32[]{:S(2)}, u32[]{:S(2)}) %collective-permute-start.20) | collective-permute-done | bytes 458784 | tf_op jit(solution)/shard_map/ppermute | solution.py:96
  108.4 0.6 collective-permute-start.21
  109.2 1.5 %collective-permute-start.24 = (bf16[80,3584]{1,0:T(8,128)(2,1)S(1)}, bf16[80,3584]{1,0:T(8,128)(2,1)S(1)}, u32[]{:S(2)}, u32[]{:S(2)}) collective-permute-start(bf16[80,3584]{1,0:T(8,128)(2,1)S(1)} %fusion.13), channel_id=1, source_target_pairs={{0,2},{1,3},{2,0},{3,1},{4,6},{5,7},{6,4},{7,5},{8,10},{9,11},{10,... | collective-permute-start | bytes 1720328 | tf_op jit(solution)/shard_map/ppermute | solution.py:96
  110.8 2.7 %collective-permute-start.27 = (bf16[32,3584]{1,0:T(8,128)(2,1)S(1)}, bf16[32,3584]{1,0:T(8,128)(2,1)S(1)}, u32[]{:S(2)}, u32[]{:S(2)}) collective-permute-start(bf16[32,3584]{1,0:T(8,128)(2,1)S(1)} %fusion.2), channel_id=1, source_target_pairs={{0,8},{1,9},{2,10},{3,11},{4,12},{5,13},{6,14},{7,15},{8,0},{9,1},... | collective-permute-start | bytes 688136 | tf_op jit(solution)/shard_map/ppermute | solution.py:96
  113.4 7.8 %collective-permute-done.21 = bf16[80,3584]{1,0:T(8,128)(2,1)S(1)} collective-permute-done((bf16[80,3584]{1,0:T(8,128)(2,1)S(1)}, bf16[80,3584]{1,0:T(8,128)(2,1)S(1)}, u32[]{:S(2)}, u32[]{:S(2)}) %collective-permute-start.21) | collective-permute-done | bytes 573472 | tf_op jit(solution)/shard_map/ppermute | solution.py:96
  121.3 0.4 collective-permute-done.24
  121.8 0.7 copy-done.19
  122.6 0.1 fusion.6
  122.7 1.4 %collective-permute-start.29 = (bf16[32,3584]{1,0:T(8,128)(2,1)S(1)}, bf16[32,3584]{1,0:T(8,128)(2,1)S(1)}, u32[]{:S(2)}, u32[]{:S(2)}) collective-permute-start(bf16[32,3584]{1,0:T(8,128)(2,1)S(1)} %pad_maximum_fusion.13), channel_id=1, source_target_pairs={{0,2},{1,3},{2,0},{3,1},{4,6},{5,7},{6,4},{7,5},{8,10},{9,11},{10,... | collective-permute-start | bytes 688136 | tf_op jit(solution)/shard_map/ppermute | solution.py:96
  124.1 0.2 fusion.4
  124.3 3.5 %collective-permute-start.25 = (bf16[32,3584]{1,0:T(8,128)(2,1)S(1)}, bf16[32,3584]{1,0:T(8,128)(2,1)S(1)}, u32[]{:S(2)}, u32[]{:S(2)}) collective-permute-start(bf16[32,3584]{1,0:T(8,128)(2,1)S(1)} %get-tuple-element.40), channel_id=1, source_target_pairs={{0,12},{1,13},{2,14},{3,15},{4,0},{5,1},{6,2},{7,3},{8,4},{9,5},{1... | collective-permute-start | bytes 688136 | tf_op jit(solution)/shard_map/ppermute | solution.py:96
  127.8 0.8 collective-permute-start.28
  128.6 4.0 %collective-permute-done.25 = bf16[32,3584]{1,0:T(8,128)(2,1)S(1)} collective-permute-done((bf16[32,3584]{1,0:T(8,128)(2,1)S(1)}, bf16[32,3584]{1,0:T(8,128)(2,1)S(1)}, u32[]{:S(2)}, u32[]{:S(2)}) %collective-permute-start.25) | collective-permute-done | bytes 229408 | tf_op jit(solution)/shard_map/ppermute | solution.py:96
  132.7 2.9 %collective-permute-done.26 = bf16[32,3584]{1,0:T(8,128)(2,1)S(1)} collective-permute-done((bf16[32,3584]{1,0:T(8,128)(2,1)S(1)}, bf16[32,3584]{1,0:T(8,128)(2,1)S(1)}, u32[]{:S(2)}, u32[]{:S(2)}) %collective-permute-start.26) | collective-permute-done | bytes 229408 | tf_op jit(solution)/shard_map/ppermute | solution.py:96
  135.6 0.1 convert_add_fusion
  135.9 0.2 slice_reduce_fusion
  136.1 0.7 fusion.16
  136.8 0.6 collective-permute-done.30.other_ref
  137.4 1.3 shard_map.108
  (103 shorter events, 2.1 us)
Async XLA Ops:
  0.7 15.6 %copy-start.6 = (s32[2]{0:T(128)}, s32[2]{0:T(128)S(1)}, u32[]{:S(2)}) copy-start(s32[2]{0:T(128)S(1)} %pad_add_fusion.here_ref) | copy-start | bytes 28
  2.4 0.7 copy-start.4
  3.1 19.2 %copy-start.3 = (bf16[32,3712]{1,0:T(8,128)(2,1)}, bf16[32,3712]{1,0:T(8,128)(2,1)S(1)}, u32[]{:S(2)}) copy-start(bf16[32,3712]{1,0:T(8,128)(2,1)S(1)} %get-tuple-element.22.refs_0_) | copy-start | bytes 712708
  3.1 13.2 %collective-permute-start.1 = (bf16[32,3712]{1,0:T(8,128)(2,1)S(1)}, bf16[32,3712]{1,0:T(8,128)(2,1)S(1)}, u32[]{:S(2)}, u32[]{:S(2)}) collective-permute-start(bf16[32,3712]{1,0:T(8,128)(2,1)S(1)} %get-tuple-element.22.refs_0_), channel_id=1, source_target_pairs={{0,2},{1,3},{2,0},{3,1},{4,6},{5,7},{6,4},{7,5},{8,10},{9,11},{10,... | collective-permute-start | bytes 712712 | tf_op jit(solution)/shard_map/ppermute | solution.py:96
  6.1 10.3 %collective-permute-start = (bf16[32,3712]{1,0:T(8,128)(2,1)S(1)}, bf16[32,3712]{1,0:T(8,128)(2,1)S(1)}, u32[]{:S(2)}, u32[]{:S(2)}) collective-permute-start(bf16[32,3712]{1,0:T(8,128)(2,1)S(1)} %get-tuple-element.22.refs_0_), channel_id=1, source_target_pairs={{0,1},{1,0},{2,3},{3,2},{4,5},{5,4},{6,7},{7,6},{8,9},{9,8},{10,11... | collective-permute-start | bytes 712712 | tf_op jit(solution)/shard_map/ppermute | solution.py:96
  7.5 9.8 %collective-permute-start.3 = (bf16[32,3712]{1,0:T(8,128)(2,1)S(1)}, bf16[32,3712]{1,0:T(8,128)(2,1)S(1)}, u32[]{:S(2)}, u32[]{:S(2)}) collective-permute-start(bf16[32,3712]{1,0:T(8,128)(2,1)S(1)} %get-tuple-element.22.refs_0_), channel_id=1, source_target_pairs={{0,12},{1,13},{2,14},{3,15},{4,0},{5,1},{6,2},{7,3},{8,4},{9,5},{1... | collective-permute-start | bytes 712712 | tf_op jit(solution)/shard_map/ppermute | solution.py:96
  11.1 10.5 %collective-permute-start.2 = (bf16[32,3712]{1,0:T(8,128)(2,1)S(1)}, bf16[32,3712]{1,0:T(8,128)(2,1)S(1)}, u32[]{:S(2)}, u32[]{:S(2)}) collective-permute-start(bf16[32,3712]{1,0:T(8,128)(2,1)S(1)} %get-tuple-element.22.refs_0_), channel_id=1, source_target_pairs={{0,4},{1,5},{2,6},{3,7},{4,8},{5,9},{6,10},{7,11},{8,12},{9,13},{1... | collective-permute-start | bytes 712712 | tf_op jit(solution)/shard_map/ppermute | solution.py:96
  11.8 1.7 %copy-start = (bf16[1,2048,576]{1,2,0:T(8,128)(2,1)S(1)}, bf16[1,2048,576]{1,2,0:T(8,128)(2,1)}, u32[]{:S(2)}) copy-start(bf16[1,2048,576]{1,2,0:T(8,128)(2,1)} %param.16) | copy-start | bytes 7077892
  13.5 0.9 copy-start.5
  16.3 5.4 %copy-start.1 = (f32[32,640]{1,0:T(8,128)}, f32[32,640]{1,0:T(8,128)S(1)}, u32[]{:S(2)}) copy-start(f32[32,640]{1,0:T(8,128)S(1)} %get-tuple-element.23) | copy-start | bytes 245764
  16.3 23.0 %copy-start.16 = (bf16[32,3712]{1,0:T(8,128)(2,1)}, bf16[32,3712]{1,0:T(8,128)(2,1)S(1)}, u32[]{:S(2)}) copy-start(bf16[32,3712]{1,0:T(8,128)(2,1)S(1)} %collective-permute-done.1.refs_2_) | copy-start | bytes 712708
  16.4 23.0 %copy-start.17 = (bf16[32,3712]{1,0:T(8,128)(2,1)}, bf16[32,3712]{1,0:T(8,128)(2,1)S(1)}, u32[]{:S(2)}) copy-start(bf16[32,3712]{1,0:T(8,128)(2,1)S(1)} %collective-permute-done.refs_1_) | copy-start | bytes 712708
  17.4 4.3 %copy-start.8 = (bf16[32,3712]{1,0:T(8,128)(2,1)}, bf16[32,3712]{1,0:T(8,128)(2,1)S(1)}, u32[]{:S(2)}) copy-start(bf16[32,3712]{1,0:T(8,128)(2,1)S(1)} %collective-permute-done.3._.refs_4_) | copy-start | bytes 712708
  21.6 17.7 %copy-start.15 = (bf16[32,3712]{1,0:T(8,128)(2,1)}, bf16[32,3712]{1,0:T(8,128)(2,1)S(1)}, u32[]{:S(2)}) copy-start(bf16[32,3712]{1,0:T(8,128)(2,1)S(1)} %collective-permute-done.2.refs_3_) | copy-start | bytes 712708
  21.7 14.1 %collective-permute-start.5 = (bf16[80,3712]{1,0:T(8,128)(2,1)S(1)}, bf16[80,3712]{1,0:T(8,128)(2,1)S(1)}, u32[]{:S(2)}, u32[]{:S(2)}) collective-permute-start(bf16[80,3712]{1,0:T(8,128)(2,1)S(1)} %get-tuple-element.56), channel_id=1, source_target_pairs={{0,2},{1,3},{2,0},{3,1},{4,6},{5,7},{6,4},{7,5},{8,10},{9,11},{10,... | collective-permute-start | bytes 1781768 | tf_op jit(solution)/shard_map/ppermute | solution.py:96
  22.3 12.5 %collective-permute-start.6 = (bf16[32,3712]{1,0:T(8,128)(2,1)S(1)}, bf16[32,3712]{1,0:T(8,128)(2,1)S(1)}, u32[]{:S(2)}, u32[]{:S(2)}) collective-permute-start(bf16[32,3712]{1,0:T(8,128)(2,1)S(1)} %get-tuple-element.22.refs_0_), channel_id=1, source_target_pairs={{0,8},{1,9},{2,10},{3,11},{4,12},{5,13},{6,14},{7,15},{8,0},{9,1},... | collective-permute-start | bytes 712712 | tf_op jit(solution)/shard_map/ppermute | solution.py:96
  23.0 12.9 %collective-permute-start.4 = (bf16[80,3712]{1,0:T(8,128)(2,1)S(1)}, bf16[80,3712]{1,0:T(8,128)(2,1)S(1)}, u32[]{:S(2)}, u32[]{:S(2)}) collective-permute-start(bf16[80,3712]{1,0:T(8,128)(2,1)S(1)} %get-tuple-element.57), channel_id=1, source_target_pairs={{0,1},{1,0},{2,3},{3,2},{4,5},{5,4},{6,7},{7,6},{8,9},{9,8},{10,11... | collective-permute-start | bytes 1781768 | tf_op jit(solution)/shard_map/ppermute | solution.py:96
  35.8 3.3 %copy-start.10 = (bf16[32,3712]{1,0:T(8,128)(2,1)}, bf16[32,3712]{1,0:T(8,128)(2,1)S(1)}, u32[]{:S(2)}) copy-start(bf16[32,3712]{1,0:T(8,128)(2,1)S(1)} %add.140.refs_7_) | copy-start | bytes 712708
  35.9 3.3 %copy-start.11 = (bf16[80,3712]{1,0:T(8,128)(2,1)}, bf16[80,3712]{1,0:T(8,128)(2,1)S(1)}, u32[]{:S(2)}) copy-start(bf16[80,3712]{1,0:T(8,128)(2,1)S(1)} %collective-permute-done.5.refs_6_) | copy-start | bytes 1781764
  35.9 3.3 %copy-start.12 = (bf16[80,3712]{1,0:T(8,128)(2,1)}, bf16[80,3712]{1,0:T(8,128)(2,1)S(1)}, u32[]{:S(2)}) copy-start(bf16[80,3712]{1,0:T(8,128)(2,1)S(1)} %collective-permute-done.4.refs_5_) | copy-start | bytes 1781764
  36.0 10.9 %collective-permute-start.8 = (bf16[64,3712]{1,0:T(8,128)(2,1)S(1)}, bf16[64,3712]{1,0:T(8,128)(2,1)S(1)}, u32[]{:S(2)}, u32[]{:S(2)}) collective-permute-start(bf16[64,3712]{1,0:T(8,128)(2,1)S(1)} %get-tuple-element.60), channel_id=1, source_target_pairs={{0,2},{1,3},{2,0},{3,1},{4,6},{5,7},{6,4},{7,5},{8,10},{9,11},{10,... | collective-permute-start | bytes 1425416 | tf_op jit(solution)/shard_map/ppermute | solution.py:96
  37.6 1.7 %copy-start.9 = (bf16[32,3712]{1,0:T(8,128)(2,1)S(1)}, bf16[32,3712]{1,0:T(8,128)(2,1)}, u32[]{:S(2)}) copy-start(bf16[32,3712]{1,0:T(8,128)(2,1)} %copy-done.8) | copy-start | bytes 712708
  37.6 10.5 %collective-permute-start.7 = (bf16[64,3712]{1,0:T(8,128)(2,1)S(1)}, bf16[64,3712]{1,0:T(8,128)(2,1)S(1)}, u32[]{:S(2)}, u32[]{:S(2)}) collective-permute-start(bf16[64,3712]{1,0:T(8,128)(2,1)S(1)} %get-tuple-element.61), channel_id=1, source_target_pairs={{0,1},{1,0},{2,3},{3,2},{4,5},{5,4},{6,7},{7,6},{8,9},{9,8},{10,11... | collective-permute-start | bytes 1425416 | tf_op jit(solution)/shard_map/ppermute | solution.py:96
  39.3 16.7 %collective-permute-start.12 = (bf16[192,3712]{1,0:T(8,128)(2,1)S(1)}, bf16[192,3712]{1,0:T(8,128)(2,1)S(1)}, u32[]{:S(2)}, u32[]{:S(2)}) collective-permute-start(bf16[192,3712]{1,0:T(8,128)(2,1)S(1)} %pad_maximum_fusion), channel_id=1, source_target_pairs={{0,16},{16,0},{1,17},{17,1},{2,18},{18,2},{3,19},{19,3},{4,20},{20... | collective-permute-start | bytes 4276232 | tf_op jit(solution)/shard_map/ppermute | solution.py:68
  39.5 15.5 %collective-permute-start.11 = (bf16[128,3712]{1,0:T(8,128)(2,1)S(1)}, bf16[128,3712]{1,0:T(8,128)(2,1)S(1)}, u32[]{:S(2)}, u32[]{:S(2)}) collective-permute-start(bf16[128,3712]{1,0:T(8,128)(2,1)S(1)} %pad_maximum_fusion.1), channel_id=1, source_target_pairs={{0,16},{16,0},{1,17},{17,1},{2,18},{18,2},{3,19},{19,3},{4,20},{20... | collective-permute-start | bytes 2850824 | tf_op jit(solution)/shard_map/ppermute | solution.py:68
  46.9 2.0 %copy-start.13 = (bf16[64,3712]{1,0:T(8,128)(2,1)}, bf16[64,3712]{1,0:T(8,128)(2,1)S(1)}, u32[]{:S(2)}) copy-start(bf16[64,3712]{1,0:T(8,128)(2,1)S(1)} %collective-permute-done.8.refs_9_) | copy-start | bytes 1425412
  48.2 0.8 copy-start.14
  48.2 7.7 %collective-permute-start.13 = (bf16[128,3712]{1,0:T(8,128)(2,1)S(1)}, bf16[128,3712]{1,0:T(8,128)(2,1)S(1)}, u32[]{:S(2)}, u32[]{:S(2)}) collective-permute-start(bf16[128,3712]{1,0:T(8,128)(2,1)S(1)} %pad_maximum_fusion.2), channel_id=1, source_target_pairs={{0,16},{16,0},{1,17},{17,1},{2,18},{18,2},{3,19},{19,3},{4,20},{20... | collective-permute-start | bytes 2850824 | tf_op jit(solution)/shard_map/ppermute | solution.py:68
  48.3 5.7 %collective-permute-start.9 = (bf16[16,3712]{1,0:T(8,128)(2,1)S(1)}, bf16[16,3712]{1,0:T(8,128)(2,1)S(1)}, u32[]{:S(2)}, u32[]{:S(2)}) collective-permute-start(bf16[16,3712]{1,0:T(8,128)(2,1)S(1)} %slice.294), channel_id=1, source_target_pairs={{0,1},{1,0},{2,3},{3,2},{4,5},{5,4},{6,7},{7,6},{8,9},{9,8},{10,11... | collective-permute-start | bytes 356360 | tf_op jit(solution)/shard_map/ppermute | solution.py:96
  49.0 5.4 %collective-permute-start.10 = (bf16[16,3712]{1,0:T(8,128)(2,1)S(1)}, bf16[16,3712]{1,0:T(8,128)(2,1)S(1)}, u32[]{:S(2)}, u32[]{:S(2)}) collective-permute-start(bf16[16,3712]{1,0:T(8,128)(2,1)S(1)} %slice.295), channel_id=1, source_target_pairs={{0,2},{1,3},{2,0},{3,1},{4,6},{5,7},{6,4},{7,5},{8,10},{9,11},{10,... | collective-permute-start | bytes 356360 | tf_op jit(solution)/shard_map/ppermute | solution.py:96
  54.0 2.9 %copy-start.24 = (bf16[16,3712]{1,0:T(8,128)(2,1)}, bf16[16,3712]{1,0:T(8,128)(2,1)S(1)}, u32[]{:S(2)}) copy-start(bf16[16,3712]{1,0:T(8,128)(2,1)S(1)} %collective-permute-done.9.refs_10_) | copy-start | bytes 356356
  54.4 2.6 %copy-start.25 = (bf16[16,3712]{1,0:T(8,128)(2,1)}, bf16[16,3712]{1,0:T(8,128)(2,1)S(1)}, u32[]{:S(2)}) copy-start(bf16[16,3712]{1,0:T(8,128)(2,1)S(1)} %collective-permute-done.10.refs_11_) | copy-start | bytes 356356
  54.4 1.6 %collective-permute-start.14 = (bf16[32,3712]{1,0:T(8,128)(2,1)S(1)}, bf16[32,3712]{1,0:T(8,128)(2,1)S(1)}, u32[]{:S(2)}, u32[]{:S(2)}) collective-permute-start(bf16[32,3712]{1,0:T(8,128)(2,1)S(1)} %pad_maximum_fusion.11), channel_id=1, source_target_pairs={{0,16},{16,0},{1,17},{17,1},{2,18},{18,2},{3,19},{19,3},{4,20},{20... | collective-permute-start | bytes 712712 | tf_op jit(solution)/shard_map/ppermute | solution.py:68
  54.5 30.8 %collective-permute-start.31 = (f32[1,32,640]{2,1,0:T(8,128)S(1)}, f32[1,32,640]{2,1,0:T(8,128)S(1)}, u32[]{:S(2)}, u32[]{:S(2)}) collective-permute-start(f32[1,32,640]{2,1,0:T(8,128)S(1)} %bitcast.16), channel_id=1, source_target_pairs={{0,16},{16,0},{1,17},{17,1},{2,18},{18,2},{3,19},{19,3},{4,20},{20... | collective-permute-start | bytes 245768 | tf_op jit(solution)/shard_map/ppermute | solution.py:68
  55.0 2.0 %copy-start.22 = (bf16[128,3712]{1,0:T(8,128)(2,1)}, bf16[128,3712]{1,0:T(8,128)(2,1)S(1)}, u32[]{:S(2)}) copy-start(bf16[128,3712]{1,0:T(8,128)(2,1)S(1)} %collective-permute-done.11.refs_13_) | copy-start | bytes 2850820
  56.0 1.0 copy-start.26
  56.0 1.0 copy-start.23
  56.0 1.5 %copy-start.18 = (bf16[192,3712]{1,0:T(8,128)(2,1)}, bf16[192,3712]{1,0:T(8,128)(2,1)S(1)}, u32[]{:S(2)}) copy-start(bf16[192,3712]{1,0:T(8,128)(2,1)S(1)} %collective-permute-done.12.refs_14_) | copy-start | bytes 4276228
  57.5 27.8 %copy-start.2 = (f32[32,640]{1,0:T(8,128)S(1)}, f32[32,640]{1,0:T(8,128)}, u32[]{:S(2)}) copy-start(f32[32,640]{1,0:T(8,128)} %copy-done.1) | copy-start | bytes 245764
  85.1 9.9 %copy-start.20 = (bf16[160,3584]{1,0:T(8,128)(2,1)S(1)}, bf16[160,3584]{1,0:T(8,128)(2,1)}, u32[]{:S(2)}) copy-start(bf16[160,3584]{1,0:T(8,128)(2,1)} %get-tuple-element.33) | copy-start | bytes 3440644
  85.1 6.5 %collective-permute-start.17 = (bf16[160,3584]{1,0:T(8,128)(2,1)}, bf16[160,3584]{1,0:T(8,128)(2,1)S(1)}, u32[]{:S(2)}, u32[]{:S(2)}) collective-permute-start(bf16[160,3584]{1,0:T(8,128)(2,1)} %get-tuple-element.34), channel_id=1, source_target_pairs={{0,16},{16,0},{1,17},{17,1},{2,18},{18,2},{3,19},{19,3},{4,20},{20... | collective-permute-start | bytes 3440648 | tf_op jit(solution)/shard_map/ppermute | solution.py:68
  85.4 3.1 %collective-permute-start.18 = (bf16[32,3584]{1,0:T(8,128)(2,1)}, bf16[32,3584]{1,0:T(8,128)(2,1)S(1)}, u32[]{:S(2)}, u32[]{:S(2)}) collective-permute-start(bf16[32,3584]{1,0:T(8,128)(2,1)} %get-tuple-element.36), channel_id=1, source_target_pairs={{0,16},{16,0},{1,17},{17,1},{2,18},{18,2},{3,19},{19,3},{4,20},{20... | collective-permute-start | bytes 688136 | tf_op jit(solution)/shard_map/ppermute | solution.py:68
  85.9 35.9 %collective-permute-start.15 = (bf16[160,3584]{1,0:T(8,128)(2,1)}, bf16[160,3584]{1,0:T(8,128)(2,1)S(1)}, u32[]{:S(2)}, u32[]{:S(2)}) collective-permute-start(bf16[160,3584]{1,0:T(8,128)(2,1)} %get-tuple-element.30), channel_id=1, source_target_pairs={{0,16},{16,0},{1,17},{17,1},{2,18},{18,2},{3,19},{19,3},{4,20},{20... | collective-permute-start | bytes 3440648 | tf_op jit(solution)/shard_map/ppermute | solution.py:68
  86.2 12.2 %collective-permute-start.16 = (bf16[160,3584]{1,0:T(8,128)(2,1)}, bf16[160,3584]{1,0:T(8,128)(2,1)S(1)}, u32[]{:S(2)}, u32[]{:S(2)}) collective-permute-start(bf16[160,3584]{1,0:T(8,128)(2,1)} %get-tuple-element.32), channel_id=1, source_target_pairs={{0,16},{16,0},{1,17},{17,1},{2,18},{18,2},{3,19},{19,3},{4,20},{20... | collective-permute-start | bytes 3440648 | tf_op jit(solution)/shard_map/ppermute | solution.py:68
  89.5 5.3 %collective-permute-start.22 = (bf16[16,3584]{1,0:T(8,128)(2,1)S(1)}, bf16[16,3584]{1,0:T(8,128)(2,1)S(1)}, u32[]{:S(2)}, u32[]{:S(2)}) collective-permute-start(bf16[16,3584]{1,0:T(8,128)(2,1)S(1)} %get-tuple-element.58), channel_id=1, source_target_pairs={{0,2},{1,3},{2,0},{3,1},{4,6},{5,7},{6,4},{7,5},{8,10},{9,11},{10,... | collective-permute-start | bytes 344072 | tf_op jit(solution)/shard_map/ppermute | solution.py:96
  90.1 4.9 %collective-permute-start.19 = (bf16[16,3584]{1,0:T(8,128)(2,1)S(1)}, bf16[16,3584]{1,0:T(8,128)(2,1)S(1)}, u32[]{:S(2)}, u32[]{:S(2)}) collective-permute-start(bf16[16,3584]{1,0:T(8,128)(2,1)S(1)} %get-tuple-element.59), channel_id=1, source_target_pairs={{0,1},{1,0},{2,3},{3,2},{4,5},{5,4},{6,7},{7,6},{8,9},{9,8},{10,11... | collective-permute-start | bytes 344072 | tf_op jit(solution)/shard_map/ppermute | solution.py:96
  95.1 3.3 %copy-start.21 = (bf16[160,3584]{1,0:T(8,128)(2,1)S(1)}, bf16[160,3584]{1,0:T(8,128)(2,1)}, u32[]{:S(2)}) copy-start(bf16[160,3584]{1,0:T(8,128)(2,1)} %get-tuple-element.31) | copy-start | bytes 3440644
  95.2 13.8 %collective-permute-start.23 = (bf16[64,3584]{1,0:T(8,128)(2,1)S(1)}, bf16[64,3584]{1,0:T(8,128)(2,1)S(1)}, u32[]{:S(2)}, u32[]{:S(2)}) collective-permute-start(bf16[64,3584]{1,0:T(8,128)(2,1)S(1)} %pad_maximum_fusion.10), channel_id=1, source_target_pairs={{0,1},{1,0},{2,3},{3,2},{4,5},{5,4},{6,7},{7,6},{8,9},{9,8},{10,11... | collective-permute-start | bytes 1376264 | tf_op jit(solution)/shard_map/ppermute | solution.py:96
  96.8 11.3 %collective-permute-start.20 = (bf16[64,3584]{1,0:T(8,128)(2,1)S(1)}, bf16[64,3584]{1,0:T(8,128)(2,1)S(1)}, u32[]{:S(2)}, u32[]{:S(2)}) collective-permute-start(bf16[64,3584]{1,0:T(8,128)(2,1)S(1)} %pad_maximum_fusion.9), channel_id=1, source_target_pairs={{0,2},{1,3},{2,0},{3,1},{4,6},{5,7},{6,4},{7,5},{8,10},{9,11},{10,... | collective-permute-start | bytes 1376264 | tf_op jit(solution)/shard_map/ppermute | solution.py:96
  108.4 12.8 %collective-permute-start.21 = (bf16[80,3584]{1,0:T(8,128)(2,1)S(1)}, bf16[80,3584]{1,0:T(8,128)(2,1)S(1)}, u32[]{:S(2)}, u32[]{:S(2)}) collective-permute-start(bf16[80,3584]{1,0:T(8,128)(2,1)S(1)} %pad_maximum_fusion.6), channel_id=1, source_target_pairs={{0,1},{1,0},{2,3},{3,2},{4,5},{5,4},{6,7},{7,6},{8,9},{9,8},{10,11... | collective-permute-start | bytes 1720328 | tf_op jit(solution)/shard_map/ppermute | solution.py:96
  109.2 12.6 %collective-permute-start.24 = (bf16[80,3584]{1,0:T(8,128)(2,1)S(1)}, bf16[80,3584]{1,0:T(8,128)(2,1)S(1)}, u32[]{:S(2)}, u32[]{:S(2)}) collective-permute-start(bf16[80,3584]{1,0:T(8,128)(2,1)S(1)} %fusion.13), channel_id=1, source_target_pairs={{0,2},{1,3},{2,0},{3,1},{4,6},{5,7},{6,4},{7,5},{8,10},{9,11},{10,... | collective-permute-start | bytes 1720328 | tf_op jit(solution)/shard_map/ppermute | solution.py:96
  110.8 17.9 %collective-permute-start.27 = (bf16[32,3584]{1,0:T(8,128)(2,1)S(1)}, bf16[32,3584]{1,0:T(8,128)(2,1)S(1)}, u32[]{:S(2)}, u32[]{:S(2)}) collective-permute-start(bf16[32,3584]{1,0:T(8,128)(2,1)S(1)} %fusion.2), channel_id=1, source_target_pairs={{0,8},{1,9},{2,10},{3,11},{4,12},{5,13},{6,14},{7,15},{8,0},{9,1},... | collective-permute-start | bytes 688136 | tf_op jit(solution)/shard_map/ppermute | solution.py:96
  121.3 1.3 copy-start.19
  122.7 13.0 %collective-permute-start.29 = (bf16[32,3584]{1,0:T(8,128)(2,1)S(1)}, bf16[32,3584]{1,0:T(8,128)(2,1)S(1)}, u32[]{:S(2)}, u32[]{:S(2)}) collective-permute-start(bf16[32,3584]{1,0:T(8,128)(2,1)S(1)} %pad_maximum_fusion.13), channel_id=1, source_target_pairs={{0,2},{1,3},{2,0},{3,1},{4,6},{5,7},{6,4},{7,5},{8,10},{9,11},{10,... | collective-permute-start | bytes 688136 | tf_op jit(solution)/shard_map/ppermute | solution.py:96
  124.3 8.4 %collective-permute-start.25 = (bf16[32,3584]{1,0:T(8,128)(2,1)S(1)}, bf16[32,3584]{1,0:T(8,128)(2,1)S(1)}, u32[]{:S(2)}, u32[]{:S(2)}) collective-permute-start(bf16[32,3584]{1,0:T(8,128)(2,1)S(1)} %get-tuple-element.40), channel_id=1, source_target_pairs={{0,12},{1,13},{2,14},{3,15},{4,0},{5,1},{6,2},{7,3},{8,4},{9,5},{1... | collective-permute-start | bytes 688136 | tf_op jit(solution)/shard_map/ppermute | solution.py:96
  127.8 7.8 %collective-permute-start.26 = (bf16[32,3584]{1,0:T(8,128)(2,1)S(1)}, bf16[32,3584]{1,0:T(8,128)(2,1)S(1)}, u32[]{:S(2)}, u32[]{:S(2)}) collective-permute-start(bf16[32,3584]{1,0:T(8,128)(2,1)S(1)} %get-tuple-element.41), channel_id=1, source_target_pairs={{0,4},{1,5},{2,6},{3,7},{4,8},{5,9},{6,10},{7,11},{8,12},{9,13},{1... | collective-permute-start | bytes 688136 | tf_op jit(solution)/shard_map/ppermute | solution.py:96
  127.8 9.6 %copy-start.7 = (s32[2]{0:T(128)S(1)}, s32[2]{0:T(128)}, u32[]{:S(2)}) copy-start(s32[2]{0:T(128)} %copy-done.6) | copy-start | bytes 28
  127.8 7.9 %collective-permute-start.28 = (bf16[32,3584]{1,0:T(8,128)(2,1)S(1)}, bf16[32,3584]{1,0:T(8,128)(2,1)S(1)}, u32[]{:S(2)}, u32[]{:S(2)}) collective-permute-start(bf16[32,3584]{1,0:T(8,128)(2,1)S(1)} %pad_maximum_fusion.12), channel_id=1, source_target_pairs={{0,1},{1,0},{2,3},{3,2},{4,5},{5,4},{6,7},{7,6},{8,9},{9,8},{10,11... | collective-permute-start | bytes 688136 | tf_op jit(solution)/shard_map/ppermute | solution.py:96
  135.8 1.6 %collective-permute-start.30 = (bf16[32,3584]{1,0:T(8,128)(2,1)S(1)}, bf16[32,3584]{1,0:T(8,128)(2,1)S(1)}, u32[]{:S(2)}, u32[]{:S(2)}) collective-permute-start(bf16[32,3584]{1,0:T(8,128)(2,1)S(1)} %add_convert_fusion.1.own_ref), channel_id=1, source_target_pairs={{0,16},{16,0},{1,17},{17,1},{2,18},{18,2},{3,19},{19,3},{4,20},{20... | collective-permute-start | bytes 688136 | tf_op jit(solution)/shard_map/ppermute | solution.py:68

commit v6 on v5

--- a/solution.py
+++ b/solution.py
@@ -437,7 +437,7 @@
     return pl.pallas_call(
         ahead_kernel,
         out_shape=[pltpu.VMEM((depth,) + w.shape[1:], w.dtype) for w in weights]
-        + [jax.ShapeDtypeStruct(follows[0].shape, follows[0].dtype)],
+        + [pltpu.VMEM(follows[0].shape, follows[0].dtype)],
         in_specs=[pl.BlockSpec(memory_space=pl.ANY)] * 5,
         out_specs=[pl.BlockSpec(memory_space=pltpu.VMEM)] * 4,
         scratch_shapes=[pltpu.SemaphoreType.DMA((3, depth))],
@@ -464,10 +464,13 @@
     else:
         out_rows = [own[0].shape[0]] * 2
     stages, copies = (group_count, 10 * group_count) if planes else (1, 2)
+    kinds = [
+        (pltpu.VMEM, pltpu.VMEM) if r < half else (jax.ShapeDtypeStruct, pl.ANY) for r in out_rows
+    ]
     weight_bytes = 3 * expert_count * width * hidden * 2
     sums = pl.pallas_call(
         functools.partial(expert_kernel, (planes, group_count, expert_count, width, top)),
-        out_shape=[jax.ShapeDtypeStruct((r, width), jnp.bfloat16) for r in out_rows]
+        out_shape=[out((r, width), jnp.bfloat16) for r, (out, _) in zip(out_rows, kinds)]
         + [pltpu.VMEM(w.shape, w.dtype) for w in ahead],
         input_output_aliases={
             1 + len(own) + len(other) + 3 + k: len(out_rows) + k for k in range(3)
@@ -475,7 +478,7 @@
         in_specs=[pl.BlockSpec(memory_space=pltpu.SMEM)]
         + [pl.BlockSpec(memory_space=pl.ANY)] * (len(own) + len(other) + 3)
         + [pl.BlockSpec(memory_space=pltpu.VMEM)] * 3,
-        out_specs=[pl.BlockSpec(memory_space=pl.ANY)] * len(out_rows)
+        out_specs=[pl.BlockSpec(memory_space=space) for _, space in kinds]
         + [pl.BlockSpec(memory_space=pltpu.VMEM)] * 3,
         scratch_shapes=[
             pltpu.VMEM((expert_count, slot_rows, width), jnp.bfloat16),

time: 139 us -> 138 us (level)
  waiting for transfers between devices: 48.9 us -> 50.9 us
  other arithmetic: 6.12 us -> 4.23 us
    ppermute x22, waiting for transfers between devices: 45.3 us -> 47.2 us  [send(): return lax.ppermute(x, 'ep', [(i, target(i)) for i in range(count)])]
  transfers between devices with their start and end apart: 32 -> 32, of which waited for: 16 -> 18; matrix products, arithmetic and copies ran while one was open for 4% -> 3% of each run, Pallas kernels for 29% -> 29%
where the time goes in v6:
time: 138 us; the launch traced here: 137 us
  waiting for transfers between devices  50.9 us (37%)
  Pallas kernels  43.5 us (32%)
  starting transfers between devices  31.2 us (23%)
  local copies, waits for them, and re-layouts  5.86 us (4%)
  other arithmetic  4.23 us (3%)
  between operations  1.79 us (1%)
    ppermute x22, waiting for transfers between devices, send(): return lax.ppermute(x, 'ep', [(i, target(i)) for i in range(count)])  47.2 us
    ppermute x22, starting transfers between devices, send(): return lax.ppermute(x, 'ep', [(i, target(i)) for i in range(count)])  28.8 us
    pallas_call x1, Pallas kernels, expert_sums(): pl.pallas_call(functools.partial(expert_kernel, (planes, group_count, exp...  28 us
    pallas_call x1, Pallas kernels, weights_ahead(): pl.pallas_call(ahead_kernel, out_shape=[pltpu.VMEM((depth,) + w.shape[1:]...  10.5 us
    unnamed x54, local copies, waits for them, and re-layouts  5.61 us
    ppermute x10, waiting for transfers between devices, swap_ctx(): return lax.ppermute(x, 'ctx', [(0, 1), (1, 0)])  3.68 us
  transfers between devices with their start and end apart: 32, of which 18 were waited for; matrix products, arithmetic and copies ran while one was open for 3% of the time, Pallas kernels for 29%

profile of v6, /device:TPU:0, one launch (start us, length us, event | category | flops | bytes accessed | tf_op | source)
XLA Modules:
  0.0 137.4 jit_solution(2609714707762312299)
XLA Ops:
  0.7 1.7 %shard_map.104 = (bf16[32,3712]{1,0:T(8,128)(2,1)S(1)}, bf16[32,3712]{1,0:T(8,128)(2,1)S(1)}) custom-call(s32[2]{0:T(128)S(1)} %pad_add_fusion.here_ref, bf16[64,3584]{1,0:T(8,128)(2,1)} %rows_hbm.1, s32[8,64]{1,0:T(8,128)} %bitcast.17, f32[8,64]{1,0:T(8,128)} %bitcast.18), custom_call_target="tpu_custom_call" | custom-call | tf_op jit(solution)/shard_map/pallas_call | solution.py:547
  2.4 0.7 copy-done.4
  3.1 3.0 %collective-permute-start.1 = (bf16[32,3712]{1,0:T(8,128)(2,1)S(1)}, bf16[32,3712]{1,0:T(8,128)(2,1)S(1)}, u32[]{:S(2)}, u32[]{:S(2)}) collective-permute-start(bf16[32,3712]{1,0:T(8,128)(2,1)S(1)} %get-tuple-element.22.refs_0_), channel_id=1, source_target_pairs={{0,2},{1,3},{2,0},{3,1},{4,6},{5,7},{6,4},{7,5},{8,10},{9,11},{10,... | collective-permute-start | bytes 712712 | tf_op jit(solution)/shard_map/ppermute | solution.py:96
  6.1 1.5 %collective-permute-start = (bf16[32,3712]{1,0:T(8,128)(2,1)S(1)}, bf16[32,3712]{1,0:T(8,128)(2,1)S(1)}, u32[]{:S(2)}, u32[]{:S(2)}) collective-permute-start(bf16[32,3712]{1,0:T(8,128)(2,1)S(1)} %get-tuple-element.22.refs_0_), channel_id=1, source_target_pairs={{0,1},{1,0},{2,3},{3,2},{4,5},{5,4},{6,7},{7,6},{8,9},{9,8},{10,11... | collective-permute-start | bytes 712712 | tf_op jit(solution)/shard_map/ppermute | solution.py:96
  7.5 3.6 %collective-permute-start.3 = (bf16[32,3712]{1,0:T(8,128)(2,1)S(1)}, bf16[32,3712]{1,0:T(8,128)(2,1)S(1)}, u32[]{:S(2)}, u32[]{:S(2)}) collective-permute-start(bf16[32,3712]{1,0:T(8,128)(2,1)S(1)} %get-tuple-element.22.refs_0_), channel_id=1, source_target_pairs={{0,12},{1,13},{2,14},{3,15},{4,0},{5,1},{6,2},{7,3},{8,4},{9,5},{1... | collective-permute-start | bytes 712712 | tf_op jit(solution)/shard_map/ppermute | solution.py:96
  11.8 1.7 %copy-done = bf16[1,2048,576]{1,2,0:T(8,128)(2,1)S(1)} copy-done((bf16[1,2048,576]{1,2,0:T(8,128)(2,1)S(1)}, bf16[1,2048,576]{1,2,0:T(8,128)(2,1)}, u32[]{:S(2)}) %copy-start) | copy-done | bytes 2359320
  13.5 0.9 copy-done.5
  14.4 1.9 %shard_map.105 = (f32[32,640]{1,0:T(8,128)S(1)}, f32[32,640]{1,0:T(8,128)S(1)}, bf16[32,3712]{1,0:T(8,128)(2,1)S(1)}) custom-call(s32[2]{0:T(128)S(1)} %pad_add_fusion.here_ref, s32[1]{0:T(128)S(6)} %copy.21.lengths_ref, bf16[64,576]{1,0:T(8,128)(2,1)S(1)} %bitcast.15, bf16[576,2048]{1,0:T(8,128)(2,1)S(1)} %bitcast.12), custom_call_target="tpu_custom_call" | custom-call | flops 285212672 | bytes 2359296 | tf_op jit(solution)/shard_map/pallas_call | solution.py:51
  16.4 1.0 collective-permute-done.3._.refs_4_
  17.5 4.2 %collective-permute-done.2.refs_3_ = bf16[32,3712]{1,0:T(8,128)(2,1)S(1)} collective-permute-done((bf16[32,3712]{1,0:T(8,128)(2,1)S(1)}, bf16[32,3712]{1,0:T(8,128)(2,1)S(1)}, u32[]{:S(2)}, u32[]{:S(2)}) %collective-permute-start.2) | collective-permute-done | bytes 237600 | tf_op jit(solution)/shard_map/ppermute | solution.py:96
  21.7 0.6 collective-permute-start.5
  22.3 0.7 collective-permute-start.6
  23.0 0.5 collective-permute-start.4
  23.6 10.5 %shard_map.106 = (bf16[3,3584,512]{2,1,0:T(8,128)(2,1)S(1)}, bf16[3,3584,512]{2,1,0:T(8,128)(2,1)S(1)}, bf16[3,512,3584]{2,1,0:T(8,128)(2,1)S(1)}, bf16[32,3712]{1,0:T(8,128)(2,1)S(1)}) custom-call(bf16[8,3584,512]{2,1,0:T(8,128)(2,1)} %refs_17_.1, bf16[8,3584,512]{2,1,0:T(8,128)(2,1)} %refs_18_.1, bf16[8,512,3584]{2,1,0:T(8,128)(2,1)} %refs_19_.1, ...), custom_call_target="tpu_custom_call" | custom-call | bytes 33030144 | tf_op jit(solution)/shard_map/pallas_call | solution.py:437
  34.2 1.2 collective-permute-done.5.refs_6_
  35.5 0.2 collective-permute-done.4.refs_5_
  35.8 1.6 %collective-permute-start.8 = (bf16[64,3712]{1,0:T(8,128)(2,1)S(1)}, bf16[64,3712]{1,0:T(8,128)(2,1)S(1)}, u32[]{:S(2)}, u32[]{:S(2)}) collective-permute-start(bf16[64,3712]{1,0:T(8,128)(2,1)S(1)} %get-tuple-element.60), channel_id=1, source_target_pairs={{0,2},{1,3},{2,0},{3,1},{4,6},{5,7},{6,4},{7,5},{8,10},{9,11},{10,... | collective-permute-start | bytes 1425416 | tf_op jit(solution)/shard_map/ppermute | solution.py:96
  37.4 0.5 collective-permute-start.7
  37.9 0.1 pad_maximum_fusion
  38.2 0.2 copy-done.9
  38.4 0.4 collective-permute-start.11
  38.8 7.2 %collective-permute-done.8.refs_9_ = bf16[64,3712]{1,0:T(8,128)(2,1)S(1)} collective-permute-done((bf16[64,3712]{1,0:T(8,128)(2,1)S(1)}, bf16[64,3712]{1,0:T(8,128)(2,1)S(1)}, u32[]{:S(2)}, u32[]{:S(2)}) %collective-permute-start.8) | collective-permute-done | bytes 475168 | tf_op jit(solution)/shard_map/ppermute | solution.py:96
  46.0 1.2 collective-permute-done.7.refs_8_
  47.4 0.6 collective-permute-start.9
  48.0 0.6 collective-permute-start.10
  48.6 4.5 %collective-permute-done.9.refs_10_ = bf16[16,3712]{1,0:T(8,128)(2,1)S(1)} collective-permute-done((bf16[16,3712]{1,0:T(8,128)(2,1)S(1)}, bf16[16,3712]{1,0:T(8,128)(2,1)S(1)}, u32[]{:S(2)}, u32[]{:S(2)}) %collective-permute-start.9) | collective-permute-done | bytes 118816 | tf_op jit(solution)/shard_map/ppermute | solution.py:96
  53.1 0.3 collective-permute-done.10.refs_11_
  53.6 0.5 collective-permute-start.31
  54.1 1.0 collective-permute-done.14.refs_16_
  55.1 1.1 copy-done.18
  56.3 0.2 copy-done.23
  56.5 28.0 %shard_map.107 = (bf16[160,3584]{1,0:T(8,128)(2,1)}, bf16[160,3584]{1,0:T(8,128)(2,1)}, bf16[160,3584]{1,0:T(8,128)(2,1)}, bf16[32,3584]{1,0:T(8,128)(2,1)S(1)},...) custom-call(s32[2]{0:T(128)} %copy-done.6, ...), custom_call_target="tpu_custom_call", output_to_operand_aliasing={{8}: (21, {}), {9}: (22, {}), {10}: (23, {})} | custom-call | flops 11274289152 | bytes 88080384 | tf_op jit(solution)/shard_map/pallas_call | solution.py:471
  84.5 0.2 collective-permute-start.17
  84.7 0.1 fusion.18
  84.9 0.4 collective-permute-start.18
  85.4 0.2 collective-permute-start.15
  85.6 0.4 collective-permute-start.16
  86.0 2.1 %collective-permute-done.18 = bf16[32,3584]{1,0:T(8,128)(2,1)S(1)} collective-permute-done((bf16[32,3584]{1,0:T(8,128)(2,1)S(1)}, bf16[32,3584]{1,0:T(8,128)(2,1)S(1)}, u32[]{:S(2)}, u32[]{:S(2)}) %collective-permute-start.18) | collective-permute-done | bytes 229408 | tf_op jit(solution)/shard_map/ppermute | solution.py:68
  88.1 0.6 collective-permute-start.22
  88.7 1.5 %collective-permute-start.19 = (bf16[16,3584]{1,0:T(8,128)(2,1)S(1)}, bf16[16,3584]{1,0:T(8,128)(2,1)S(1)}, u32[]{:S(2)}, u32[]{:S(2)}) collective-permute-start(bf16[16,3584]{1,0:T(8,128)(2,1)S(1)} %get-tuple-element.59), channel_id=1, source_target_pairs={{0,1},{1,0},{2,3},{3,2},{4,5},{5,4},{6,7},{7,6},{8,9},{9,8},{10,11... | collective-permute-start | bytes 344072 | tf_op jit(solution)/shard_map/ppermute | solution.py:96
  90.2 1.1 add_convert_fusion
  91.2 2.1 %collective-permute-done.22 = bf16[16,3584]{1,0:T(8,128)(2,1)S(1)} collective-permute-done((bf16[16,3584]{1,0:T(8,128)(2,1)S(1)}, bf16[16,3584]{1,0:T(8,128)(2,1)S(1)}, u32[]{:S(2)}, u32[]{:S(2)}) %collective-permute-start.22) | collective-permute-done | bytes 114720 | tf_op jit(solution)/shard_map/ppermute | solution.py:96
  93.4 0.2 collective-permute-done.19
  93.8 1.6 %collective-permute-start.23 = (bf16[64,3584]{1,0:T(8,128)(2,1)S(1)}, bf16[64,3584]{1,0:T(8,128)(2,1)S(1)}, u32[]{:S(2)}, u32[]{:S(2)}) collective-permute-start(bf16[64,3584]{1,0:T(8,128)(2,1)S(1)} %pad_maximum_fusion.10), channel_id=1, source_target_pairs={{0,1},{1,0},{2,3},{3,2},{4,5},{5,4},{6,7},{7,6},{8,9},{9,8},{10,11... | collective-permute-start | bytes 1376264 | tf_op jit(solution)/shard_map/ppermute | solution.py:96
  95.4 1.6 %collective-permute-start.20 = (bf16[64,3584]{1,0:T(8,128)(2,1)S(1)}, bf16[64,3584]{1,0:T(8,128)(2,1)S(1)}, u32[]{:S(2)}, u32[]{:S(2)}) collective-permute-start(bf16[64,3584]{1,0:T(8,128)(2,1)S(1)} %pad_maximum_fusion.9), channel_id=1, source_target_pairs={{0,2},{1,3},{2,0},{3,1},{4,6},{5,7},{6,4},{7,5},{8,10},{9,11},{10,... | collective-permute-start | bytes 1376264 | tf_op jit(solution)/shard_map/ppermute | solution.py:96
  97.1 9.6 %collective-permute-done.20 = bf16[64,3584]{1,0:T(8,128)(2,1)S(1)} collective-permute-done((bf16[64,3584]{1,0:T(8,128)(2,1)S(1)}, bf16[64,3584]{1,0:T(8,128)(2,1)S(1)}, u32[]{:S(2)}, u32[]{:S(2)}) %collective-permute-start.20) | collective-permute-done | bytes 458784 | tf_op jit(solution)/shard_map/ppermute | solution.py:96
  106.9 0.6 collective-permute-start.21
  107.8 1.5 %collective-permute-start.24 = (bf16[80,3584]{1,0:T(8,128)(2,1)S(1)}, bf16[80,3584]{1,0:T(8,128)(2,1)S(1)}, u32[]{:S(2)}, u32[]{:S(2)}) collective-permute-start(bf16[80,3584]{1,0:T(8,128)(2,1)S(1)} %fusion.13), channel_id=1, source_target_pairs={{0,2},{1,3},{2,0},{3,1},{4,6},{5,7},{6,4},{7,5},{8,10},{9,11},{10,... | collective-permute-start | bytes 1720328 | tf_op jit(solution)/shard_map/ppermute | solution.py:96
  109.4 2.2 %collective-permute-start.27 = (bf16[32,3584]{1,0:T(8,128)(2,1)S(1)}, bf16[32,3584]{1,0:T(8,128)(2,1)S(1)}, u32[]{:S(2)}, u32[]{:S(2)}) collective-permute-start(bf16[32,3584]{1,0:T(8,128)(2,1)S(1)} %fusion.2), channel_id=1, source_target_pairs={{0,8},{1,9},{2,10},{3,11},{4,12},{5,13},{6,14},{7,15},{8,0},{9,1},... | collective-permute-start | bytes 688136 | tf_op jit(solution)/shard_map/ppermute | solution.py:96
  111.6 8.2 %collective-permute-done.21 = bf16[80,3584]{1,0:T(8,128)(2,1)S(1)} collective-permute-done((bf16[80,3584]{1,0:T(8,128)(2,1)S(1)}, bf16[80,3584]{1,0:T(8,128)(2,1)S(1)}, u32[]{:S(2)}, u32[]{:S(2)}) %collective-permute-start.21) | collective-permute-done | bytes 573472 | tf_op jit(solution)/shard_map/ppermute | solution.py:96
  119.9 0.5 collective-permute-done.24
  120.4 0.7 copy-done.19
  121.1 0.1 fusion.6
  121.3 1.4 %collective-permute-start.29 = (bf16[32,3584]{1,0:T(8,128)(2,1)S(1)}, bf16[32,3584]{1,0:T(8,128)(2,1)S(1)}, u32[]{:S(2)}, u32[]{:S(2)}) collective-permute-start(bf16[32,3584]{1,0:T(8,128)(2,1)S(1)} %pad_maximum_fusion.13), channel_id=1, source_target_pairs={{0,2},{1,3},{2,0},{3,1},{4,6},{5,7},{6,4},{7,5},{8,10},{9,11},{10,... | collective-permute-start | bytes 688136 | tf_op jit(solution)/shard_map/ppermute | solution.py:96
  122.7 0.2 fusion.4
  122.8 3.4 %collective-permute-start.25 = (bf16[32,3584]{1,0:T(8,128)(2,1)S(1)}, bf16[32,3584]{1,0:T(8,128)(2,1)S(1)}, u32[]{:S(2)}, u32[]{:S(2)}) collective-permute-start(bf16[32,3584]{1,0:T(8,128)(2,1)S(1)} %get-tuple-element.40), channel_id=1, source_target_pairs={{0,12},{1,13},{2,14},{3,15},{4,0},{5,1},{6,2},{7,3},{8,4},{9,5},{1... | collective-permute-start | bytes 688136 | tf_op jit(solution)/shard_map/ppermute | solution.py:96
  126.2 1.3 collective-permute-start.28
  127.6 3.8 %collective-permute-done.25 = bf16[32,3584]{1,0:T(8,128)(2,1)S(1)} collective-permute-done((bf16[32,3584]{1,0:T(8,128)(2,1)S(1)}, bf16[32,3584]{1,0:T(8,128)(2,1)S(1)}, u32[]{:S(2)}, u32[]{:S(2)}) %collective-permute-start.25) | collective-permute-done | bytes 229408 | tf_op jit(solution)/shard_map/ppermute | solution.py:96
  131.4 2.9 %collective-permute-done.26 = bf16[32,3584]{1,0:T(8,128)(2,1)S(1)} collective-permute-done((bf16[32,3584]{1,0:T(8,128)(2,1)S(1)}, bf16[32,3584]{1,0:T(8,128)(2,1)S(1)}, u32[]{:S(2)}, u32[]{:S(2)}) %collective-permute-start.26) | collective-permute-done | bytes 229408 | tf_op jit(solution)/shard_map/ppermute | solution.py:96
  134.3 0.1 convert_add_fusion
  134.6 0.2 slice_reduce_fusion
  134.8 0.7 fusion.16
  135.5 0.6 collective-permute-done.30.other_ref
  136.1 1.3 shard_map.108
  (103 shorter events, 2.3 us)
Async XLA Ops:
  0.7 15.6 %copy-start.6 = (s32[2]{0:T(128)}, s32[2]{0:T(128)S(1)}, u32[]{:S(2)}) copy-start(s32[2]{0:T(128)S(1)} %pad_add_fusion.here_ref) | copy-start | bytes 28
  2.4 0.7 copy-start.4
  3.1 19.2 %copy-start.3 = (bf16[32,3712]{1,0:T(8,128)(2,1)}, bf16[32,3712]{1,0:T(8,128)(2,1)S(1)}, u32[]{:S(2)}) copy-start(bf16[32,3712]{1,0:T(8,128)(2,1)S(1)} %get-tuple-element.22.refs_0_) | copy-start | bytes 712708
  3.1 13.2 %collective-permute-start.1 = (bf16[32,3712]{1,0:T(8,128)(2,1)S(1)}, bf16[32,3712]{1,0:T(8,128)(2,1)S(1)}, u32[]{:S(2)}, u32[]{:S(2)}) collective-permute-start(bf16[32,3712]{1,0:T(8,128)(2,1)S(1)} %get-tuple-element.22.refs_0_), channel_id=1, source_target_pairs={{0,2},{1,3},{2,0},{3,1},{4,6},{5,7},{6,4},{7,5},{8,10},{9,11},{10,... | collective-permute-start | bytes 712712 | tf_op jit(solution)/shard_map/ppermute | solution.py:96
  6.1 10.3 %collective-permute-start = (bf16[32,3712]{1,0:T(8,128)(2,1)S(1)}, bf16[32,3712]{1,0:T(8,128)(2,1)S(1)}, u32[]{:S(2)}, u32[]{:S(2)}) collective-permute-start(bf16[32,3712]{1,0:T(8,128)(2,1)S(1)} %get-tuple-element.22.refs_0_), channel_id=1, source_target_pairs={{0,1},{1,0},{2,3},{3,2},{4,5},{5,4},{6,7},{7,6},{8,9},{9,8},{10,11... | collective-permute-start | bytes 712712 | tf_op jit(solution)/shard_map/ppermute | solution.py:96
  7.5 9.8 %collective-permute-start.3 = (bf16[32,3712]{1,0:T(8,128)(2,1)S(1)}, bf16[32,3712]{1,0:T(8,128)(2,1)S(1)}, u32[]{:S(2)}, u32[]{:S(2)}) collective-permute-start(bf16[32,3712]{1,0:T(8,128)(2,1)S(1)} %get-tuple-element.22.refs_0_), channel_id=1, source_target_pairs={{0,12},{1,13},{2,14},{3,15},{4,0},{5,1},{6,2},{7,3},{8,4},{9,5},{1... | collective-permute-start | bytes 712712 | tf_op jit(solution)/shard_map/ppermute | solution.py:96
  11.1 10.5 %collective-permute-start.2 = (bf16[32,3712]{1,0:T(8,128)(2,1)S(1)}, bf16[32,3712]{1,0:T(8,128)(2,1)S(1)}, u32[]{:S(2)}, u32[]{:S(2)}) collective-permute-start(bf16[32,3712]{1,0:T(8,128)(2,1)S(1)} %get-tuple-element.22.refs_0_), channel_id=1, source_target_pairs={{0,4},{1,5},{2,6},{3,7},{4,8},{5,9},{6,10},{7,11},{8,12},{9,13},{1... | collective-permute-start | bytes 712712 | tf_op jit(solution)/shard_map/ppermute | solution.py:96
  11.8 1.7 %copy-start = (bf16[1,2048,576]{1,2,0:T(8,128)(2,1)S(1)}, bf16[1,2048,576]{1,2,0:T(8,128)(2,1)}, u32[]{:S(2)}) copy-start(bf16[1,2048,576]{1,2,0:T(8,128)(2,1)} %param.16) | copy-start | bytes 7077892
  13.5 0.9 copy-start.5
  16.3 5.4 %copy-start.1 = (f32[32,640]{1,0:T(8,128)}, f32[32,640]{1,0:T(8,128)S(1)}, u32[]{:S(2)}) copy-start(f32[32,640]{1,0:T(8,128)S(1)} %get-tuple-element.23) | copy-start | bytes 245764
  16.3 21.8 %copy-start.16 = (bf16[32,3712]{1,0:T(8,128)(2,1)}, bf16[32,3712]{1,0:T(8,128)(2,1)S(1)}, u32[]{:S(2)}) copy-start(bf16[32,3712]{1,0:T(8,128)(2,1)S(1)} %collective-permute-done.1.refs_2_) | copy-start | bytes 712708
  16.4 21.8 %copy-start.17 = (bf16[32,3712]{1,0:T(8,128)(2,1)}, bf16[32,3712]{1,0:T(8,128)(2,1)S(1)}, u32[]{:S(2)}) copy-start(bf16[32,3712]{1,0:T(8,128)(2,1)S(1)} %collective-permute-done.refs_1_) | copy-start | bytes 712708
  17.4 4.3 %copy-start.8 = (bf16[32,3712]{1,0:T(8,128)(2,1)}, bf16[32,3712]{1,0:T(8,128)(2,1)S(1)}, u32[]{:S(2)}) copy-start(bf16[32,3712]{1,0:T(8,128)(2,1)S(1)} %collective-permute-done.3._.refs_4_) | copy-start | bytes 712708
  21.6 16.6 %copy-start.15 = (bf16[32,3712]{1,0:T(8,128)(2,1)}, bf16[32,3712]{1,0:T(8,128)(2,1)S(1)}, u32[]{:S(2)}) copy-start(bf16[32,3712]{1,0:T(8,128)(2,1)S(1)} %collective-permute-done.2.refs_3_) | copy-start | bytes 712708
  21.7 13.7 %collective-permute-start.5 = (bf16[80,3712]{1,0:T(8,128)(2,1)S(1)}, bf16[80,3712]{1,0:T(8,128)(2,1)S(1)}, u32[]{:S(2)}, u32[]{:S(2)}) collective-permute-start(bf16[80,3712]{1,0:T(8,128)(2,1)S(1)} %get-tuple-element.56), channel_id=1, source_target_pairs={{0,2},{1,3},{2,0},{3,1},{4,6},{5,7},{6,4},{7,5},{8,10},{9,11},{10,... | collective-permute-start | bytes 1781768 | tf_op jit(solution)/shard_map/ppermute | solution.py:96
  22.3 11.8 %collective-permute-start.6 = (bf16[32,3712]{1,0:T(8,128)(2,1)S(1)}, bf16[32,3712]{1,0:T(8,128)(2,1)S(1)}, u32[]{:S(2)}, u32[]{:S(2)}) collective-permute-start(bf16[32,3712]{1,0:T(8,128)(2,1)S(1)} %get-tuple-element.22.refs_0_), channel_id=1, source_target_pairs={{0,8},{1,9},{2,10},{3,11},{4,12},{5,13},{6,14},{7,15},{8,0},{9,1},... | collective-permute-start | bytes 712712 | tf_op jit(solution)/shard_map/ppermute | solution.py:96
  23.0 12.7 %collective-permute-start.4 = (bf16[80,3712]{1,0:T(8,128)(2,1)S(1)}, bf16[80,3712]{1,0:T(8,128)(2,1)S(1)}, u32[]{:S(2)}, u32[]{:S(2)}) collective-permute-start(bf16[80,3712]{1,0:T(8,128)(2,1)S(1)} %get-tuple-element.57), channel_id=1, source_target_pairs={{0,1},{1,0},{2,3},{3,2},{4,5},{5,4},{6,7},{7,6},{8,9},{9,8},{10,11... | collective-permute-start | bytes 1781768 | tf_op jit(solution)/shard_map/ppermute | solution.py:96
  34.2 3.7 %copy-start.10 = (bf16[32,3712]{1,0:T(8,128)(2,1)}, bf16[32,3712]{1,0:T(8,128)(2,1)S(1)}, u32[]{:S(2)}) copy-start(bf16[32,3712]{1,0:T(8,128)(2,1)S(1)} %add.140.refs_7_) | copy-start | bytes 712708
  35.5 2.5 %copy-start.11 = (bf16[80,3712]{1,0:T(8,128)(2,1)}, bf16[80,3712]{1,0:T(8,128)(2,1)S(1)}, u32[]{:S(2)}) copy-start(bf16[80,3712]{1,0:T(8,128)(2,1)S(1)} %collective-permute-done.5.refs_6_) | copy-start | bytes 1781764
  35.7 2.4 %copy-start.12 = (bf16[80,3712]{1,0:T(8,128)(2,1)}, bf16[80,3712]{1,0:T(8,128)(2,1)S(1)}, u32[]{:S(2)}) copy-start(bf16[80,3712]{1,0:T(8,128)(2,1)S(1)} %collective-permute-done.4.refs_5_) | copy-start | bytes 1781764
  35.8 10.2 %collective-permute-start.8 = (bf16[64,3712]{1,0:T(8,128)(2,1)S(1)}, bf16[64,3712]{1,0:T(8,128)(2,1)S(1)}, u32[]{:S(2)}, u32[]{:S(2)}) collective-permute-start(bf16[64,3712]{1,0:T(8,128)(2,1)S(1)} %get-tuple-element.60), channel_id=1, source_target_pairs={{0,2},{1,3},{2,0},{3,1},{4,6},{5,7},{6,4},{7,5},{8,10},{9,11},{10,... | collective-permute-start | bytes 1425416 | tf_op jit(solution)/shard_map/ppermute | solution.py:96
  37.4 0.9 copy-start.9
  37.4 9.8 %collective-permute-start.7 = (bf16[64,3712]{1,0:T(8,128)(2,1)S(1)}, bf16[64,3712]{1,0:T(8,128)(2,1)S(1)}, u32[]{:S(2)}, u32[]{:S(2)}) collective-permute-start(bf16[64,3712]{1,0:T(8,128)(2,1)S(1)} %get-tuple-element.61), channel_id=1, source_target_pairs={{0,1},{1,0},{2,3},{3,2},{4,5},{5,4},{6,7},{7,6},{8,9},{9,8},{10,11... | collective-permute-start | bytes 1425416 | tf_op jit(solution)/shard_map/ppermute | solution.py:96
  38.1 17.0 %collective-permute-start.12 = (bf16[192,3712]{1,0:T(8,128)(2,1)S(1)}, bf16[192,3712]{1,0:T(8,128)(2,1)S(1)}, u32[]{:S(2)}, u32[]{:S(2)}) collective-permute-start(bf16[192,3712]{1,0:T(8,128)(2,1)S(1)} %pad_maximum_fusion), channel_id=1, source_target_pairs={{0,16},{16,0},{1,17},{17,1},{2,18},{18,2},{3,19},{19,3},{4,20},{20... | collective-permute-start | bytes 4276232 | tf_op jit(solution)/shard_map/ppermute | solution.py:68
  38.4 15.6 %collective-permute-start.11 = (bf16[128,3712]{1,0:T(8,128)(2,1)S(1)}, bf16[128,3712]{1,0:T(8,128)(2,1)S(1)}, u32[]{:S(2)}, u32[]{:S(2)}) collective-permute-start(bf16[128,3712]{1,0:T(8,128)(2,1)S(1)} %pad_maximum_fusion.1), channel_id=1, source_target_pairs={{0,16},{16,0},{1,17},{17,1},{2,18},{18,2},{3,19},{19,3},{4,20},{20... | collective-permute-start | bytes 2850824 | tf_op jit(solution)/shard_map/ppermute | solution.py:68
  46.0 2.0 %copy-start.13 = (bf16[64,3712]{1,0:T(8,128)(2,1)}, bf16[64,3712]{1,0:T(8,128)(2,1)S(1)}, u32[]{:S(2)}) copy-start(bf16[64,3712]{1,0:T(8,128)(2,1)S(1)} %collective-permute-done.8.refs_9_) | copy-start | bytes 1425412
  47.2 0.8 copy-start.14
  47.3 7.7 %collective-permute-start.13 = (bf16[128,3712]{1,0:T(8,128)(2,1)S(1)}, bf16[128,3712]{1,0:T(8,128)(2,1)S(1)}, u32[]{:S(2)}, u32[]{:S(2)}) collective-permute-start(bf16[128,3712]{1,0:T(8,128)(2,1)S(1)} %pad_maximum_fusion.2), channel_id=1, source_target_pairs={{0,16},{16,0},{1,17},{17,1},{2,18},{18,2},{3,19},{19,3},{4,20},{20... | collective-permute-start | bytes 2850824 | tf_op jit(solution)/shard_map/ppermute | solution.py:68
  47.4 5.7 %collective-permute-start.9 = (bf16[16,3712]{1,0:T(8,128)(2,1)S(1)}, bf16[16,3712]{1,0:T(8,128)(2,1)S(1)}, u32[]{:S(2)}, u32[]{:S(2)}) collective-permute-start(bf16[16,3712]{1,0:T(8,128)(2,1)S(1)} %slice.294), channel_id=1, source_target_pairs={{0,1},{1,0},{2,3},{3,2},{4,5},{5,4},{6,7},{7,6},{8,9},{9,8},{10,11... | collective-permute-start | bytes 356360 | tf_op jit(solution)/shard_map/ppermute | solution.py:96
  48.0 5.4 %collective-permute-start.10 = (bf16[16,3712]{1,0:T(8,128)(2,1)S(1)}, bf16[16,3712]{1,0:T(8,128)(2,1)S(1)}, u32[]{:S(2)}, u32[]{:S(2)}) collective-permute-start(bf16[16,3712]{1,0:T(8,128)(2,1)S(1)} %slice.295), channel_id=1, source_target_pairs={{0,2},{1,3},{2,0},{3,1},{4,6},{5,7},{6,4},{7,5},{8,10},{9,11},{10,... | collective-permute-start | bytes 356360 | tf_op jit(solution)/shard_map/ppermute | solution.py:96
  53.1 3.1 %copy-start.24 = (bf16[16,3712]{1,0:T(8,128)(2,1)}, bf16[16,3712]{1,0:T(8,128)(2,1)S(1)}, u32[]{:S(2)}) copy-start(bf16[16,3712]{1,0:T(8,128)(2,1)S(1)} %collective-permute-done.9.refs_10_) | copy-start | bytes 356356
  53.5 2.8 %copy-start.25 = (bf16[16,3712]{1,0:T(8,128)(2,1)}, bf16[16,3712]{1,0:T(8,128)(2,1)S(1)}, u32[]{:S(2)}) copy-start(bf16[16,3712]{1,0:T(8,128)(2,1)S(1)} %collective-permute-done.10.refs_11_) | copy-start | bytes 356356
  53.5 1.6 %collective-permute-start.14 = (bf16[32,3712]{1,0:T(8,128)(2,1)S(1)}, bf16[32,3712]{1,0:T(8,128)(2,1)S(1)}, u32[]{:S(2)}, u32[]{:S(2)}) collective-permute-start(bf16[32,3712]{1,0:T(8,128)(2,1)S(1)} %pad_maximum_fusion.11), channel_id=1, source_target_pairs={{0,16},{16,0},{1,17},{17,1},{2,18},{18,2},{3,19},{19,3},{4,20},{20... | collective-permute-start | bytes 712712 | tf_op jit(solution)/shard_map/ppermute | solution.py:68
  53.6 31.2 %collective-permute-start.31 = (f32[1,32,640]{2,1,0:T(8,128)S(1)}, f32[1,32,640]{2,1,0:T(8,128)S(1)}, u32[]{:S(2)}, u32[]{:S(2)}) collective-permute-start(f32[1,32,640]{2,1,0:T(8,128)S(1)} %bitcast.16), channel_id=1, source_target_pairs={{0,16},{16,0},{1,17},{17,1},{2,18},{18,2},{3,19},{19,3},{4,20},{20... | collective-permute-start | bytes 245768 | tf_op jit(solution)/shard_map/ppermute | solution.py:68
  54.1 2.2 %copy-start.22 = (bf16[128,3712]{1,0:T(8,128)(2,1)}, bf16[128,3712]{1,0:T(8,128)(2,1)S(1)}, u32[]{:S(2)}) copy-start(bf16[128,3712]{1,0:T(8,128)(2,1)S(1)} %collective-permute-done.11.refs_13_) | copy-start | bytes 2850820
  55.0 1.2 copy-start.26
  55.0 1.5 %copy-start.23 = (bf16[128,3712]{1,0:T(8,128)(2,1)}, bf16[128,3712]{1,0:T(8,128)(2,1)S(1)}, u32[]{:S(2)}) copy-start(bf16[128,3712]{1,0:T(8,128)(2,1)S(1)} %collective-permute-done.13.refs_15_) | copy-start | bytes 2850820
  55.1 1.1 copy-start.18
  56.5 28.2 %copy-start.2 = (f32[32,640]{1,0:T(8,128)S(1)}, f32[32,640]{1,0:T(8,128)}, u32[]{:S(2)}) copy-start(f32[32,640]{1,0:T(8,128)} %copy-done.1) | copy-start | bytes 245764
  84.5 9.1 %copy-start.20 = (bf16[160,3584]{1,0:T(8,128)(2,1)S(1)}, bf16[160,3584]{1,0:T(8,128)(2,1)}, u32[]{:S(2)}) copy-start(bf16[160,3584]{1,0:T(8,128)(2,1)} %get-tuple-element.33) | copy-start | bytes 3440644
  84.5 5.6 %collective-permute-start.17 = (bf16[160,3584]{1,0:T(8,128)(2,1)}, bf16[160,3584]{1,0:T(8,128)(2,1)S(1)}, u32[]{:S(2)}, u32[]{:S(2)}) collective-permute-start(bf16[160,3584]{1,0:T(8,128)(2,1)} %get-tuple-element.34), channel_id=1, source_target_pairs={{0,16},{16,0},{1,17},{17,1},{2,18},{18,2},{3,19},{19,3},{4,20},{20... | collective-permute-start | bytes 3440648 | tf_op jit(solution)/shard_map/ppermute | solution.py:68
  84.9 3.2 %collective-permute-start.18 = (bf16[32,3584]{1,0:T(8,128)(2,1)S(1)}, bf16[32,3584]{1,0:T(8,128)(2,1)S(1)}, u32[]{:S(2)}, u32[]{:S(2)}) collective-permute-start(bf16[32,3584]{1,0:T(8,128)(2,1)S(1)} %get-tuple-element.36), channel_id=1, source_target_pairs={{0,16},{16,0},{1,17},{17,1},{2,18},{18,2},{3,19},{19,3},{4,20},{20... | collective-permute-start | bytes 688136 | tf_op jit(solution)/shard_map/ppermute | solution.py:68
  85.4 35.0 %collective-permute-start.15 = (bf16[160,3584]{1,0:T(8,128)(2,1)}, bf16[160,3584]{1,0:T(8,128)(2,1)S(1)}, u32[]{:S(2)}, u32[]{:S(2)}) collective-permute-start(bf16[160,3584]{1,0:T(8,128)(2,1)} %get-tuple-element.30), channel_id=1, source_target_pairs={{0,16},{16,0},{1,17},{17,1},{2,18},{18,2},{3,19},{19,3},{4,20},{20... | collective-permute-start | bytes 3440648 | tf_op jit(solution)/shard_map/ppermute | solution.py:68
  85.6 11.4 %collective-permute-start.16 = (bf16[160,3584]{1,0:T(8,128)(2,1)}, bf16[160,3584]{1,0:T(8,128)(2,1)S(1)}, u32[]{:S(2)}, u32[]{:S(2)}) collective-permute-start(bf16[160,3584]{1,0:T(8,128)(2,1)} %get-tuple-element.32), channel_id=1, source_target_pairs={{0,16},{16,0},{1,17},{17,1},{2,18},{18,2},{3,19},{19,3},{4,20},{20... | collective-permute-start | bytes 3440648 | tf_op jit(solution)/shard_map/ppermute | solution.py:68
  88.1 5.3 %collective-permute-start.22 = (bf16[16,3584]{1,0:T(8,128)(2,1)S(1)}, bf16[16,3584]{1,0:T(8,128)(2,1)S(1)}, u32[]{:S(2)}, u32[]{:S(2)}) collective-permute-start(bf16[16,3584]{1,0:T(8,128)(2,1)S(1)} %get-tuple-element.58), channel_id=1, source_target_pairs={{0,2},{1,3},{2,0},{3,1},{4,6},{5,7},{6,4},{7,5},{8,10},{9,11},{10,... | collective-permute-start | bytes 344072 | tf_op jit(solution)/shard_map/ppermute | solution.py:96
  88.7 4.9 %collective-permute-start.19 = (bf16[16,3584]{1,0:T(8,128)(2,1)S(1)}, bf16[16,3584]{1,0:T(8,128)(2,1)S(1)}, u32[]{:S(2)}, u32[]{:S(2)}) collective-permute-start(bf16[16,3584]{1,0:T(8,128)(2,1)S(1)} %get-tuple-element.59), channel_id=1, source_target_pairs={{0,1},{1,0},{2,3},{3,2},{4,5},{5,4},{6,7},{7,6},{8,9},{9,8},{10,11... | collective-permute-start | bytes 344072 | tf_op jit(solution)/shard_map/ppermute | solution.py:96
  93.7 3.3 %copy-start.21 = (bf16[160,3584]{1,0:T(8,128)(2,1)S(1)}, bf16[160,3584]{1,0:T(8,128)(2,1)}, u32[]{:S(2)}) copy-start(bf16[160,3584]{1,0:T(8,128)(2,1)} %get-tuple-element.31) | copy-start | bytes 3440644
  93.8 13.8 %collective-permute-start.23 = (bf16[64,3584]{1,0:T(8,128)(2,1)S(1)}, bf16[64,3584]{1,0:T(8,128)(2,1)S(1)}, u32[]{:S(2)}, u32[]{:S(2)}) collective-permute-start(bf16[64,3584]{1,0:T(8,128)(2,1)S(1)} %pad_maximum_fusion.10), channel_id=1, source_target_pairs={{0,1},{1,0},{2,3},{3,2},{4,5},{5,4},{6,7},{7,6},{8,9},{9,8},{10,11... | collective-permute-start | bytes 1376264 | tf_op jit(solution)/shard_map/ppermute | solution.py:96
  95.4 11.3 %collective-permute-start.20 = (bf16[64,3584]{1,0:T(8,128)(2,1)S(1)}, bf16[64,3584]{1,0:T(8,128)(2,1)S(1)}, u32[]{:S(2)}, u32[]{:S(2)}) collective-permute-start(bf16[64,3584]{1,0:T(8,128)(2,1)S(1)} %pad_maximum_fusion.9), channel_id=1, source_target_pairs={{0,2},{1,3},{2,0},{3,1},{4,6},{5,7},{6,4},{7,5},{8,10},{9,11},{10,... | collective-permute-start | bytes 1376264 | tf_op jit(solution)/shard_map/ppermute | solution.py:96
  106.9 12.8 %collective-permute-start.21 = (bf16[80,3584]{1,0:T(8,128)(2,1)S(1)}, bf16[80,3584]{1,0:T(8,128)(2,1)S(1)}, u32[]{:S(2)}, u32[]{:S(2)}) collective-permute-start(bf16[80,3584]{1,0:T(8,128)(2,1)S(1)} %pad_maximum_fusion.6), channel_id=1, source_target_pairs={{0,1},{1,0},{2,3},{3,2},{4,5},{5,4},{6,7},{7,6},{8,9},{9,8},{10,11... | collective-permute-start | bytes 1720328 | tf_op jit(solution)/shard_map/ppermute | solution.py:96
  107.8 12.5 %collective-permute-start.24 = (bf16[80,3584]{1,0:T(8,128)(2,1)S(1)}, bf16[80,3584]{1,0:T(8,128)(2,1)S(1)}, u32[]{:S(2)}, u32[]{:S(2)}) collective-permute-start(bf16[80,3584]{1,0:T(8,128)(2,1)S(1)} %fusion.13), channel_id=1, source_target_pairs={{0,2},{1,3},{2,0},{3,1},{4,6},{5,7},{6,4},{7,5},{8,10},{9,11},{10,... | collective-permute-start | bytes 1720328 | tf_op jit(solution)/shard_map/ppermute | solution.py:96
  109.4 18.2 %collective-permute-start.27 = (bf16[32,3584]{1,0:T(8,128)(2,1)S(1)}, bf16[32,3584]{1,0:T(8,128)(2,1)S(1)}, u32[]{:S(2)}, u32[]{:S(2)}) collective-permute-start(bf16[32,3584]{1,0:T(8,128)(2,1)S(1)} %fusion.2), channel_id=1, source_target_pairs={{0,8},{1,9},{2,10},{3,11},{4,12},{5,13},{6,14},{7,15},{8,0},{9,1},... | collective-permute-start | bytes 688136 | tf_op jit(solution)/shard_map/ppermute | solution.py:96
  119.9 1.3 copy-start.19
  121.3 13.2 %collective-permute-start.29 = (bf16[32,3584]{1,0:T(8,128)(2,1)S(1)}, bf16[32,3584]{1,0:T(8,128)(2,1)S(1)}, u32[]{:S(2)}, u32[]{:S(2)}) collective-permute-start(bf16[32,3584]{1,0:T(8,128)(2,1)S(1)} %pad_maximum_fusion.13), channel_id=1, source_target_pairs={{0,2},{1,3},{2,0},{3,1},{4,6},{5,7},{6,4},{7,5},{8,10},{9,11},{10,... | collective-permute-start | bytes 688136 | tf_op jit(solution)/shard_map/ppermute | solution.py:96
  122.8 8.5 %collective-permute-start.25 = (bf16[32,3584]{1,0:T(8,128)(2,1)S(1)}, bf16[32,3584]{1,0:T(8,128)(2,1)S(1)}, u32[]{:S(2)}, u32[]{:S(2)}) collective-permute-start(bf16[32,3584]{1,0:T(8,128)(2,1)S(1)} %get-tuple-element.40), channel_id=1, source_target_pairs={{0,12},{1,13},{2,14},{3,15},{4,0},{5,1},{6,2},{7,3},{8,4},{9,5},{1... | collective-permute-start | bytes 688136 | tf_op jit(solution)/shard_map/ppermute | solution.py:96
  126.2 8.1 %collective-permute-start.26 = (bf16[32,3584]{1,0:T(8,128)(2,1)S(1)}, bf16[32,3584]{1,0:T(8,128)(2,1)S(1)}, u32[]{:S(2)}, u32[]{:S(2)}) collective-permute-start(bf16[32,3584]{1,0:T(8,128)(2,1)S(1)} %get-tuple-element.41), channel_id=1, source_target_pairs={{0,4},{1,5},{2,6},{3,7},{4,8},{5,9},{6,10},{7,11},{8,12},{9,13},{1... | collective-permute-start | bytes 688136 | tf_op jit(solution)/shard_map/ppermute | solution.py:96
  126.2 9.9 %copy-start.7 = (s32[2]{0:T(128)S(1)}, s32[2]{0:T(128)}, u32[]{:S(2)}) copy-start(s32[2]{0:T(128)} %copy-done.6) | copy-start | bytes 28
  126.2 8.2 %collective-permute-start.28 = (bf16[32,3584]{1,0:T(8,128)(2,1)S(1)}, bf16[32,3584]{1,0:T(8,128)(2,1)S(1)}, u32[]{:S(2)}, u32[]{:S(2)}) collective-permute-start(bf16[32,3584]{1,0:T(8,128)(2,1)S(1)} %pad_maximum_fusion.12), channel_id=1, source_target_pairs={{0,1},{1,0},{2,3},{3,2},{4,5},{5,4},{6,7},{7,6},{8,9},{9,8},{10,11... | collective-permute-start | bytes 688136 | tf_op jit(solution)/shard_map/ppermute | solution.py:96
  134.5 1.6 %collective-permute-start.30 = (bf16[32,3584]{1,0:T(8,128)(2,1)S(1)}, bf16[32,3584]{1,0:T(8,128)(2,1)S(1)}, u32[]{:S(2)}, u32[]{:S(2)}) collective-permute-start(bf16[32,3584]{1,0:T(8,128)(2,1)S(1)} %add_convert_fusion.1.own_ref), channel_id=1, source_target_pairs={{0,16},{16,0},{1,17},{17,1},{2,18},{18,2},{3,19},{19,3},{4,20},{20... | collective-permute-start | bytes 688136 | tf_op jit(solution)/shard_map/ppermute | solution.py:68
